TPU v7x, 128 devices: a whole 4x4x4 slice. The times are simulated.
128 devices in a mesh: site: 8 (over y, core), sector: 16 (over z, x).
Axes of the slice: x: 4, y: 4, z: 4, core: 2. Of those that a mesh axis runs over, the one named last changes fastest.
Arguments:
- held_env: float32 [8, 3, 16, 384, 384], P('site', None, 'sector'), may hold values from -6 to 6
- incoming: float32 [4, 3, 16, 384, 384], P(None, None, 'sector'), may hold values from -6 to 6
- states: float32 [8, 4, 16, 384, 384], P('site', None, 'sector'), may hold values from -0.3125 to 0.3125
- weight_table: float32 [16, 4, 3, 3], replicated, may hold values from -2 to 2
- site_kind: int32 [8], P('site'), may hold values from 0 to 15
- sector_sizes: int32 [16], replicated, may hold values from 1 to 384, 5376 in all
- charge_shift: int32 [4], replicated, may hold values from 0 to 2, as said below
Outputs:
- final_env: float32 [8, 3, 16, 384, 384], P('site', None, 'sector')
Inputs may be any that keep to these rules, and one draw needn't show every extreme that they name: `charge_shift`: each of 0, 1 and 2 appears among the shifts. `sector_sizes`: the sizes sum to 5376; the largest equals 384.
All inputs are finite; a program needn't handle non-finite values.
Results may differ from a plain program's by a relative error of at most 0.00015.
Values sent between devices are 32-bit elements; how exact they have to be, the bound alone decides.
No kernel may reach another device: no remote copies, remote signals or barrier semaphores. Data moves between devices by JAX's collectives and lax.ppermute only.
A program may use at most 128 MiB of HBM per device.

v0:
```python
import functools

import jax
import jax.numpy as jnp
from jax import lax
from jax.experimental import pallas as pl
from jax.experimental.pallas import tpu as pltpu
from jax.sharding import PartitionSpec as P


TICKS = 4
AXES = ("site", "sector")
LOW = 144
VMEM = pl.BlockSpec(memory_space=pltpu.VMEM)
SMEM = pl.BlockSpec(memory_space=pltpu.SMEM)
HBM = pl.BlockSpec(memory_space=pltpu.HBM)
PARAMS = pltpu.CompilerParams(vmem_limit_bytes=24 * 1024 * 1024)


def halves(value):
    high = value.astype(jnp.bfloat16)
    return high, (value - high.astype(jnp.float32)).astype(jnp.bfloat16)


def dot(left, right):
    return jnp.dot(left, right, preferred_element_type=jnp.float32)


def shift_of(place, state):
    return place[3 + state]


def fill(state, place, count, states_ref, plain_ref, turned_ref):
    block = states_ref.shape[-1]
    owner = place[1]
    sectors = place.shape[0] - 3 - count
    live_in = place[3 + count + owner]
    live_out = place[3 + count + lax.rem(owner + shift_of(place, state), sectors)]
    rows = lax.broadcasted_iota(jnp.int32, (block, block), 0)
    columns = lax.broadcasted_iota(jnp.int32, (block, block), 1)
    keep = (rows < live_in) & (columns < live_out)
    masked = jnp.where(keep, states_ref[0, state, 0], jnp.float32(0.0))
    high, low = halves(masked)
    plain_ref[state, 0:block, :] = high
    plain_ref[state, block : 2 * block, :] = low
    plain_ref[state, 2 * block :, :] = high
    high, low = halves(masked.T)
    turned_ref[state, :, 0:block] = high
    turned_ref[state, :, block : 2 * block] = high
    turned_ref[state, :, 2 * block :] = low


def products(offset, place, weights, env_ref, plain_ref, turned_ref, store, ready=None):
    terms = env_ref.shape[0]
    count = plain_ref.shape[0]

    def one_state(state, found):
        mine = shift_of(place, state) == offset

        @pl.when(mine)
        def _():
            if ready is not None:
                ready(state)
            base = (place[2] * count + state) * terms * terms

            def one_term(out_term):
                mixed = weights[base + out_term] * env_ref[0]
                for term in range(1, terms):
                    mixed += weights[base + term * terms + out_term] * env_ref[term]
                high, low = halves(mixed)
                right = dot(turned_ref[state], jnp.concatenate([high, low, high], axis=0))
                high, low = halves(right)
                triple = dot(jnp.concatenate([high, high, low], axis=1), plain_ref[state])
                store(out_term, triple, found == 0)

            pl.loop(0, terms)(one_term)

        return found + mine.astype(jnp.int32)

    lax.fori_loop(0, count, one_state, jnp.int32(0))


def split_store(low_ref, high_ref):
    def store(term, value, first):
        @pl.when(first)
        def _():
            low_ref[term] = value[:LOW]
            high_ref[term] = value[LOW:]

        @pl.when(jnp.logical_not(first))
        def _():
            low_ref[term] += value[:LOW]
            high_ref[term] += value[LOW:]

    return store


def whole_store(ref):
    def store(term, value, first):
        @pl.when(first)
        def _():
            ref[term] = value

        @pl.when(jnp.logical_not(first))
        def _():
            ref[term] += value

    return store


def gather_kernel(tick, place, weights, stay, low, high, far, incoming, plain, turned,
                  out_low, out_high, env):
    @pl.when(place[0] == 0)
    def _():
        pltpu.sync_copy(incoming.at[tick, :, 0], env)

    @pl.when(place[0] != 0)
    def _():
        env[:, :LOW] = stay[:, :LOW] + low[...]
        env[:, LOW:] = stay[:, LOW:] + high[...] + far[...]

    products(2, place, weights, env, plain, turned, split_store(out_low, out_high))


def first_kernel(place, weights, env, states, out_low, out_high, plain, turned):
    def ready(state):
        fill(state, place, plain.shape[0], states, plain, turned)

    products(2, place, weights, env, plain, turned, split_store(out_low, out_high), ready)


def first_one_kernel(place, weights, env, states, plain_in, turned_in,
                     out_low, out_high, plain, turned):
    def ready(state):
        fill(state, place, plain.shape[0], states, plain, turned)

    products(1, place, weights, env, plain, turned, split_store(out_low, out_high), ready)


def first_zero_kernel(place, weights, env, states, plain_in, turned_in,
                      out, plain, turned):
    def ready(state):
        fill(state, place, plain.shape[0], states, plain, turned)

    products(0, place, weights, env, plain, turned, whole_store(out), ready)


def one_kernel(place, weights, env, plain, turned, out_low, out_high):
    products(1, place, weights, env, plain, turned, split_store(out_low, out_high))


def zero_kernel(place, weights, env, plain, turned, out):
    products(0, place, weights, env, plain, turned, whole_store(out))


def final_kernel(tick, place, stay, low, high, far, incoming, env):
    @pl.when(place[0] == 0)
    def _():
        pltpu.sync_copy(incoming.at[tick, :, 0], env)

    @pl.when(place[0] != 0)
    def _():
        env[:, :LOW] = stay[:, :LOW] + low[...]
        env[:, LOW:] = stay[:, LOW:] + high[...] + far[...]


def shape(*dims):
    return jax.ShapeDtypeStruct(dims, jnp.float32)


def estimate(block, terms):
    return pl.CostEstimate(
        flops=terms * 12 * block**3, bytes_accessed=16 * block * block * terms, transcendentals=0
    )


def routes(tick, columns, sites, sectors):
    relay, lift, far_one, far_two, stay = [], [], [], [], []
    for site in range(min(sites - 1, tick + TICKS)):
        for sector in range(sectors):
            here = site * sectors + sector
            after = (sector + 1) % sectors
            relay.append((here, site * sectors + after))
            lift.append((here, (site + 1) * sectors + after))
            stay.append((here, (site + 1) * sectors + sector))
            target = (sector + 2) % sectors
            back = (target // columns) * columns + (target + 1) % columns
            far_one.append((here, site * sectors + back))
            far_two.append((site * sectors + back, (site + 1) * sectors + target))
    return relay, lift, far_one, far_two, stay


def local(sites, held_env, incoming, states, weight_table, site_kind, sector_sizes, charge_shift):
    terms, block = held_env.shape[1], held_env.shape[3]
    sectors = sector_sizes.shape[0]
    columns = 4
    here = jnp.stack([lax.axis_index("site"), lax.axis_index("sector")]).astype(jnp.int32)
    place = jnp.concatenate([here, site_kind, charge_shift, sector_sizes])
    weights = weight_table.reshape(-1)
    count = states.shape[1]
    env = held_env[0, :, 0]
    parts = [shape(terms, LOW, block), shape(terms, block - LOW, block)]
    whole = shape(terms, block, block)
    split_states = [
        jax.ShapeDtypeStruct((count, 3 * block, block), jnp.bfloat16),
        jax.ShapeDtypeStruct((count, block, 3 * block), jnp.bfloat16),
    ]
    cost = estimate(block, terms)
    scalars = (place, weights)
    few = (place, weights)
    plain, turned, moved = None, None, None

    def call(kernel, inputs, outputs, aliases={}):
        specs = [SMEM if value.ndim == 1 else VMEM for value in inputs]
        specs = [HBM if value is incoming else spec for spec, value in zip(specs, inputs)]
        return pl.pallas_call(
            kernel,
            in_specs=specs,
            out_specs=[VMEM] * len(outputs),
            out_shape=outputs,
            input_output_aliases=aliases,
            compiler_params=PARAMS,
            cost_estimate=cost,
        )(*inputs)

    for tick in range(TICKS):
        relay, lift, far_one, far_two, stay = routes(tick, columns, sites, sectors)
        if tick == 0:
            two_low, two_high, plain, turned = call(
                first_kernel, scalars + (env, states), parts + split_states
            )
        else:
            two_low, two_high, env = call(
                functools.partial(gather_kernel, tick - 1),
                few + moved + (incoming, plain, turned),
                parts + [whole],
            )
        two_low = lax.ppermute(two_low, AXES, relay)
        far = lax.ppermute(two_high, AXES, far_one)
        if tick == 0:
            zero, plain, turned = call(
                first_zero_kernel,
                scalars + (env, states, plain, turned),
                [whole] + split_states,
                {4: 1, 5: 2},
            )
        else:
            (zero,) = call(zero_kernel, few + (env, plain, turned), [whole])
        kept = lax.ppermute(zero, AXES, stay)
        if tick == 0:
            one_low, one_high, plain, turned = call(
                first_one_kernel,
                scalars + (env, states, plain, turned),
                parts + split_states,
                {4: 2, 5: 3},
            )
        else:
            one_low, one_high = call(one_kernel, few + (env, plain, turned), parts)
        high = lax.ppermute(one_high, AXES, lift)
        low = lax.ppermute(one_low + two_low, AXES, lift)
        far = lax.ppermute(far, AXES, far_two)
        moved = (kept, low, high, far)
    (env,) = call(
        functools.partial(final_kernel, TICKS - 1), (place,) + moved + (incoming,), [whole]
    )
    return env[None, :, None]


def solution(mesh):
    return jax.shard_map(
        functools.partial(local, mesh.shape["site"]),
        mesh=mesh,
        in_specs=(
            P("site", None, "sector", None, None),
            P(None, None, "sector", None, None),
            P("site", None, "sector", None, None),
            P(),
            P("site"),
            P(),
            P(),
        ),
        out_specs=P("site", None, "sector", None, None),
        check_vma=False,
    )
```

profile of v0, /device:TPU:1, one launch (start us, length us, event | category | flops | bytes accessed | tf_op | source)
XLA Modules:
  0.0 308.5 jit_solution(592159245138352516)
XLA Ops:
  0.7 0.9 copy.13
  1.5 0.2 reshape.3.weights
  1.7 0.8 concatenate.3.place
  2.5 1.7 copy-done
  4.2 1.5 copy-done.1
  5.6 4.9 %shard_map.73 = (f32[3,144,384]{2,1,0:T(8,128)S(1)}, f32[3,240,384]{2,1,0:T(8,128)S(1)}, bf16[4,1152,384]{2,1,0:T(8,128)(2,1)S(1)}, bf16[4,384,1152]{2,1,0:T(8,128)(2,1)S(1)}) custom-call(s32[23]{0:T(128)S(1)} %concatenate.3.place, f32[576]{0:T(1024)S(1)} %reshape.3.weights, f32[3,384,384]{2,1,0:T(8,128)S(1)} %bitcast.8, f32[1,4,1,384,384]{4,3,2,1,0:T(8,128)S(1)} %copy-done), custom_call_target="tpu_custom_call" | custom-call | flops 2038431744 | bytes 7077888 | tf_op jit(solution)/shard_map/pallas_call | solution.py:216
  10.5 5.2 %collective-permute-start.4 = (f32[3,240,384]{2,1,0:T(8,128)S(1)}, f32[3,240,384]{2,1,0:T(8,128)S(1)}, u32[]{:S(2)}, u32[]{:S(2)}) collective-permute-start(f32[3,240,384]{2,1,0:T(8,128)S(1)} %get-tuple-element.39), channel_id=1, source_target_pairs={{0,3},{1,0},{2,5},{3,6},{4,7},{5,4},{6,9},{7,10},{8,11},{9,8},{10,... | collective-permute-start | bytes 3317768 | tf_op jit(solution)/shard_map/ppermute | solution.py:239
  15.7 4.9 %shard_map.74 = (f32[3,384,384]{2,1,0:T(8,128)S(1)}, bf16[4,1152,384]{2,1,0:T(8,128)(2,1)S(1)}, bf16[4,384,1152]{2,1,0:T(8,128)(2,1)S(1)}) custom-call(s32[23]{0:T(128)S(1)} %concatenate.3.place, f32[576]{0:T(1024)S(1)} %reshape.3.weights, f32[3,384,384]{2,1,0:T(8,128)S(1)} %bitcast.9, ...), custom_call_target="tpu_custom_call", output_to_operand_aliasing={{1}: (4, {}), {2}: (5, {})} | custom-call | flops 2038431744 | bytes 7077888 | tf_op jit(solution)/shard_map/pallas_call | solution.py:216
  20.6 4.1 %collective-permute-start = (f32[3,384,384]{2,1,0:T(8,128)S(1)}, f32[3,384,384]{2,1,0:T(8,128)S(1)}, u32[]{:S(2)}, u32[]{:S(2)}) collective-permute-start(f32[3,384,384]{2,1,0:T(8,128)S(1)} %get-tuple-element.33), channel_id=1, source_target_pairs={{0,16},{1,17},{2,18},{3,19},{4,20},{5,21},{6,22},{7,23},{8,24},{9,... | collective-permute-start | bytes 5308424 | tf_op jit(solution)/shard_map/ppermute | solution.py:249
  24.7 1.9 collective-permute-start.1
  26.6 0.0 slice-start
  26.6 0.0 slice-start.1
  26.6 9.2 %shard_map.75 = (f32[3,144,384]{2,1,0:T(8,128)S(1)}, f32[3,240,384]{2,1,0:T(8,128)S(1)}, bf16[4,1152,384]{2,1,0:T(8,128)(2,1)S(1)}, bf16[4,384,1152]{2,1,0:T(8,128)(2,1)S(1)}) custom-call(s32[23]{0:T(128)S(1)} %concatenate.3.place, f32[576]{0:T(1024)S(1)} %reshape.3.weights, ...), custom_call_target="tpu_custom_call", output_to_operand_aliasing={{2}: (4, {}), {3}: (5, {})} | custom-call | flops 2038431744 | bytes 7077888 | tf_op jit(solution)/shard_map/pallas_call | solution.py:216
  35.8 3.5 %collective-permute-start.3 = (f32[3,240,384]{2,1,0:T(8,128)S(1)}, f32[3,240,384]{2,1,0:T(8,128)S(1)}, u32[]{:S(2)}, u32[]{:S(2)}) collective-permute-start(f32[3,240,384]{2,1,0:T(8,128)S(1)} %get-tuple-element.38), channel_id=1, source_target_pairs={{0,17},{1,18},{2,19},{3,20},{4,21},{5,22},{6,23},{7,24},{8,25},{9,... | collective-permute-start | bytes 3317768 | tf_op jit(solution)/shard_map/ppermute | solution.py:259
  39.3 0.0 collective-permute-done.4
  39.3 7.2 %collective-permute-start.5 = (f32[3,240,384]{2,1,0:T(8,128)S(1)}, f32[3,240,384]{2,1,0:T(8,128)S(1)}, u32[]{:S(2)}, u32[]{:S(2)}) collective-permute-start(f32[3,240,384]{2,1,0:T(8,128)S(1)} %collective-permute-done.4), channel_id=1, source_target_pairs={{3,18},{0,19},{5,20},{6,21},{7,22},{4,23},{9,24},{10,25},{11,26},{... | collective-permute-start | bytes 3317768 | tf_op jit(solution)/shard_map/ppermute | solution.py:261
  46.5 0.0 collective-permute-done.1
  46.5 0.1 add.12
  46.6 2.7 collective-permute-start.2
  49.3 18.8 %collective-permute-done.3.high = f32[3,240,384]{2,1,0:T(8,128)S(1)} collective-permute-done((f32[3,240,384]{2,1,0:T(8,128)S(1)}, f32[3,240,384]{2,1,0:T(8,128)S(1)}, u32[]{:S(2)}, u32[]{:S(2)}) %collective-permute-start.3) | collective-permute-done | bytes 1105952 | tf_op jit(solution)/shard_map/ppermute | solution.py:259
  68.1 14.2 %collective-permute-done.2.low = f32[3,144,384]{2,1,0:T(8,128)S(1)} collective-permute-done((f32[3,144,384]{2,1,0:T(8,128)S(1)}, f32[3,144,384]{2,1,0:T(8,128)S(1)}, u32[]{:S(2)}, u32[]{:S(2)}) %collective-permute-start.2) | collective-permute-done | bytes 663584 | tf_op jit(solution)/shard_map/ppermute | solution.py:260
  82.3 0.0 collective-permute-done.stay
  82.3 5.0 %shard_map.76 = (f32[3,144,384]{2,1,0:T(8,128)S(1)}, f32[3,240,384]{2,1,0:T(8,128)S(1)}, f32[3,384,384]{2,1,0:T(8,128)S(1)}) custom-call(s32[23]{0:T(128)S(1)} %concatenate.3.place, f32[576]{0:T(1024)S(1)} %reshape.3.weights, f32[3,384,384]{2,1,0:T(8,128)S(1)} %collective-permute-done.stay, f32[3,144,384]{2,1,0:T(8,128)S(1)} %collective-permute-done.2.low, ...), custom_call_target="tpu_custom_call" | custom-call | flops 2038431744 | bytes 7077888 | tf_op jit(solution)/shard_map/pallas_call | solution.py:216
  87.3 1.9 collective-permute-start.10
  89.2 4.6 %shard_map.77 = f32[3,384,384]{2,1,0:T(8,128)S(1)} custom-call(s32[23]{0:T(128)S(1)} %concatenate.3.place, f32[576]{0:T(1024)S(1)} %reshape.3.weights, f32[3,384,384]{2,1,0:T(8,128)S(1)} %get-tuple-element.42.env, bf16[4,1152,384]{2,1,0:T(8,128)(2,1)S(1)} %get-tuple-element.40.plain, bf16[4,384,1152]{2,1,0:T(8,128)(2,1)S(1)} %get-tuple-element.41.turned), custom_call_target="tpu_custom_call" | custom-call | flops 2038431744 | bytes 7077888 | tf_op jit(solution)/shard_map/pallas_call | solution.py:216
  93.9 5.8 %collective-permute-start.6 = (f32[3,384,384]{2,1,0:T(8,128)S(1)}, f32[3,384,384]{2,1,0:T(8,128)S(1)}, u32[]{:S(2)}, u32[]{:S(2)}) collective-permute-start(f32[3,384,384]{2,1,0:T(8,128)S(1)} %shard_map.77), channel_id=1, source_target_pairs={{0,16},{1,17},{2,18},{3,19},{4,20},{5,21},{6,22},{7,23},{8,24},{9,... | collective-permute-start | bytes 5308424 | tf_op jit(solution)/shard_map/ppermute | solution.py:249
  99.7 3.6 %collective-permute-start.7 = (f32[3,144,384]{2,1,0:T(8,128)S(1)}, f32[3,144,384]{2,1,0:T(8,128)S(1)}, u32[]{:S(2)}, u32[]{:S(2)}) collective-permute-start(f32[3,144,384]{2,1,0:T(8,128)S(1)} %get-tuple-element.44), channel_id=1, source_target_pairs={{0,1},{1,2},{2,3},{3,4},{4,5},{5,6},{6,7},{7,8},{8,9},{9,10},{10,1... | collective-permute-start | bytes 1990664 | tf_op jit(solution)/shard_map/ppermute | solution.py:238
  103.3 8.7 %shard_map.78 = (f32[3,144,384]{2,1,0:T(8,128)S(1)}, f32[3,240,384]{2,1,0:T(8,128)S(1)}) custom-call(s32[23]{0:T(128)S(1)} %concatenate.3.place, f32[576]{0:T(1024)S(1)} %reshape.3.weights, f32[3,384,384]{2,1,0:T(8,128)S(1)} %get-tuple-element.42.env, bf16[4,1152,384]{2,1,0:T(8,128)(2,1)S(1)} %get-tuple-element.40.plain, ...), custom_call_target="tpu_custom_call" | custom-call | flops 2038431744 | bytes 7077888 | tf_op jit(solution)/shard_map/pallas_call | solution.py:216
  112.1 1.9 collective-permute-start.9
  114.0 7.1 %collective-permute-start.11 = (f32[3,240,384]{2,1,0:T(8,128)S(1)}, f32[3,240,384]{2,1,0:T(8,128)S(1)}, u32[]{:S(2)}, u32[]{:S(2)}) collective-permute-start(f32[3,240,384]{2,1,0:T(8,128)S(1)} %collective-permute-done.10), channel_id=1, source_target_pairs={{3,18},{0,19},{5,20},{6,21},{7,22},{4,23},{9,24},{10,25},{11,26},{... | collective-permute-start | bytes 3317768 | tf_op jit(solution)/shard_map/ppermute | solution.py:261
  121.1 0.0 collective-permute-done.7
  121.1 0.1 add.13
  121.2 1.9 collective-permute-start.8
  123.2 20.8 %collective-permute-done.9.high = f32[3,240,384]{2,1,0:T(8,128)S(1)} collective-permute-done((f32[3,240,384]{2,1,0:T(8,128)S(1)}, f32[3,240,384]{2,1,0:T(8,128)S(1)}, u32[]{:S(2)}, u32[]{:S(2)}) %collective-permute-start.9) | collective-permute-done | bytes 1105952 | tf_op jit(solution)/shard_map/ppermute | solution.py:259
  144.0 13.6 %collective-permute-done.8.low = f32[3,144,384]{2,1,0:T(8,128)S(1)} collective-permute-done((f32[3,144,384]{2,1,0:T(8,128)S(1)}, f32[3,144,384]{2,1,0:T(8,128)S(1)}, u32[]{:S(2)}, u32[]{:S(2)}) %collective-permute-start.8) | collective-permute-done | bytes 663584 | tf_op jit(solution)/shard_map/ppermute | solution.py:260
  157.6 5.0 %shard_map.79 = (f32[3,144,384]{2,1,0:T(8,128)S(1)}, f32[3,240,384]{2,1,0:T(8,128)S(1)}, f32[3,384,384]{2,1,0:T(8,128)S(1)}) custom-call(s32[23]{0:T(128)S(1)} %concatenate.3.place, f32[576]{0:T(1024)S(1)} %reshape.3.weights, f32[3,384,384]{2,1,0:T(8,128)S(1)} %collective-permute-done.6.stay, f32[3,144,384]{2,1,0:T(8,128)S(1)} %collective-permute-done.8.low, ...), custom_call_target="tpu_custom_call" | custom-call | flops 2038431744 | bytes 7077888 | tf_op jit(solution)/shard_map/pallas_call | solution.py:216
  162.6 2.1 collective-permute-start.16
  164.7 4.6 %shard_map.80 = f32[3,384,384]{2,1,0:T(8,128)S(1)} custom-call(s32[23]{0:T(128)S(1)} %concatenate.3.place, f32[576]{0:T(1024)S(1)} %reshape.3.weights, f32[3,384,384]{2,1,0:T(8,128)S(1)} %get-tuple-element.47.env, bf16[4,1152,384]{2,1,0:T(8,128)(2,1)S(1)} %get-tuple-element.40.plain, bf16[4,384,1152]{2,1,0:T(8,128)(2,1)S(1)} %get-tuple-element.41.turned), custom_call_target="tpu_custom_call" | custom-call | flops 2038431744 | bytes 7077888 | tf_op jit(solution)/shard_map/pallas_call | solution.py:216
  169.3 4.4 %collective-permute-start.12 = (f32[3,384,384]{2,1,0:T(8,128)S(1)}, f32[3,384,384]{2,1,0:T(8,128)S(1)}, u32[]{:S(2)}, u32[]{:S(2)}) collective-permute-start(f32[3,384,384]{2,1,0:T(8,128)S(1)} %shard_map.80), channel_id=1, source_target_pairs={{0,16},{1,17},{2,18},{3,19},{4,20},{5,21},{6,22},{7,23},{8,24},{9,... | collective-permute-start | bytes 5308424 | tf_op jit(solution)/shard_map/ppermute | solution.py:249
  173.8 3.6 %collective-permute-start.13 = (f32[3,144,384]{2,1,0:T(8,128)S(1)}, f32[3,144,384]{2,1,0:T(8,128)S(1)}, u32[]{:S(2)}, u32[]{:S(2)}) collective-permute-start(f32[3,144,384]{2,1,0:T(8,128)S(1)} %get-tuple-element.49), channel_id=1, source_target_pairs={{0,1},{1,2},{2,3},{3,4},{4,5},{5,6},{6,7},{7,8},{8,9},{9,10},{10,1... | collective-permute-start | bytes 1990664 | tf_op jit(solution)/shard_map/ppermute | solution.py:238
  177.4 8.7 %shard_map.81 = (f32[3,144,384]{2,1,0:T(8,128)S(1)}, f32[3,240,384]{2,1,0:T(8,128)S(1)}) custom-call(s32[23]{0:T(128)S(1)} %concatenate.3.place, f32[576]{0:T(1024)S(1)} %reshape.3.weights, f32[3,384,384]{2,1,0:T(8,128)S(1)} %get-tuple-element.47.env, bf16[4,1152,384]{2,1,0:T(8,128)(2,1)S(1)} %get-tuple-element.40.plain, ...), custom_call_target="tpu_custom_call" | custom-call | flops 2038431744 | bytes 7077888 | tf_op jit(solution)/shard_map/pallas_call | solution.py:216
  186.1 1.9 collective-permute-start.15
  188.1 7.9 %collective-permute-start.17 = (f32[3,240,384]{2,1,0:T(8,128)S(1)}, f32[3,240,384]{2,1,0:T(8,128)S(1)}, u32[]{:S(2)}, u32[]{:S(2)}) collective-permute-start(f32[3,240,384]{2,1,0:T(8,128)S(1)} %collective-permute-done.16), channel_id=1, source_target_pairs={{3,18},{0,19},{5,20},{6,21},{7,22},{4,23},{9,24},{10,25},{11,26},{... | collective-permute-start | bytes 3317768 | tf_op jit(solution)/shard_map/ppermute | solution.py:261
  196.0 0.0 collective-permute-done.13
  196.0 0.1 add.14
  196.1 1.9 collective-permute-start.14
  198.0 20.0 %collective-permute-done.15.high = f32[3,240,384]{2,1,0:T(8,128)S(1)} collective-permute-done((f32[3,240,384]{2,1,0:T(8,128)S(1)}, f32[3,240,384]{2,1,0:T(8,128)S(1)}, u32[]{:S(2)}, u32[]{:S(2)}) %collective-permute-start.15) | collective-permute-done | bytes 1105952 | tf_op jit(solution)/shard_map/ppermute | solution.py:259
  218.0 14.1 %collective-permute-done.14.low = f32[3,144,384]{2,1,0:T(8,128)S(1)} collective-permute-done((f32[3,144,384]{2,1,0:T(8,128)S(1)}, f32[3,144,384]{2,1,0:T(8,128)S(1)}, u32[]{:S(2)}, u32[]{:S(2)}) %collective-permute-start.14) | collective-permute-done | bytes 663584 | tf_op jit(solution)/shard_map/ppermute | solution.py:260
  232.1 0.0 collective-permute-done.12.stay
  232.1 0.0 collective-permute-done.17.far
  232.1 5.0 %shard_map.82 = (f32[3,144,384]{2,1,0:T(8,128)S(1)}, f32[3,240,384]{2,1,0:T(8,128)S(1)}, f32[3,384,384]{2,1,0:T(8,128)S(1)}) custom-call(s32[23]{0:T(128)S(1)} %concatenate.3.place, f32[576]{0:T(1024)S(1)} %reshape.3.weights, f32[3,384,384]{2,1,0:T(8,128)S(1)} %collective-permute-done.12.stay, f32[3,144,384]{2,1,0:T(8,128)S(1)} %collective-permute-done.14.low, ...), custom_call_target="tpu_custom_call" | custom-call | flops 2038431744 | bytes 7077888 | tf_op jit(solution)/shard_map/pallas_call | solution.py:216
  237.1 1.9 collective-permute-start.22
  239.0 4.6 %shard_map.83 = f32[3,384,384]{2,1,0:T(8,128)S(1)} custom-call(s32[23]{0:T(128)S(1)} %concatenate.3.place, f32[576]{0:T(1024)S(1)} %reshape.3.weights, f32[3,384,384]{2,1,0:T(8,128)S(1)} %get-tuple-element.52.env, bf16[4,1152,384]{2,1,0:T(8,128)(2,1)S(1)} %get-tuple-element.40.plain, bf16[4,384,1152]{2,1,0:T(8,128)(2,1)S(1)} %get-tuple-element.41.turned), custom_call_target="tpu_custom_call" | custom-call | flops 2038431744 | bytes 7077888 | tf_op jit(solution)/shard_map/pallas_call | solution.py:216
  243.7 4.5 %collective-permute-start.18 = (f32[3,384,384]{2,1,0:T(8,128)S(1)}, f32[3,384,384]{2,1,0:T(8,128)S(1)}, u32[]{:S(2)}, u32[]{:S(2)}) collective-permute-start(f32[3,384,384]{2,1,0:T(8,128)S(1)} %shard_map.83), channel_id=1, source_target_pairs={{0,16},{1,17},{2,18},{3,19},{4,20},{5,21},{6,22},{7,23},{8,24},{9,... | collective-permute-start | bytes 5308424 | tf_op jit(solution)/shard_map/ppermute | solution.py:249
  248.1 3.6 %collective-permute-start.19 = (f32[3,144,384]{2,1,0:T(8,128)S(1)}, f32[3,144,384]{2,1,0:T(8,128)S(1)}, u32[]{:S(2)}, u32[]{:S(2)}) collective-permute-start(f32[3,144,384]{2,1,0:T(8,128)S(1)} %get-tuple-element.54), channel_id=1, source_target_pairs={{0,1},{1,2},{2,3},{3,4},{4,5},{5,6},{6,7},{7,8},{8,9},{9,10},{10,1... | collective-permute-start | bytes 1990664 | tf_op jit(solution)/shard_map/ppermute | solution.py:238
  251.8 8.7 %shard_map.84 = (f32[3,144,384]{2,1,0:T(8,128)S(1)}, f32[3,240,384]{2,1,0:T(8,128)S(1)}) custom-call(s32[23]{0:T(128)S(1)} %concatenate.3.place, f32[576]{0:T(1024)S(1)} %reshape.3.weights, f32[3,384,384]{2,1,0:T(8,128)S(1)} %get-tuple-element.52.env, bf16[4,1152,384]{2,1,0:T(8,128)(2,1)S(1)} %get-tuple-element.40.plain, ...), custom_call_target="tpu_custom_call" | custom-call | flops 2038431744 | bytes 7077888 | tf_op jit(solution)/shard_map/pallas_call | solution.py:216
  260.5 1.9 collective-permute-start.21
  262.4 0.0 collective-permute-done.22
  262.4 8.0 %collective-permute-start.23 = (f32[3,240,384]{2,1,0:T(8,128)S(1)}, f32[3,240,384]{2,1,0:T(8,128)S(1)}, u32[]{:S(2)}, u32[]{:S(2)}) collective-permute-start(f32[3,240,384]{2,1,0:T(8,128)S(1)} %collective-permute-done.22), channel_id=1, source_target_pairs={{3,18},{0,19},{5,20},{6,21},{7,22},{4,23},{9,24},{10,25},{11,26},{... | collective-permute-start | bytes 3317768 | tf_op jit(solution)/shard_map/ppermute | solution.py:261
  270.5 0.1 add.15
  270.6 1.9 collective-permute-start.20
  272.5 19.9 %collective-permute-done.21.high = f32[3,240,384]{2,1,0:T(8,128)S(1)} collective-permute-done((f32[3,240,384]{2,1,0:T(8,128)S(1)}, f32[3,240,384]{2,1,0:T(8,128)S(1)}, u32[]{:S(2)}, u32[]{:S(2)}) %collective-permute-start.21) | collective-permute-done | bytes 1105952 | tf_op jit(solution)/shard_map/ppermute | solution.py:259
  292.4 14.0 %collective-permute-done.20.low = f32[3,144,384]{2,1,0:T(8,128)S(1)} collective-permute-done((f32[3,144,384]{2,1,0:T(8,128)S(1)}, f32[3,144,384]{2,1,0:T(8,128)S(1)}, u32[]{:S(2)}, u32[]{:S(2)}) %collective-permute-start.20) | collective-permute-done | bytes 663584 | tf_op jit(solution)/shard_map/ppermute | solution.py:260
  306.4 2.1 shard_map.85
  (13 shorter events, 0.0 us)
Async XLA Ops:
  2.5 1.7 copy-start
  4.2 1.5 copy-start.1
  10.5 28.8 %collective-permute-start.4 = (f32[3,240,384]{2,1,0:T(8,128)S(1)}, f32[3,240,384]{2,1,0:T(8,128)S(1)}, u32[]{:S(2)}, u32[]{:S(2)}) collective-permute-start(f32[3,240,384]{2,1,0:T(8,128)S(1)} %get-tuple-element.39), channel_id=1, source_target_pairs={{0,3},{1,0},{2,5},{3,6},{4,7},{5,4},{6,9},{7,10},{8,11},{9,8},{10,... | collective-permute-start | bytes 3317768 | tf_op jit(solution)/shard_map/ppermute | solution.py:239
  20.6 61.7 %collective-permute-start = (f32[3,384,384]{2,1,0:T(8,128)S(1)}, f32[3,384,384]{2,1,0:T(8,128)S(1)}, u32[]{:S(2)}, u32[]{:S(2)}) collective-permute-start(f32[3,384,384]{2,1,0:T(8,128)S(1)} %get-tuple-element.33), channel_id=1, source_target_pairs={{0,16},{1,17},{2,18},{3,19},{4,20},{5,21},{6,22},{7,23},{8,24},{9,... | collective-permute-start | bytes 5308424 | tf_op jit(solution)/shard_map/ppermute | solution.py:249
  24.7 21.9 %collective-permute-start.1 = (f32[3,144,384]{2,1,0:T(8,128)S(1)}, f32[3,144,384]{2,1,0:T(8,128)S(1)}, u32[]{:S(2)}, u32[]{:S(2)}) collective-permute-start(f32[3,144,384]{2,1,0:T(8,128)S(1)} %get-tuple-element.37), channel_id=1, source_target_pairs={{0,1},{1,2},{2,3},{3,4},{4,5},{5,6},{6,7},{7,8},{8,9},{9,10},{10,1... | collective-permute-start | bytes 1990664 | tf_op jit(solution)/shard_map/ppermute | solution.py:238
  26.6 55.7 %slice-start = ((s8[7077888]{0:T(1024)(128)(4,1)}), s8[4194304]{0:T(1024)(128)(4,1)S(1)}, s32[]{:S(2)}) async-start(s8[7077888]{0:T(1024)(128)(4,1)} %bitcast.6), calls=%async_computation | async-start | bytes 8388608
  26.6 55.7 %slice-start.1 = ((s8[7077888]{0:T(1024)(128)(4,1)}), s8[2883584]{0:T(1024)(128)(4,1)S(1)}, s32[]{:S(2)}) async-start(s8[7077888]{0:T(1024)(128)(4,1)} %bitcast.6), calls=%async_computation.1 | async-start | bytes 5767168
  35.8 32.2 %collective-permute-start.3 = (f32[3,240,384]{2,1,0:T(8,128)S(1)}, f32[3,240,384]{2,1,0:T(8,128)S(1)}, u32[]{:S(2)}, u32[]{:S(2)}) collective-permute-start(f32[3,240,384]{2,1,0:T(8,128)S(1)} %get-tuple-element.38), channel_id=1, source_target_pairs={{0,17},{1,18},{2,19},{3,20},{4,21},{5,22},{6,23},{7,24},{8,25},{9,... | collective-permute-start | bytes 3317768 | tf_op jit(solution)/shard_map/ppermute | solution.py:259
  39.3 43.0 %collective-permute-start.5 = (f32[3,240,384]{2,1,0:T(8,128)S(1)}, f32[3,240,384]{2,1,0:T(8,128)S(1)}, u32[]{:S(2)}, u32[]{:S(2)}) collective-permute-start(f32[3,240,384]{2,1,0:T(8,128)S(1)} %collective-permute-done.4), channel_id=1, source_target_pairs={{3,18},{0,19},{5,20},{6,21},{7,22},{4,23},{9,24},{10,25},{11,26},{... | collective-permute-start | bytes 3317768 | tf_op jit(solution)/shard_map/ppermute | solution.py:261
  46.6 35.7 %collective-permute-start.2 = (f32[3,144,384]{2,1,0:T(8,128)S(1)}, f32[3,144,384]{2,1,0:T(8,128)S(1)}, u32[]{:S(2)}, u32[]{:S(2)}) collective-permute-start(f32[3,144,384]{2,1,0:T(8,128)S(1)} %add.12), channel_id=1, source_target_pairs={{0,17},{1,18},{2,19},{3,20},{4,21},{5,22},{6,23},{7,24},{8,25},{9,... | collective-permute-start | bytes 1990664 | tf_op jit(solution)/shard_map/ppermute | solution.py:260
  87.3 26.7 %collective-permute-start.10 = (f32[3,240,384]{2,1,0:T(8,128)S(1)}, f32[3,240,384]{2,1,0:T(8,128)S(1)}, u32[]{:S(2)}, u32[]{:S(2)}) collective-permute-start(f32[3,240,384]{2,1,0:T(8,128)S(1)} %get-tuple-element.46), channel_id=1, source_target_pairs={{0,3},{1,0},{2,5},{3,6},{4,7},{5,4},{6,9},{7,10},{8,11},{9,8},{10,... | collective-permute-start | bytes 3317768 | tf_op jit(solution)/shard_map/ppermute | solution.py:239
  93.9 63.7 %collective-permute-start.6 = (f32[3,384,384]{2,1,0:T(8,128)S(1)}, f32[3,384,384]{2,1,0:T(8,128)S(1)}, u32[]{:S(2)}, u32[]{:S(2)}) collective-permute-start(f32[3,384,384]{2,1,0:T(8,128)S(1)} %shard_map.77), channel_id=1, source_target_pairs={{0,16},{1,17},{2,18},{3,19},{4,20},{5,21},{6,22},{7,23},{8,24},{9,... | collective-permute-start | bytes 5308424 | tf_op jit(solution)/shard_map/ppermute | solution.py:249
  99.7 21.4 %collective-permute-start.7 = (f32[3,144,384]{2,1,0:T(8,128)S(1)}, f32[3,144,384]{2,1,0:T(8,128)S(1)}, u32[]{:S(2)}, u32[]{:S(2)}) collective-permute-start(f32[3,144,384]{2,1,0:T(8,128)S(1)} %get-tuple-element.44), channel_id=1, source_target_pairs={{0,1},{1,2},{2,3},{3,4},{4,5},{5,6},{6,7},{7,8},{8,9},{9,10},{10,1... | collective-permute-start | bytes 1990664 | tf_op jit(solution)/shard_map/ppermute | solution.py:238
  112.1 31.9 %collective-permute-start.9 = (f32[3,240,384]{2,1,0:T(8,128)S(1)}, f32[3,240,384]{2,1,0:T(8,128)S(1)}, u32[]{:S(2)}, u32[]{:S(2)}) collective-permute-start(f32[3,240,384]{2,1,0:T(8,128)S(1)} %get-tuple-element.45), channel_id=1, source_target_pairs={{0,17},{1,18},{2,19},{3,20},{4,21},{5,22},{6,23},{7,24},{8,25},{9,... | collective-permute-start | bytes 3317768 | tf_op jit(solution)/shard_map/ppermute | solution.py:259
  114.0 43.6 %collective-permute-start.11 = (f32[3,240,384]{2,1,0:T(8,128)S(1)}, f32[3,240,384]{2,1,0:T(8,128)S(1)}, u32[]{:S(2)}, u32[]{:S(2)}) collective-permute-start(f32[3,240,384]{2,1,0:T(8,128)S(1)} %collective-permute-done.10), channel_id=1, source_target_pairs={{3,18},{0,19},{5,20},{6,21},{7,22},{4,23},{9,24},{10,25},{11,26},{... | collective-permute-start | bytes 3317768 | tf_op jit(solution)/shard_map/ppermute | solution.py:261
  121.2 36.4 %collective-permute-start.8 = (f32[3,144,384]{2,1,0:T(8,128)S(1)}, f32[3,144,384]{2,1,0:T(8,128)S(1)}, u32[]{:S(2)}, u32[]{:S(2)}) collective-permute-start(f32[3,144,384]{2,1,0:T(8,128)S(1)} %add.13), channel_id=1, source_target_pairs={{0,17},{1,18},{2,19},{3,20},{4,21},{5,22},{6,23},{7,24},{8,25},{9,... | collective-permute-start | bytes 1990664 | tf_op jit(solution)/shard_map/ppermute | solution.py:260
  162.6 25.4 %collective-permute-start.16 = (f32[3,240,384]{2,1,0:T(8,128)S(1)}, f32[3,240,384]{2,1,0:T(8,128)S(1)}, u32[]{:S(2)}, u32[]{:S(2)}) collective-permute-start(f32[3,240,384]{2,1,0:T(8,128)S(1)} %get-tuple-element.51), channel_id=1, source_target_pairs={{0,3},{1,0},{2,5},{3,6},{4,7},{5,4},{6,9},{7,10},{8,11},{9,8},{10,... | collective-permute-start | bytes 3317768 | tf_op jit(solution)/shard_map/ppermute | solution.py:239
  169.3 62.8 %collective-permute-start.12 = (f32[3,384,384]{2,1,0:T(8,128)S(1)}, f32[3,384,384]{2,1,0:T(8,128)S(1)}, u32[]{:S(2)}, u32[]{:S(2)}) collective-permute-start(f32[3,384,384]{2,1,0:T(8,128)S(1)} %shard_map.80), channel_id=1, source_target_pairs={{0,16},{1,17},{2,18},{3,19},{4,20},{5,21},{6,22},{7,23},{8,24},{9,... | collective-permute-start | bytes 5308424 | tf_op jit(solution)/shard_map/ppermute | solution.py:249
  173.8 22.2 %collective-permute-start.13 = (f32[3,144,384]{2,1,0:T(8,128)S(1)}, f32[3,144,384]{2,1,0:T(8,128)S(1)}, u32[]{:S(2)}, u32[]{:S(2)}) collective-permute-start(f32[3,144,384]{2,1,0:T(8,128)S(1)} %get-tuple-element.49), channel_id=1, source_target_pairs={{0,1},{1,2},{2,3},{3,4},{4,5},{5,6},{6,7},{7,8},{8,9},{9,10},{10,1... | collective-permute-start | bytes 1990664 | tf_op jit(solution)/shard_map/ppermute | solution.py:238
  186.1 31.9 %collective-permute-start.15 = (f32[3,240,384]{2,1,0:T(8,128)S(1)}, f32[3,240,384]{2,1,0:T(8,128)S(1)}, u32[]{:S(2)}, u32[]{:S(2)}) collective-permute-start(f32[3,240,384]{2,1,0:T(8,128)S(1)} %get-tuple-element.50), channel_id=1, source_target_pairs={{0,17},{1,18},{2,19},{3,20},{4,21},{5,22},{6,23},{7,24},{8,25},{9,... | collective-permute-start | bytes 3317768 | tf_op jit(solution)/shard_map/ppermute | solution.py:259
  188.1 44.0 %collective-permute-start.17 = (f32[3,240,384]{2,1,0:T(8,128)S(1)}, f32[3,240,384]{2,1,0:T(8,128)S(1)}, u32[]{:S(2)}, u32[]{:S(2)}) collective-permute-start(f32[3,240,384]{2,1,0:T(8,128)S(1)} %collective-permute-done.16), channel_id=1, source_target_pairs={{3,18},{0,19},{5,20},{6,21},{7,22},{4,23},{9,24},{10,25},{11,26},{... | collective-permute-start | bytes 3317768 | tf_op jit(solution)/shard_map/ppermute | solution.py:261
  196.1 36.0 %collective-permute-start.14 = (f32[3,144,384]{2,1,0:T(8,128)S(1)}, f32[3,144,384]{2,1,0:T(8,128)S(1)}, u32[]{:S(2)}, u32[]{:S(2)}) collective-permute-start(f32[3,144,384]{2,1,0:T(8,128)S(1)} %add.14), channel_id=1, source_target_pairs={{0,17},{1,18},{2,19},{3,20},{4,21},{5,22},{6,23},{7,24},{8,25},{9,... | collective-permute-start | bytes 1990664 | tf_op jit(solution)/shard_map/ppermute | solution.py:260
  237.1 25.3 %collective-permute-start.22 = (f32[3,240,384]{2,1,0:T(8,128)S(1)}, f32[3,240,384]{2,1,0:T(8,128)S(1)}, u32[]{:S(2)}, u32[]{:S(2)}) collective-permute-start(f32[3,240,384]{2,1,0:T(8,128)S(1)} %get-tuple-element.56), channel_id=1, source_target_pairs={{0,3},{1,0},{2,5},{3,6},{4,7},{5,4},{6,9},{7,10},{8,11},{9,8},{10,... | collective-permute-start | bytes 3317768 | tf_op jit(solution)/shard_map/ppermute | solution.py:239
  243.7 62.8 %collective-permute-start.18 = (f32[3,384,384]{2,1,0:T(8,128)S(1)}, f32[3,384,384]{2,1,0:T(8,128)S(1)}, u32[]{:S(2)}, u32[]{:S(2)}) collective-permute-start(f32[3,384,384]{2,1,0:T(8,128)S(1)} %shard_map.83), channel_id=1, source_target_pairs={{0,16},{1,17},{2,18},{3,19},{4,20},{5,21},{6,22},{7,23},{8,24},{9,... | collective-permute-start | bytes 5308424 | tf_op jit(solution)/shard_map/ppermute | solution.py:249
  248.1 22.3 %collective-permute-start.19 = (f32[3,144,384]{2,1,0:T(8,128)S(1)}, f32[3,144,384]{2,1,0:T(8,128)S(1)}, u32[]{:S(2)}, u32[]{:S(2)}) collective-permute-start(f32[3,144,384]{2,1,0:T(8,128)S(1)} %get-tuple-element.54), channel_id=1, source_target_pairs={{0,1},{1,2},{2,3},{3,4},{4,5},{5,6},{6,7},{7,8},{8,9},{9,10},{10,1... | collective-permute-start | bytes 1990664 | tf_op jit(solution)/shard_map/ppermute | solution.py:238
  260.5 31.9 %collective-permute-start.21 = (f32[3,240,384]{2,1,0:T(8,128)S(1)}, f32[3,240,384]{2,1,0:T(8,128)S(1)}, u32[]{:S(2)}, u32[]{:S(2)}) collective-permute-start(f32[3,240,384]{2,1,0:T(8,128)S(1)} %get-tuple-element.55), channel_id=1, source_target_pairs={{0,17},{1,18},{2,19},{3,20},{4,21},{5,22},{6,23},{7,24},{8,25},{9,... | collective-permute-start | bytes 3317768 | tf_op jit(solution)/shard_map/ppermute | solution.py:259
  262.4 44.0 %collective-permute-start.23 = (f32[3,240,384]{2,1,0:T(8,128)S(1)}, f32[3,240,384]{2,1,0:T(8,128)S(1)}, u32[]{:S(2)}, u32[]{:S(2)}) collective-permute-start(f32[3,240,384]{2,1,0:T(8,128)S(1)} %collective-permute-done.22), channel_id=1, source_target_pairs={{3,18},{0,19},{5,20},{6,21},{7,22},{4,23},{9,24},{10,25},{11,26},{... | collective-permute-start | bytes 3317768 | tf_op jit(solution)/shard_map/ppermute | solution.py:261
  270.6 35.9 %collective-permute-start.20 = (f32[3,144,384]{2,1,0:T(8,128)S(1)}, f32[3,144,384]{2,1,0:T(8,128)S(1)}, u32[]{:S(2)}, u32[]{:S(2)}) collective-permute-start(f32[3,144,384]{2,1,0:T(8,128)S(1)} %add.15), channel_id=1, source_target_pairs={{0,17},{1,18},{2,19},{3,20},{4,21},{5,22},{6,23},{7,24},{8,25},{9,... | collective-permute-start | bytes 1990664 | tf_op jit(solution)/shard_map/ppermute | solution.py:260
where the time goes:
time: 309 us
  waiting for transfers between devices  135 us (44%)
  starting transfers between devices  90.7 us (29%)
  Pallas kernels  75.9 us (25%)
  local copies, waits for them, and re-layouts  4.99 us (2%)
    ppermute x4, waiting for transfers between devices, local(): high = lax.ppermute(one_high, AXES, lift)  79.5 us
    pallas_call x13, Pallas kernels, call(): pl.pallas_call(kernel, in_specs=specs, out_specs=[VMEM] * len(outputs), o...  75.9 us
    ppermute x4, waiting for transfers between devices, local(): low = lax.ppermute(one_low + two_low, AXES, lift)  56 us
    ppermute x4, starting transfers between devices, local(): far = lax.ppermute(far, AXES, far_two)  30.3 us
    ppermute x4, starting transfers between devices, local(): kept = lax.ppermute(zero, AXES, stay)  18.8 us
    ppermute x4, starting transfers between devices, local(): two_low = lax.ppermute(two_low, AXES, relay)  12.8 us
    ppermute x4, starting transfers between devices, local(): far = lax.ppermute(two_high, AXES, far_one)  11.1 us
    ppermute x4, starting transfers between devices, local(): high = lax.ppermute(one_high, AXES, lift)  9.21 us
  transfers between devices with their start and end apart: 24, of which 8 were waited for; matrix products, arithmetic and copies ran while one was open for 0% of the time, Pallas kernels for 18%

commit v1 on v0

--- a/solution.py
+++ b/solution.py
@@ -10,7 +10,7 @@
 
 TICKS = 4
 AXES = ("site", "sector")
-LOW = 144
+LOW = 136
 VMEM = pl.BlockSpec(memory_space=pltpu.VMEM)
 SMEM = pl.BlockSpec(memory_space=pltpu.SMEM)
 HBM = pl.BlockSpec(memory_space=pltpu.HBM)
@@ -82,28 +82,16 @@
 
 def split_store(low_ref, high_ref):
     def store(term, value, first):
-        @pl.when(first)
-        def _():
-            low_ref[term] = value[:LOW]
-            high_ref[term] = value[LOW:]
-
-        @pl.when(jnp.logical_not(first))
-        def _():
-            low_ref[term] += value[:LOW]
-            high_ref[term] += value[LOW:]
+        low, high = low_ref[term], high_ref[term]
+        low_ref[term] = jnp.where(first, jnp.float32(0.0), low) + value[:LOW]
+        high_ref[term] = jnp.where(first, jnp.float32(0.0), high) + value[LOW:]
 
     return store
 
 
 def whole_store(ref):
     def store(term, value, first):
-        @pl.when(first)
-        def _():
-            ref[term] = value
-
-        @pl.when(jnp.logical_not(first))
-        def _():
-            ref[term] += value
+        ref[term] = jnp.where(first, jnp.float32(0.0), ref[term]) + value
 
     return store
 
@@ -185,8 +173,8 @@
             stay.append((here, (site + 1) * sectors + sector))
             target = (sector + 2) % sectors
             back = (target // columns) * columns + (target + 1) % columns
-            far_one.append((here, site * sectors + back))
-            far_two.append((site * sectors + back, (site + 1) * sectors + target))
+            far_one.append((here, (site + 1) * sectors + back))
+            far_two.append(((site + 1) * sectors + back, (site + 1) * sectors + target))
     return relay, lift, far_one, far_two, stay
 
 

time: 309 us -> 305 us (0.987)
  starting transfers between devices: 90.7 us -> 83.5 us
  waiting for transfers between devices: 135 us -> 139 us
    ppermute x4, starting transfers between devices: 30.3 us -> 9.74 us  [local(): far = lax.ppermute(far, AXES, far_two)]
    ppermute x4, starting transfers between devices: 8.43 us -> 22.4 us  [local(): low = lax.ppermute(one_low + two_low, AXES, lift)]
    ppermute x4, waiting for transfers between devices: 0.01 us -> 12.9 us  [local(): far = lax.ppermute(two_high, AXES, far_one)]
    ppermute x4, starting transfers between devices: 18.8 us -> 12.1 us  [local(): kept = lax.ppermute(zero, AXES, stay)]
    ppermute x4, waiting for transfers between devices: 79.5 us -> 72.9 us  [local(): high = lax.ppermute(one_high, AXES, lift)]
    ppermute x4, starting transfers between devices: 9.21 us -> 13.9 us  [local(): high = lax.ppermute(one_high, AXES, lift)]
    ppermute x4, waiting for transfers between devices: 56 us -> 52.5 us  [local(): low = lax.ppermute(one_low + two_low, AXES, lift)]
  transfers between devices with their start and end apart: 24 -> 24, of which waited for: 8 -> 14; matrix products, arithmetic and copies ran while one was open for 0% -> 0% of each run, Pallas kernels for 18% -> 17%
where the time goes in v1:
time: 305 us; the launch traced here: 303 us
  waiting for transfers between devices  139 us (46%)
  starting transfers between devices  83.5 us (27%)
  Pallas kernels  74.4 us (24%)
  local copies, waits for them, and re-layouts  4.99 us (2%)
    pallas_call x13, Pallas kernels, call(): pl.pallas_call(kernel, in_specs=specs, out_specs=[VMEM] * len(outputs), o...  74.4 us
    ppermute x4, waiting for transfers between devices, local(): high = lax.ppermute(one_high, AXES, lift)  72.9 us
    ppermute x4, waiting for transfers between devices, local(): low = lax.ppermute(one_low + two_low, AXES, lift)  52.5 us
    ppermute x4, starting transfers between devices, local(): low = lax.ppermute(one_low + two_low, AXES, lift)  22.4 us
    ppermute x4, starting transfers between devices, local(): high = lax.ppermute(one_high, AXES, lift)  13.9 us
    ppermute x4, starting transfers between devices, local(): far = lax.ppermute(two_high, AXES, far_one)  12.9 us
    ppermute x4, waiting for transfers between devices, local(): far = lax.ppermute(two_high, AXES, far_one)  12.9 us
    ppermute x4, starting transfers between devices, local(): two_low = lax.ppermute(two_low, AXES, relay)  12.5 us
  transfers between devices with their start and end apart: 24, of which 14 were waited for; matrix products, arithmetic and copies ran while one was open for 0% of the time, Pallas kernels for 17%

profile of v1, /device:TPU:1, one launch (start us, length us, event | category | flops | bytes accessed | tf_op | source)
XLA Modules:
  0.0 303.4 jit_solution(17875172170501348343)
XLA Ops:
  0.7 0.9 copy.13
  1.5 0.2 reshape.3.weights
  1.7 0.8 concatenate.3.place
  2.5 1.7 copy-done
  4.2 1.5 copy-done.1
  5.6 4.8 %shard_map.73 = (f32[3,136,384]{2,1,0:T(8,128)S(1)}, f32[3,248,384]{2,1,0:T(8,128)S(1)}, bf16[4,1152,384]{2,1,0:T(8,128)(2,1)S(1)}, bf16[4,384,1152]{2,1,0:T(8,128)(2,1)S(1)}) custom-call(s32[23]{0:T(128)S(1)} %concatenate.3.place, f32[576]{0:T(1024)S(1)} %reshape.3.weights, f32[3,384,384]{2,1,0:T(8,128)S(1)} %bitcast.8, f32[1,4,1,384,384]{4,3,2,1,0:T(8,128)S(1)} %copy-done), custom_call_target="tpu_custom_call" | custom-call | flops 2038431744 | bytes 7077888 | tf_op jit(solution)/shard_map/pallas_call | solution.py:204
  10.5 6.8 %collective-permute-start.4 = (f32[3,248,384]{2,1,0:T(8,128)S(1)}, f32[3,248,384]{2,1,0:T(8,128)S(1)}, u32[]{:S(2)}, u32[]{:S(2)}) collective-permute-start(f32[3,248,384]{2,1,0:T(8,128)S(1)} %get-tuple-element.39), channel_id=1, source_target_pairs={{0,19},{1,16},{2,21},{3,22},{4,23},{5,20},{6,25},{7,26},{8,27},{9,... | collective-permute-start | bytes 3428360 | tf_op jit(solution)/shard_map/ppermute | solution.py:227
  17.2 4.8 %shard_map.74 = (f32[3,384,384]{2,1,0:T(8,128)S(1)}, bf16[4,1152,384]{2,1,0:T(8,128)(2,1)S(1)}, bf16[4,384,1152]{2,1,0:T(8,128)(2,1)S(1)}) custom-call(s32[23]{0:T(128)S(1)} %concatenate.3.place, f32[576]{0:T(1024)S(1)} %reshape.3.weights, f32[3,384,384]{2,1,0:T(8,128)S(1)} %bitcast.9, ...), custom_call_target="tpu_custom_call", output_to_operand_aliasing={{1}: (4, {}), {2}: (5, {})} | custom-call | flops 2038431744 | bytes 7077888 | tf_op jit(solution)/shard_map/pallas_call | solution.py:204
  22.0 1.9 collective-permute-start
  24.0 1.9 collective-permute-start.1
  25.9 0.0 slice-start
  25.9 0.0 slice-start.1
  25.9 9.0 %shard_map.75 = (f32[3,136,384]{2,1,0:T(8,128)S(1)}, f32[3,248,384]{2,1,0:T(8,128)S(1)}, bf16[4,1152,384]{2,1,0:T(8,128)(2,1)S(1)}, bf16[4,384,1152]{2,1,0:T(8,128)(2,1)S(1)}) custom-call(s32[23]{0:T(128)S(1)} %concatenate.3.place, f32[576]{0:T(1024)S(1)} %reshape.3.weights, ...), custom_call_target="tpu_custom_call", output_to_operand_aliasing={{2}: (4, {}), {3}: (5, {})} | custom-call | flops 2038431744 | bytes 7077888 | tf_op jit(solution)/shard_map/pallas_call | solution.py:204
  34.9 5.1 %collective-permute-start.3 = (f32[3,248,384]{2,1,0:T(8,128)S(1)}, f32[3,248,384]{2,1,0:T(8,128)S(1)}, u32[]{:S(2)}, u32[]{:S(2)}) collective-permute-start(f32[3,248,384]{2,1,0:T(8,128)S(1)} %get-tuple-element.38), channel_id=1, source_target_pairs={{0,17},{1,18},{2,19},{3,20},{4,21},{5,22},{6,23},{7,24},{8,25},{9,... | collective-permute-start | bytes 3428360 | tf_op jit(solution)/shard_map/ppermute | solution.py:247
  40.0 1.2 collective-permute-done.4
  41.2 4.0 %collective-permute-start.5 = (f32[3,248,384]{2,1,0:T(8,128)S(1)}, f32[3,248,384]{2,1,0:T(8,128)S(1)}, u32[]{:S(2)}, u32[]{:S(2)}) collective-permute-start(f32[3,248,384]{2,1,0:T(8,128)S(1)} %collective-permute-done.4), channel_id=1, source_target_pairs={{19,18},{16,19},{21,20},{22,21},{23,22},{20,23},{25,24},{26,25},{2... | collective-permute-start | bytes 3428360 | tf_op jit(solution)/shard_map/ppermute | solution.py:249
  45.2 0.0 collective-permute-done.1
  45.2 0.1 add.12
  45.3 5.1 %collective-permute-start.2 = (f32[3,136,384]{2,1,0:T(8,128)S(1)}, f32[3,136,384]{2,1,0:T(8,128)S(1)}, u32[]{:S(2)}, u32[]{:S(2)}) collective-permute-start(f32[3,136,384]{2,1,0:T(8,128)S(1)} %add.12), channel_id=1, source_target_pairs={{0,17},{1,18},{2,19},{3,20},{4,21},{5,22},{6,23},{7,24},{8,25},{9,... | collective-permute-start | bytes 1880072 | tf_op jit(solution)/shard_map/ppermute | solution.py:248
  50.4 20.1 %collective-permute-done.3.high = f32[3,248,384]{2,1,0:T(8,128)S(1)} collective-permute-done((f32[3,248,384]{2,1,0:T(8,128)S(1)}, f32[3,248,384]{2,1,0:T(8,128)S(1)}, u32[]{:S(2)}, u32[]{:S(2)}) %collective-permute-start.3) | collective-permute-done | bytes 1142816 | tf_op jit(solution)/shard_map/ppermute | solution.py:247
  70.6 12.4 %collective-permute-done.2.low = f32[3,136,384]{2,1,0:T(8,128)S(1)} collective-permute-done((f32[3,136,384]{2,1,0:T(8,128)S(1)}, f32[3,136,384]{2,1,0:T(8,128)S(1)}, u32[]{:S(2)}, u32[]{:S(2)}) %collective-permute-start.2) | collective-permute-done | bytes 626720 | tf_op jit(solution)/shard_map/ppermute | solution.py:248
  83.0 0.0 collective-permute-done.stay
  83.0 4.9 %shard_map.76 = (f32[3,136,384]{2,1,0:T(8,128)S(1)}, f32[3,248,384]{2,1,0:T(8,128)S(1)}, f32[3,384,384]{2,1,0:T(8,128)S(1)}) custom-call(s32[23]{0:T(128)S(1)} %concatenate.3.place, f32[576]{0:T(1024)S(1)} %reshape.3.weights, f32[3,384,384]{2,1,0:T(8,128)S(1)} %collective-permute-done.stay, f32[3,136,384]{2,1,0:T(8,128)S(1)} %collective-permute-done.2.low, ...), custom_call_target="tpu_custom_call" | custom-call | flops 2038431744 | bytes 7077888 | tf_op jit(solution)/shard_map/pallas_call | solution.py:204
  87.9 2.1 collective-permute-start.10
  90.0 4.6 %shard_map.77 = f32[3,384,384]{2,1,0:T(8,128)S(1)} custom-call(s32[23]{0:T(128)S(1)} %concatenate.3.place, f32[576]{0:T(1024)S(1)} %reshape.3.weights, f32[3,384,384]{2,1,0:T(8,128)S(1)} %get-tuple-element.42.env, bf16[4,1152,384]{2,1,0:T(8,128)(2,1)S(1)} %get-tuple-element.40.plain, bf16[4,384,1152]{2,1,0:T(8,128)(2,1)S(1)} %get-tuple-element.41.turned), custom_call_target="tpu_custom_call" | custom-call | flops 2038431744 | bytes 7077888 | tf_op jit(solution)/shard_map/pallas_call | solution.py:204
  94.6 2.5 collective-permute-start.6
  97.1 4.1 %collective-permute-start.7 = (f32[3,136,384]{2,1,0:T(8,128)S(1)}, f32[3,136,384]{2,1,0:T(8,128)S(1)}, u32[]{:S(2)}, u32[]{:S(2)}) collective-permute-start(f32[3,136,384]{2,1,0:T(8,128)S(1)} %get-tuple-element.44), channel_id=1, source_target_pairs={{0,1},{1,2},{2,3},{3,4},{4,5},{5,6},{6,7},{7,8},{8,9},{9,10},{10,1... | collective-permute-start | bytes 1880072 | tf_op jit(solution)/shard_map/ppermute | solution.py:226
  101.2 8.5 %shard_map.78 = (f32[3,136,384]{2,1,0:T(8,128)S(1)}, f32[3,248,384]{2,1,0:T(8,128)S(1)}) custom-call(s32[23]{0:T(128)S(1)} %concatenate.3.place, f32[576]{0:T(1024)S(1)} %reshape.3.weights, f32[3,384,384]{2,1,0:T(8,128)S(1)} %get-tuple-element.42.env, bf16[4,1152,384]{2,1,0:T(8,128)(2,1)S(1)} %get-tuple-element.40.plain, ...), custom_call_target="tpu_custom_call" | custom-call | flops 2038431744 | bytes 7077888 | tf_op jit(solution)/shard_map/pallas_call | solution.py:204
  109.8 2.3 collective-permute-start.9
  112.0 5.5 %collective-permute-done.10 = f32[3,248,384]{2,1,0:T(8,128)S(1)} collective-permute-done((f32[3,248,384]{2,1,0:T(8,128)S(1)}, f32[3,248,384]{2,1,0:T(8,128)S(1)}, u32[]{:S(2)}, u32[]{:S(2)}) %collective-permute-start.10) | collective-permute-done | bytes 1142816 | tf_op jit(solution)/shard_map/ppermute | solution.py:227
  117.5 1.9 collective-permute-start.11
  119.4 0.1 add.13
  119.5 4.9 %collective-permute-start.8 = (f32[3,136,384]{2,1,0:T(8,128)S(1)}, f32[3,136,384]{2,1,0:T(8,128)S(1)}, u32[]{:S(2)}, u32[]{:S(2)}) collective-permute-start(f32[3,136,384]{2,1,0:T(8,128)S(1)} %add.13), channel_id=1, source_target_pairs={{0,17},{1,18},{2,19},{3,20},{4,21},{5,22},{6,23},{7,24},{8,25},{9,... | collective-permute-start | bytes 1880072 | tf_op jit(solution)/shard_map/ppermute | solution.py:248
  124.3 18.4 %collective-permute-done.9.high = f32[3,248,384]{2,1,0:T(8,128)S(1)} collective-permute-done((f32[3,248,384]{2,1,0:T(8,128)S(1)}, f32[3,248,384]{2,1,0:T(8,128)S(1)}, u32[]{:S(2)}, u32[]{:S(2)}) %collective-permute-start.9) | collective-permute-done | bytes 1142816 | tf_op jit(solution)/shard_map/ppermute | solution.py:247
  142.8 13.3 %collective-permute-done.8.low = f32[3,136,384]{2,1,0:T(8,128)S(1)} collective-permute-done((f32[3,136,384]{2,1,0:T(8,128)S(1)}, f32[3,136,384]{2,1,0:T(8,128)S(1)}, u32[]{:S(2)}, u32[]{:S(2)}) %collective-permute-start.8) | collective-permute-done | bytes 626720 | tf_op jit(solution)/shard_map/ppermute | solution.py:248
  156.1 4.9 %shard_map.79 = (f32[3,136,384]{2,1,0:T(8,128)S(1)}, f32[3,248,384]{2,1,0:T(8,128)S(1)}, f32[3,384,384]{2,1,0:T(8,128)S(1)}) custom-call(s32[23]{0:T(128)S(1)} %concatenate.3.place, f32[576]{0:T(1024)S(1)} %reshape.3.weights, f32[3,384,384]{2,1,0:T(8,128)S(1)} %collective-permute-done.6.stay, f32[3,136,384]{2,1,0:T(8,128)S(1)} %collective-permute-done.8.low, ...), custom_call_target="tpu_custom_call" | custom-call | flops 2038431744 | bytes 7077888 | tf_op jit(solution)/shard_map/pallas_call | solution.py:204
  160.9 2.1 collective-permute-start.16
  163.0 4.6 %shard_map.80 = f32[3,384,384]{2,1,0:T(8,128)S(1)} custom-call(s32[23]{0:T(128)S(1)} %concatenate.3.place, f32[576]{0:T(1024)S(1)} %reshape.3.weights, f32[3,384,384]{2,1,0:T(8,128)S(1)} %get-tuple-element.47.env, bf16[4,1152,384]{2,1,0:T(8,128)(2,1)S(1)} %get-tuple-element.40.plain, bf16[4,384,1152]{2,1,0:T(8,128)(2,1)S(1)} %get-tuple-element.41.turned), custom_call_target="tpu_custom_call" | custom-call | flops 2038431744 | bytes 7077888 | tf_op jit(solution)/shard_map/pallas_call | solution.py:204
  167.6 3.6 %collective-permute-start.12 = (f32[3,384,384]{2,1,0:T(8,128)S(1)}, f32[3,384,384]{2,1,0:T(8,128)S(1)}, u32[]{:S(2)}, u32[]{:S(2)}) collective-permute-start(f32[3,384,384]{2,1,0:T(8,128)S(1)} %shard_map.80), channel_id=1, source_target_pairs={{0,16},{1,17},{2,18},{3,19},{4,20},{5,21},{6,22},{7,23},{8,24},{9,... | collective-permute-start | bytes 5308424 | tf_op jit(solution)/shard_map/ppermute | solution.py:237
  171.2 3.3 %collective-permute-start.13 = (f32[3,136,384]{2,1,0:T(8,128)S(1)}, f32[3,136,384]{2,1,0:T(8,128)S(1)}, u32[]{:S(2)}, u32[]{:S(2)}) collective-permute-start(f32[3,136,384]{2,1,0:T(8,128)S(1)} %get-tuple-element.49), channel_id=1, source_target_pairs={{0,1},{1,2},{2,3},{3,4},{4,5},{5,6},{6,7},{7,8},{8,9},{9,10},{10,1... | collective-permute-start | bytes 1880072 | tf_op jit(solution)/shard_map/ppermute | solution.py:226
  174.5 8.5 %shard_map.81 = (f32[3,136,384]{2,1,0:T(8,128)S(1)}, f32[3,248,384]{2,1,0:T(8,128)S(1)}) custom-call(s32[23]{0:T(128)S(1)} %concatenate.3.place, f32[576]{0:T(1024)S(1)} %reshape.3.weights, f32[3,384,384]{2,1,0:T(8,128)S(1)} %get-tuple-element.47.env, bf16[4,1152,384]{2,1,0:T(8,128)(2,1)S(1)} %get-tuple-element.40.plain, ...), custom_call_target="tpu_custom_call" | custom-call | flops 2038431744 | bytes 7077888 | tf_op jit(solution)/shard_map/pallas_call | solution.py:204
  183.1 3.0 collective-permute-start.15
  186.1 3.7 %collective-permute-done.16 = f32[3,248,384]{2,1,0:T(8,128)S(1)} collective-permute-done((f32[3,248,384]{2,1,0:T(8,128)S(1)}, f32[3,248,384]{2,1,0:T(8,128)S(1)}, u32[]{:S(2)}, u32[]{:S(2)}) %collective-permute-start.16) | collective-permute-done | bytes 1142816 | tf_op jit(solution)/shard_map/ppermute | solution.py:227
  189.8 1.9 collective-permute-start.17
  191.7 0.4 collective-permute-done.13
  192.1 0.1 add.14
  192.2 5.8 %collective-permute-start.14 = (f32[3,136,384]{2,1,0:T(8,128)S(1)}, f32[3,136,384]{2,1,0:T(8,128)S(1)}, u32[]{:S(2)}, u32[]{:S(2)}) collective-permute-start(f32[3,136,384]{2,1,0:T(8,128)S(1)} %add.14), channel_id=1, source_target_pairs={{0,17},{1,18},{2,19},{3,20},{4,21},{5,22},{6,23},{7,24},{8,25},{9,... | collective-permute-start | bytes 1880072 | tf_op jit(solution)/shard_map/ppermute | solution.py:248
  197.9 17.8 %collective-permute-done.15.high = f32[3,248,384]{2,1,0:T(8,128)S(1)} collective-permute-done((f32[3,248,384]{2,1,0:T(8,128)S(1)}, f32[3,248,384]{2,1,0:T(8,128)S(1)}, u32[]{:S(2)}, u32[]{:S(2)}) %collective-permute-start.15) | collective-permute-done | bytes 1142816 | tf_op jit(solution)/shard_map/ppermute | solution.py:247
  215.7 13.4 %collective-permute-done.14.low = f32[3,136,384]{2,1,0:T(8,128)S(1)} collective-permute-done((f32[3,136,384]{2,1,0:T(8,128)S(1)}, f32[3,136,384]{2,1,0:T(8,128)S(1)}, u32[]{:S(2)}, u32[]{:S(2)}) %collective-permute-start.14) | collective-permute-done | bytes 626720 | tf_op jit(solution)/shard_map/ppermute | solution.py:248
  229.2 4.9 %shard_map.82 = (f32[3,136,384]{2,1,0:T(8,128)S(1)}, f32[3,248,384]{2,1,0:T(8,128)S(1)}, f32[3,384,384]{2,1,0:T(8,128)S(1)}) custom-call(s32[23]{0:T(128)S(1)} %concatenate.3.place, f32[576]{0:T(1024)S(1)} %reshape.3.weights, f32[3,384,384]{2,1,0:T(8,128)S(1)} %collective-permute-done.12.stay, f32[3,136,384]{2,1,0:T(8,128)S(1)} %collective-permute-done.14.low, ...), custom_call_target="tpu_custom_call" | custom-call | flops 2038431744 | bytes 7077888 | tf_op jit(solution)/shard_map/pallas_call | solution.py:204
  234.1 1.9 collective-permute-start.22
  236.0 4.6 %shard_map.83 = f32[3,384,384]{2,1,0:T(8,128)S(1)} custom-call(s32[23]{0:T(128)S(1)} %concatenate.3.place, f32[576]{0:T(1024)S(1)} %reshape.3.weights, f32[3,384,384]{2,1,0:T(8,128)S(1)} %get-tuple-element.52.env, bf16[4,1152,384]{2,1,0:T(8,128)(2,1)S(1)} %get-tuple-element.40.plain, bf16[4,384,1152]{2,1,0:T(8,128)(2,1)S(1)} %get-tuple-element.41.turned), custom_call_target="tpu_custom_call" | custom-call | flops 2038431744 | bytes 7077888 | tf_op jit(solution)/shard_map/pallas_call | solution.py:204
  240.6 4.1 %collective-permute-start.18 = (f32[3,384,384]{2,1,0:T(8,128)S(1)}, f32[3,384,384]{2,1,0:T(8,128)S(1)}, u32[]{:S(2)}, u32[]{:S(2)}) collective-permute-start(f32[3,384,384]{2,1,0:T(8,128)S(1)} %shard_map.83), channel_id=1, source_target_pairs={{0,16},{1,17},{2,18},{3,19},{4,20},{5,21},{6,22},{7,23},{8,24},{9,... | collective-permute-start | bytes 5308424 | tf_op jit(solution)/shard_map/ppermute | solution.py:237
  244.7 3.1 %collective-permute-start.19 = (f32[3,136,384]{2,1,0:T(8,128)S(1)}, f32[3,136,384]{2,1,0:T(8,128)S(1)}, u32[]{:S(2)}, u32[]{:S(2)}) collective-permute-start(f32[3,136,384]{2,1,0:T(8,128)S(1)} %get-tuple-element.54), channel_id=1, source_target_pairs={{0,1},{1,2},{2,3},{3,4},{4,5},{5,6},{6,7},{7,8},{8,9},{9,10},{10,1... | collective-permute-start | bytes 1880072 | tf_op jit(solution)/shard_map/ppermute | solution.py:226
  247.8 8.5 %shard_map.84 = (f32[3,136,384]{2,1,0:T(8,128)S(1)}, f32[3,248,384]{2,1,0:T(8,128)S(1)}) custom-call(s32[23]{0:T(128)S(1)} %concatenate.3.place, f32[576]{0:T(1024)S(1)} %reshape.3.weights, f32[3,384,384]{2,1,0:T(8,128)S(1)} %get-tuple-element.52.env, bf16[4,1152,384]{2,1,0:T(8,128)(2,1)S(1)} %get-tuple-element.40.plain, ...), custom_call_target="tpu_custom_call" | custom-call | flops 2038431744 | bytes 7077888 | tf_op jit(solution)/shard_map/pallas_call | solution.py:204
  256.3 3.5 %collective-permute-start.21 = (f32[3,248,384]{2,1,0:T(8,128)S(1)}, f32[3,248,384]{2,1,0:T(8,128)S(1)}, u32[]{:S(2)}, u32[]{:S(2)}) collective-permute-start(f32[3,248,384]{2,1,0:T(8,128)S(1)} %get-tuple-element.55), channel_id=1, source_target_pairs={{0,17},{1,18},{2,19},{3,20},{4,21},{5,22},{6,23},{7,24},{8,25},{9,... | collective-permute-start | bytes 3428360 | tf_op jit(solution)/shard_map/ppermute | solution.py:247
  259.8 2.6 collective-permute-done.22
  262.4 1.9 collective-permute-start.23
  264.3 0.4 collective-permute-done.19
  264.7 0.1 add.15
  264.8 6.7 %collective-permute-start.20 = (f32[3,136,384]{2,1,0:T(8,128)S(1)}, f32[3,136,384]{2,1,0:T(8,128)S(1)}, u32[]{:S(2)}, u32[]{:S(2)}) collective-permute-start(f32[3,136,384]{2,1,0:T(8,128)S(1)} %add.15), channel_id=1, source_target_pairs={{0,17},{1,18},{2,19},{3,20},{4,21},{5,22},{6,23},{7,24},{8,25},{9,... | collective-permute-start | bytes 1880072 | tf_op jit(solution)/shard_map/ppermute | solution.py:248
  271.5 16.5 %collective-permute-done.21.high = f32[3,248,384]{2,1,0:T(8,128)S(1)} collective-permute-done((f32[3,248,384]{2,1,0:T(8,128)S(1)}, f32[3,248,384]{2,1,0:T(8,128)S(1)}, u32[]{:S(2)}, u32[]{:S(2)}) %collective-permute-start.21) | collective-permute-done | bytes 1142816 | tf_op jit(solution)/shard_map/ppermute | solution.py:247
  287.9 13.4 %collective-permute-done.20.low = f32[3,136,384]{2,1,0:T(8,128)S(1)} collective-permute-done((f32[3,136,384]{2,1,0:T(8,128)S(1)}, f32[3,136,384]{2,1,0:T(8,128)S(1)}, u32[]{:S(2)}, u32[]{:S(2)}) %collective-permute-start.20) | collective-permute-done | bytes 626720 | tf_op jit(solution)/shard_map/ppermute | solution.py:248
  301.4 2.0 shard_map.85
  (13 shorter events, 0.0 us)
Async XLA Ops:
  2.5 1.7 copy-start
  4.2 1.5 copy-start.1
  10.5 30.8 %collective-permute-start.4 = (f32[3,248,384]{2,1,0:T(8,128)S(1)}, f32[3,248,384]{2,1,0:T(8,128)S(1)}, u32[]{:S(2)}, u32[]{:S(2)}) collective-permute-start(f32[3,248,384]{2,1,0:T(8,128)S(1)} %get-tuple-element.39), channel_id=1, source_target_pairs={{0,19},{1,16},{2,21},{3,22},{4,23},{5,20},{6,25},{7,26},{8,27},{9,... | collective-permute-start | bytes 3428360 | tf_op jit(solution)/shard_map/ppermute | solution.py:227
  22.0 60.9 %collective-permute-start = (f32[3,384,384]{2,1,0:T(8,128)S(1)}, f32[3,384,384]{2,1,0:T(8,128)S(1)}, u32[]{:S(2)}, u32[]{:S(2)}) collective-permute-start(f32[3,384,384]{2,1,0:T(8,128)S(1)} %get-tuple-element.33), channel_id=1, source_target_pairs={{0,16},{1,17},{2,18},{3,19},{4,20},{5,21},{6,22},{7,23},{8,24},{9,... | collective-permute-start | bytes 5308424 | tf_op jit(solution)/shard_map/ppermute | solution.py:237
  24.0 21.3 %collective-permute-start.1 = (f32[3,136,384]{2,1,0:T(8,128)S(1)}, f32[3,136,384]{2,1,0:T(8,128)S(1)}, u32[]{:S(2)}, u32[]{:S(2)}) collective-permute-start(f32[3,136,384]{2,1,0:T(8,128)S(1)} %get-tuple-element.37), channel_id=1, source_target_pairs={{0,1},{1,2},{2,3},{3,4},{4,5},{5,6},{6,7},{7,8},{8,9},{9,10},{10,1... | collective-permute-start | bytes 1880072 | tf_op jit(solution)/shard_map/ppermute | solution.py:226
  25.9 57.1 %slice-start = ((s8[7077888]{0:T(1024)(128)(4,1)}), s8[4194304]{0:T(1024)(128)(4,1)S(1)}, s32[]{:S(2)}) async-start(s8[7077888]{0:T(1024)(128)(4,1)} %bitcast.6), calls=%async_computation | async-start | bytes 8388608
  25.9 57.0 %slice-start.1 = ((s8[7077888]{0:T(1024)(128)(4,1)}), s8[2883584]{0:T(1024)(128)(4,1)S(1)}, s32[]{:S(2)}) async-start(s8[7077888]{0:T(1024)(128)(4,1)} %bitcast.6), calls=%async_computation.1 | async-start | bytes 5767168
  34.9 35.7 %collective-permute-start.3 = (f32[3,248,384]{2,1,0:T(8,128)S(1)}, f32[3,248,384]{2,1,0:T(8,128)S(1)}, u32[]{:S(2)}, u32[]{:S(2)}) collective-permute-start(f32[3,248,384]{2,1,0:T(8,128)S(1)} %get-tuple-element.38), channel_id=1, source_target_pairs={{0,17},{1,18},{2,19},{3,20},{4,21},{5,22},{6,23},{7,24},{8,25},{9,... | collective-permute-start | bytes 3428360 | tf_op jit(solution)/shard_map/ppermute | solution.py:247
  41.2 41.7 %collective-permute-start.5 = (f32[3,248,384]{2,1,0:T(8,128)S(1)}, f32[3,248,384]{2,1,0:T(8,128)S(1)}, u32[]{:S(2)}, u32[]{:S(2)}) collective-permute-start(f32[3,248,384]{2,1,0:T(8,128)S(1)} %collective-permute-done.4), channel_id=1, source_target_pairs={{19,18},{16,19},{21,20},{22,21},{23,22},{20,23},{25,24},{26,25},{2... | collective-permute-start | bytes 3428360 | tf_op jit(solution)/shard_map/ppermute | solution.py:249
  45.3 37.6 %collective-permute-start.2 = (f32[3,136,384]{2,1,0:T(8,128)S(1)}, f32[3,136,384]{2,1,0:T(8,128)S(1)}, u32[]{:S(2)}, u32[]{:S(2)}) collective-permute-start(f32[3,136,384]{2,1,0:T(8,128)S(1)} %add.12), channel_id=1, source_target_pairs={{0,17},{1,18},{2,19},{3,20},{4,21},{5,22},{6,23},{7,24},{8,25},{9,... | collective-permute-start | bytes 1880072 | tf_op jit(solution)/shard_map/ppermute | solution.py:248
  87.9 29.6 %collective-permute-start.10 = (f32[3,248,384]{2,1,0:T(8,128)S(1)}, f32[3,248,384]{2,1,0:T(8,128)S(1)}, u32[]{:S(2)}, u32[]{:S(2)}) collective-permute-start(f32[3,248,384]{2,1,0:T(8,128)S(1)} %get-tuple-element.46), channel_id=1, source_target_pairs={{0,19},{1,16},{2,21},{3,22},{4,23},{5,20},{6,25},{7,26},{8,27},{9,... | collective-permute-start | bytes 3428360 | tf_op jit(solution)/shard_map/ppermute | solution.py:227
  94.6 61.4 %collective-permute-start.6 = (f32[3,384,384]{2,1,0:T(8,128)S(1)}, f32[3,384,384]{2,1,0:T(8,128)S(1)}, u32[]{:S(2)}, u32[]{:S(2)}) collective-permute-start(f32[3,384,384]{2,1,0:T(8,128)S(1)} %shard_map.77), channel_id=1, source_target_pairs={{0,16},{1,17},{2,18},{3,19},{4,20},{5,21},{6,22},{7,23},{8,24},{9,... | collective-permute-start | bytes 5308424 | tf_op jit(solution)/shard_map/ppermute | solution.py:237
  97.1 22.3 %collective-permute-start.7 = (f32[3,136,384]{2,1,0:T(8,128)S(1)}, f32[3,136,384]{2,1,0:T(8,128)S(1)}, u32[]{:S(2)}, u32[]{:S(2)}) collective-permute-start(f32[3,136,384]{2,1,0:T(8,128)S(1)} %get-tuple-element.44), channel_id=1, source_target_pairs={{0,1},{1,2},{2,3},{3,4},{4,5},{5,6},{6,7},{7,8},{8,9},{9,10},{10,1... | collective-permute-start | bytes 1880072 | tf_op jit(solution)/shard_map/ppermute | solution.py:226
  109.8 33.0 %collective-permute-start.9 = (f32[3,248,384]{2,1,0:T(8,128)S(1)}, f32[3,248,384]{2,1,0:T(8,128)S(1)}, u32[]{:S(2)}, u32[]{:S(2)}) collective-permute-start(f32[3,248,384]{2,1,0:T(8,128)S(1)} %get-tuple-element.45), channel_id=1, source_target_pairs={{0,17},{1,18},{2,19},{3,20},{4,21},{5,22},{6,23},{7,24},{8,25},{9,... | collective-permute-start | bytes 3428360 | tf_op jit(solution)/shard_map/ppermute | solution.py:247
  117.5 38.6 %collective-permute-start.11 = (f32[3,248,384]{2,1,0:T(8,128)S(1)}, f32[3,248,384]{2,1,0:T(8,128)S(1)}, u32[]{:S(2)}, u32[]{:S(2)}) collective-permute-start(f32[3,248,384]{2,1,0:T(8,128)S(1)} %collective-permute-done.10), channel_id=1, source_target_pairs={{19,18},{16,19},{21,20},{22,21},{23,22},{20,23},{25,24},{26,25},{2... | collective-permute-start | bytes 3428360 | tf_op jit(solution)/shard_map/ppermute | solution.py:249
  119.5 36.6 %collective-permute-start.8 = (f32[3,136,384]{2,1,0:T(8,128)S(1)}, f32[3,136,384]{2,1,0:T(8,128)S(1)}, u32[]{:S(2)}, u32[]{:S(2)}) collective-permute-start(f32[3,136,384]{2,1,0:T(8,128)S(1)} %add.13), channel_id=1, source_target_pairs={{0,17},{1,18},{2,19},{3,20},{4,21},{5,22},{6,23},{7,24},{8,25},{9,... | collective-permute-start | bytes 1880072 | tf_op jit(solution)/shard_map/ppermute | solution.py:248
  160.9 28.9 %collective-permute-start.16 = (f32[3,248,384]{2,1,0:T(8,128)S(1)}, f32[3,248,384]{2,1,0:T(8,128)S(1)}, u32[]{:S(2)}, u32[]{:S(2)}) collective-permute-start(f32[3,248,384]{2,1,0:T(8,128)S(1)} %get-tuple-element.51), channel_id=1, source_target_pairs={{0,19},{1,16},{2,21},{3,22},{4,23},{5,20},{6,25},{7,26},{8,27},{9,... | collective-permute-start | bytes 3428360 | tf_op jit(solution)/shard_map/ppermute | solution.py:227
  167.6 61.6 %collective-permute-start.12 = (f32[3,384,384]{2,1,0:T(8,128)S(1)}, f32[3,384,384]{2,1,0:T(8,128)S(1)}, u32[]{:S(2)}, u32[]{:S(2)}) collective-permute-start(f32[3,384,384]{2,1,0:T(8,128)S(1)} %shard_map.80), channel_id=1, source_target_pairs={{0,16},{1,17},{2,18},{3,19},{4,20},{5,21},{6,22},{7,23},{8,24},{9,... | collective-permute-start | bytes 5308424 | tf_op jit(solution)/shard_map/ppermute | solution.py:237
  171.2 20.9 %collective-permute-start.13 = (f32[3,136,384]{2,1,0:T(8,128)S(1)}, f32[3,136,384]{2,1,0:T(8,128)S(1)}, u32[]{:S(2)}, u32[]{:S(2)}) collective-permute-start(f32[3,136,384]{2,1,0:T(8,128)S(1)} %get-tuple-element.49), channel_id=1, source_target_pairs={{0,1},{1,2},{2,3},{3,4},{4,5},{5,6},{6,7},{7,8},{8,9},{9,10},{10,1... | collective-permute-start | bytes 1880072 | tf_op jit(solution)/shard_map/ppermute | solution.py:226
  183.1 32.7 %collective-permute-start.15 = (f32[3,248,384]{2,1,0:T(8,128)S(1)}, f32[3,248,384]{2,1,0:T(8,128)S(1)}, u32[]{:S(2)}, u32[]{:S(2)}) collective-permute-start(f32[3,248,384]{2,1,0:T(8,128)S(1)} %get-tuple-element.50), channel_id=1, source_target_pairs={{0,17},{1,18},{2,19},{3,20},{4,21},{5,22},{6,23},{7,24},{8,25},{9,... | collective-permute-start | bytes 3428360 | tf_op jit(solution)/shard_map/ppermute | solution.py:247
  189.8 39.4 %collective-permute-start.17 = (f32[3,248,384]{2,1,0:T(8,128)S(1)}, f32[3,248,384]{2,1,0:T(8,128)S(1)}, u32[]{:S(2)}, u32[]{:S(2)}) collective-permute-start(f32[3,248,384]{2,1,0:T(8,128)S(1)} %collective-permute-done.16), channel_id=1, source_target_pairs={{19,18},{16,19},{21,20},{22,21},{23,22},{20,23},{25,24},{26,25},{2... | collective-permute-start | bytes 3428360 | tf_op jit(solution)/shard_map/ppermute | solution.py:249
  192.2 37.0 %collective-permute-start.14 = (f32[3,136,384]{2,1,0:T(8,128)S(1)}, f32[3,136,384]{2,1,0:T(8,128)S(1)}, u32[]{:S(2)}, u32[]{:S(2)}) collective-permute-start(f32[3,136,384]{2,1,0:T(8,128)S(1)} %add.14), channel_id=1, source_target_pairs={{0,17},{1,18},{2,19},{3,20},{4,21},{5,22},{6,23},{7,24},{8,25},{9,... | collective-permute-start | bytes 1880072 | tf_op jit(solution)/shard_map/ppermute | solution.py:248
  234.1 28.3 %collective-permute-start.22 = (f32[3,248,384]{2,1,0:T(8,128)S(1)}, f32[3,248,384]{2,1,0:T(8,128)S(1)}, u32[]{:S(2)}, u32[]{:S(2)}) collective-permute-start(f32[3,248,384]{2,1,0:T(8,128)S(1)} %get-tuple-element.56), channel_id=1, source_target_pairs={{0,19},{1,16},{2,21},{3,22},{4,23},{5,20},{6,25},{7,26},{8,27},{9,... | collective-permute-start | bytes 3428360 | tf_op jit(solution)/shard_map/ppermute | solution.py:227
  240.6 60.8 %collective-permute-start.18 = (f32[3,384,384]{2,1,0:T(8,128)S(1)}, f32[3,384,384]{2,1,0:T(8,128)S(1)}, u32[]{:S(2)}, u32[]{:S(2)}) collective-permute-start(f32[3,384,384]{2,1,0:T(8,128)S(1)} %shard_map.83), channel_id=1, source_target_pairs={{0,16},{1,17},{2,18},{3,19},{4,20},{5,21},{6,22},{7,23},{8,24},{9,... | collective-permute-start | bytes 5308424 | tf_op jit(solution)/shard_map/ppermute | solution.py:237
  244.7 20.0 %collective-permute-start.19 = (f32[3,136,384]{2,1,0:T(8,128)S(1)}, f32[3,136,384]{2,1,0:T(8,128)S(1)}, u32[]{:S(2)}, u32[]{:S(2)}) collective-permute-start(f32[3,136,384]{2,1,0:T(8,128)S(1)} %get-tuple-element.54), channel_id=1, source_target_pairs={{0,1},{1,2},{2,3},{3,4},{4,5},{5,6},{6,7},{7,8},{8,9},{9,10},{10,1... | collective-permute-start | bytes 1880072 | tf_op jit(solution)/shard_map/ppermute | solution.py:226
  256.3 31.6 %collective-permute-start.21 = (f32[3,248,384]{2,1,0:T(8,128)S(1)}, f32[3,248,384]{2,1,0:T(8,128)S(1)}, u32[]{:S(2)}, u32[]{:S(2)}) collective-permute-start(f32[3,248,384]{2,1,0:T(8,128)S(1)} %get-tuple-element.55), channel_id=1, source_target_pairs={{0,17},{1,18},{2,19},{3,20},{4,21},{5,22},{6,23},{7,24},{8,25},{9,... | collective-permute-start | bytes 3428360 | tf_op jit(solution)/shard_map/ppermute | solution.py:247
  262.4 39.0 %collective-permute-start.23 = (f32[3,248,384]{2,1,0:T(8,128)S(1)}, f32[3,248,384]{2,1,0:T(8,128)S(1)}, u32[]{:S(2)}, u32[]{:S(2)}) collective-permute-start(f32[3,248,384]{2,1,0:T(8,128)S(1)} %collective-permute-done.22), channel_id=1, source_target_pairs={{19,18},{16,19},{21,20},{22,21},{23,22},{20,23},{25,24},{26,25},{2... | collective-permute-start | bytes 3428360 | tf_op jit(solution)/shard_map/ppermute | solution.py:249
  264.8 36.6 %collective-permute-start.20 = (f32[3,136,384]{2,1,0:T(8,128)S(1)}, f32[3,136,384]{2,1,0:T(8,128)S(1)}, u32[]{:S(2)}, u32[]{:S(2)}) collective-permute-start(f32[3,136,384]{2,1,0:T(8,128)S(1)} %add.15), channel_id=1, source_target_pairs={{0,17},{1,18},{2,19},{3,20},{4,21},{5,22},{6,23},{7,24},{8,25},{9,... | collective-permute-start | bytes 1880072 | tf_op jit(solution)/shard_map/ppermute | solution.py:248

commit v2 on v1

v2 whole, which is shorter than its diff:
```python
import functools

import jax
import jax.numpy as jnp
from jax import lax
from jax.experimental import pallas as pl
from jax.experimental.pallas import tpu as pltpu
from jax.sharding import PartitionSpec as P


TICKS = 4
AXES = ("site", "sector")
LOW = 128
VMEM = pl.BlockSpec(memory_space=pltpu.VMEM)
SMEM = pl.BlockSpec(memory_space=pltpu.SMEM)
HBM = pl.BlockSpec(memory_space=pltpu.HBM)
PARAMS = pltpu.CompilerParams(vmem_limit_bytes=24 * 1024 * 1024)


def halves(value):
    high = value.astype(jnp.bfloat16)
    return high, (value - high.astype(jnp.float32)).astype(jnp.bfloat16)


def dot(left, right):
    return jnp.dot(left, right, preferred_element_type=jnp.float32)


def shift_of(place, state):
    return place[3 + state]


def fill(state, place, count, states_ref, plain_ref, turned_ref):
    block = states_ref.shape[-1]
    owner = place[1]
    sectors = place.shape[0] - 3 - count
    live_in = place[3 + count + owner]
    live_out = place[3 + count + lax.rem(owner + shift_of(place, state), sectors)]
    rows = lax.broadcasted_iota(jnp.int32, (block, block), 0)
    columns = lax.broadcasted_iota(jnp.int32, (block, block), 1)
    keep = (rows < live_in) & (columns < live_out)
    masked = jnp.where(keep, states_ref[0, state, 0], jnp.float32(0.0))
    high, low = halves(masked)
    plain_ref[state, 0:block, :] = high
    plain_ref[state, block : 2 * block, :] = low
    plain_ref[state, 2 * block :, :] = high
    high, low = halves(masked.T)
    turned_ref[state, :, 0:block] = high
    turned_ref[state, :, block : 2 * block] = high
    turned_ref[state, :, 2 * block :] = low


def each_state(offset, place, count, body):
    def one_state(state, found):
        mine = shift_of(place, state) == offset

        @pl.when(mine)
        def _():
            body(state, found == 0)

        return found + mine.astype(jnp.int32)

    lax.fori_loop(0, count, one_state, jnp.int32(0))


def mix(place, weights, count, state, out_term, env_refs):
    pieces = []
    for ref in env_refs:
        terms = ref.shape[0]
        base = (place[2] * count + state) * terms * terms + out_term
        mixed = weights[base] * ref[0]
        for term in range(1, terms):
            mixed += weights[base + term * terms] * ref[term]
        pieces.append(mixed)
    return pieces[0] if len(pieces) == 1 else jnp.concatenate(pieces, axis=0)


def products(offset, place, weights, env_refs, plain_ref, turned_ref, stores, ready=None):
    count = plain_ref.shape[0]

    def body(state, first):
        if ready is not None:
            ready(state)

        @pl.loop(0, env_refs[0].shape[0])
        def _(out_term):
            high, low = halves(mix(place, weights, count, state, out_term, env_refs))
            right = dot(turned_ref[state], jnp.concatenate([high, low, high], axis=0))
            high, low = halves(right)
            triple = dot(jnp.concatenate([high, high, low], axis=1), plain_ref[state])
            row = 0
            for ref in stores:
                rows = ref.shape[1]
                before = jnp.where(first, jnp.float32(0.0), ref[out_term])
                ref[out_term] = before + triple[row : row + rows]
                row += rows

    each_state(offset, place, count, body)


def row_products(place, weights, env_ref, start, plain_ref, turned_ref, combine):
    count = plain_ref.shape[0]
    rows, block = env_ref.shape[1], env_ref.shape[2]

    def body(state, first):
        @pl.loop(0, env_ref.shape[0])
        def _(out_term):
            high, low = halves(mix(place, weights, count, state, out_term, [env_ref]))
            right = dot(jnp.concatenate([high, high, low], axis=1), plain_ref[state])
            high, low = halves(right)
            left = [
                turned_ref[state, :, part * block + start : part * block + start + rows]
                for part in range(3)
            ]
            triple = dot(
                jnp.concatenate(left, axis=1), jnp.concatenate([high, low, high], axis=0)
            )
            combine(out_term, triple, first)

    each_state(2, place, count, body)


def early_kernel(tick, place, weights, stay, high, far_a, far_b, incoming, plain, turned,
                 env_high, part):
    @pl.when(place[0] == 0)
    def _():
        pltpu.sync_copy(incoming.at[tick, :, 0, LOW:], env_high)

    @pl.when(place[0] != 0)
    def _():
        half = far_a.shape[1]
        env_high[:, :half] = stay[:, LOW : LOW + half] + high[:, :half] + far_a[...]
        env_high[:, half:] = stay[:, LOW + half :] + high[:, half:] + far_b[...]

    def combine(term, value, first):
        part[term] = jnp.where(first, jnp.float32(0.0), part[term]) + value

    row_products(place, weights, env_high, LOW, plain, turned, combine)


def late_kernel(tick, place, weights, stay, low, part, incoming, plain, turned,
                out_low, out_a, out_b, env_low):
    @pl.when(place[0] == 0)
    def _():
        pltpu.sync_copy(incoming.at[tick, :, 0, :LOW], env_low)

    @pl.when(place[0] != 0)
    def _():
        env_low[...] = stay[:, :LOW] + low[...]

    def combine(term, value, first):
        row = 0
        for ref in (out_low, out_a, out_b):
            rows = ref.shape[1]
            before = jnp.where(first, part[term, row : row + rows], ref[term])
            ref[term] = before + value[row : row + rows]
            row += rows

    row_products(place, weights, env_low, 0, plain, turned, combine)


def first_kernel(place, weights, env, states, out_low, out_a, out_b, plain, turned):
    def ready(state):
        fill(state, place, plain.shape[0], states, plain, turned)

    products(2, place, weights, [env], plain, turned, [out_low, out_a, out_b], ready)


def first_one_kernel(place, weights, env, states, plain_in, turned_in,
                     out_low, out_high, plain, turned):
    def ready(state):
        fill(state, place, plain.shape[0], states, plain, turned)

    products(1, place, weights, [env], plain, turned, [out_low, out_high], ready)


def first_zero_kernel(place, weights, env, states, plain_in, turned_in, out, plain, turned):
    def ready(state):
        fill(state, place, plain.shape[0], states, plain, turned)

    products(0, place, weights, [env], plain, turned, [out], ready)


def one_kernel(place, weights, env_low, env_high, plain, turned, out_low, out_high):
    products(1, place, weights, [env_low, env_high], plain, turned, [out_low, out_high])


def zero_kernel(place, weights, env_low, env_high, plain, turned, out):
    products(0, place, weights, [env_low, env_high], plain, turned, [out])


def final_kernel(tick, place, stay, high, far_a, far_b, low, incoming, env):
    @pl.when(place[0] == 0)
    def _():
        pltpu.sync_copy(incoming.at[tick, :, 0], env)

    @pl.when(place[0] != 0)
    def _():
        half = far_a.shape[1]
        env[:, :LOW] = stay[:, :LOW] + low[...]
        env[:, LOW : LOW + half] = stay[:, LOW : LOW + half] + high[:, :half] + far_a[...]
        env[:, LOW + half :] = stay[:, LOW + half :] + high[:, half:] + far_b[...]


def shape(*dims):
    return jax.ShapeDtypeStruct(dims, jnp.float32)


def estimate(block, terms):
    return pl.CostEstimate(
        flops=terms * 12 * block**3, bytes_accessed=16 * block * block * terms, transcendentals=0
    )


def routes(tick, columns, sites, sectors):
    relay, lift, far_one, far_two, stay = [], [], [], [], []
    for site in range(min(sites - 1, tick + TICKS)):
        for sector in range(sectors):
            here = site * sectors + sector
            after = (sector + 1) % sectors
            relay.append((here, site * sectors + after))
            lift.append((here, (site + 1) * sectors + after))
            stay.append((here, (site + 1) * sectors + sector))
            target = (sector + 2) % sectors
            back = (target // columns) * columns + (target + 1) % columns
            far_one.append((here, (site + 1) * sectors + back))
            far_two.append(((site + 1) * sectors + back, (site + 1) * sectors + target))
    return relay, lift, far_one, far_two, stay


def local(sites, held_env, incoming, states, weight_table, site_kind, sector_sizes, charge_shift):
    terms, block = held_env.shape[1], held_env.shape[3]
    sectors = sector_sizes.shape[0]
    columns = 4
    here = jnp.stack([lax.axis_index("site"), lax.axis_index("sector")]).astype(jnp.int32)
    place = jnp.concatenate([here, site_kind, charge_shift, sector_sizes])
    weights = weight_table.reshape(-1)
    count = states.shape[1]
    env = held_env[0, :, 0]
    half = (block - LOW) // 2
    parts = [shape(terms, LOW, block), shape(terms, block - LOW, block)]
    thirds = [shape(terms, LOW, block), shape(terms, half, block), shape(terms, half, block)]
    whole = shape(terms, block, block)
    split_states = [
        jax.ShapeDtypeStruct((count, 3 * block, block), jnp.bfloat16),
        jax.ShapeDtypeStruct((count, block, 3 * block), jnp.bfloat16),
    ]
    cost = estimate(block, terms)
    scalars = (place, weights)
    plain, turned = None, None

    def call(kernel, inputs, outputs, aliases={}):
        specs = [SMEM if value.ndim == 1 else VMEM for value in inputs]
        specs = [HBM if value is incoming else spec for spec, value in zip(specs, inputs)]
        return pl.pallas_call(
            kernel,
            in_specs=specs,
            out_specs=[VMEM] * len(outputs),
            out_shape=outputs,
            input_output_aliases=aliases,
            compiler_params=PARAMS,
            cost_estimate=cost,
        )(*inputs)

    for tick in range(TICKS):
        relay, lift, far_one, far_two, stay = routes(tick, columns, sites, sectors)
        if tick == 0:
            two_low, far_a, far_b, plain, turned = call(
                first_kernel, scalars + (env, states), thirds + split_states
            )
        else:
            two_low, far_a, far_b, env_low = call(
                functools.partial(late_kernel, tick - 1),
                scalars + (kept, low, part, incoming, plain, turned),
                thirds + [parts[0]],
            )
        far_a = lax.ppermute(far_a, AXES, far_one)
        two_low = lax.ppermute(two_low, AXES, relay)
        far_b = lax.ppermute(far_b, AXES, far_one)
        if tick == 0:
            one_low, one_high, plain, turned = call(
                first_one_kernel,
                scalars + (env, states, plain, turned),
                parts + split_states,
                {4: 2, 5: 3},
            )
        else:
            one_low, one_high = call(
                one_kernel, scalars + (env_low, env_high, plain, turned), parts
            )
        high = lax.ppermute(one_high, AXES, lift)
        if tick == 0:
            zero, plain, turned = call(
                first_zero_kernel,
                scalars + (env, states, plain, turned),
                [whole] + split_states,
                {4: 1, 5: 2},
            )
        else:
            (zero,) = call(zero_kernel, scalars + (env_low, env_high, plain, turned), [whole])
        kept = lax.ppermute(zero, AXES, stay)
        low = lax.ppermute(one_low + two_low, AXES, lift)
        far_a = lax.ppermute(far_a, AXES, far_two)
        far_b = lax.ppermute(far_b, AXES, far_two)
        if tick < TICKS - 1:
            env_high, part = call(
                functools.partial(early_kernel, tick),
                scalars + (kept, high, far_a, far_b, incoming, plain, turned),
                [parts[1], whole],
            )
    (env,) = call(
        functools.partial(final_kernel, TICKS - 1),
        (place, kept, high, far_a, far_b, low, incoming),
        [whole],
    )
    return env[None, :, None]


def solution(mesh):
    return jax.shard_map(
        functools.partial(local, mesh.shape["site"]),
        mesh=mesh,
        in_specs=(
            P("site", None, "sector", None, None),
            P(None, None, "sector", None, None),
            P("site", None, "sector", None, None),
            P(),
            P("site"),
            P(),
            P(),
        ),
        out_specs=P("site", None, "sector", None, None),
        check_vma=False,
    )
```

time: 305 us -> 354 us (1.16)
  waiting for transfers between devices: 139 us -> 179 us
  starting transfers between devices: 83.5 us -> 88.7 us
  Pallas kernels: 74.4 us -> 78.6 us
    ppermute x4, waiting for transfers between devices: 72.9 us -> 0.01 us  [local(): high = lax.ppermute(one_high, AXES, lift)]
    ppermute x4, waiting for transfers between devices: 0.79 us -> 58.6 us  [local(): two_low = lax.ppermute(two_low, AXES, relay)]
    ppermute x8 -> x16, waiting for transfers between devices: 12.9 us -> 58.3 us  [the longest x4 38.7 us: local(): far_b = lax.ppermute(far_b, AXES, far_one)]
    ppermute x8 -> x16, starting transfers between devices: 22.7 us -> 43.8 us  [the longest x4 11.5 us: local(): far_a = lax.ppermute(far_a, AXES, far_two)]
    ppermute x4, starting transfers between devices: 22.4 us -> 9.49 us  [local(): low = lax.ppermute(one_low + two_low, AXES, lift)]
    ppermute x4, waiting for transfers between devices: 52.5 us -> 61.8 us  [local(): low = lax.ppermute(one_low + two_low, AXES, lift)]
    ppermute x4, starting transfers between devices: 13.9 us -> 7.68 us  [local(): high = lax.ppermute(one_high, AXES, lift)]
    ppermute x4, starting transfers between devices: 12.1 us -> 16.5 us  [local(): kept = lax.ppermute(zero, AXES, stay)]
  transfers between devices with their start and end apart: 24 -> 32, of which waited for: 14 -> 16; matrix products, arithmetic and copies ran while one was open for 0% -> 0% of each run, Pallas kernels for 17% -> 10%
where the time goes in v2:
time: 354 us; the launch traced here: 353 us
  waiting for transfers between devices  179 us (51%)
  starting transfers between devices  88.7 us (25%)
  Pallas kernels  78.6 us (22%)
  local copies, waits for them, and re-layouts  4.99 us (1%)
    pallas_call x16, Pallas kernels, call(): pl.pallas_call(kernel, in_specs=specs, out_specs=[VMEM] * len(outputs), o...  78.6 us
    ppermute x4, waiting for transfers between devices, local(): low = lax.ppermute(one_low + two_low, AXES, lift)  61.8 us
    ppermute x4, waiting for transfers between devices, local(): two_low = lax.ppermute(two_low, AXES, relay)  58.6 us
    ppermute x4, waiting for transfers between devices, local(): far_b = lax.ppermute(far_b, AXES, far_one)  38.7 us
    ppermute x4, starting transfers between devices, local(): kept = lax.ppermute(zero, AXES, stay)  16.5 us
    ppermute x4, waiting for transfers between devices, local(): far_a = lax.ppermute(far_a, AXES, far_one)  13.5 us
    ppermute x4, starting transfers between devices, local(): far_a = lax.ppermute(far_a, AXES, far_two)  11.5 us
    ppermute x4, starting transfers between devices, local(): far_b = lax.ppermute(far_b, AXES, far_two)  11.3 us
  transfers between devices with their start and end apart: 32, of which 16 were waited for; matrix products, arithmetic and copies ran while one was open for 0% of the time, Pallas kernels for 10%

profile of v2, /device:TPU:1, one launch (start us, length us, event | category | flops | bytes accessed | tf_op | source)
XLA Modules:
  0.0 352.6 jit_solution(2494075088143998024)
XLA Ops:
  2.5 1.7 copy-done
  4.2 1.5 copy-done.1
  5.6 4.8 %shard_map.73 = (f32[3,128,384]{2,1,0:T(8,128)S(1)}, f32[3,128,384]{2,1,0:T(8,128)S(1)}, f32[3,128,384]{2,1,0:T(8,128)S(1)}, bf16[4,1152,384]{2,1,0:T(8,128)(2,1)S(1)}, bf16[4,384,1152]{2,1,0:T(8,128)(2,1)S(1)}) custom-call(s32[23]{0:T(128)S(1)} %concatenate.3.place, f32[576]{0:T(1024)S(1)} %reshape.3.weights, f32[3,384,384]{2,1,0:T(8,128)S(1)} %bitcast.8, ...), custom_call_target="tpu_custom_call" | custom-call | flops 2038431744 | bytes 7077888 | tf_op jit(solution)/shard_map/pallas_call | solution.py:255
  10.4 8.9 %shard_map.74 = (f32[3,128,384]{2,1,0:T(8,128)S(1)}, f32[3,256,384]{2,1,0:T(8,128)S(1)}, bf16[4,1152,384]{2,1,0:T(8,128)(2,1)S(1)}, bf16[4,384,1152]{2,1,0:T(8,128)(2,1)S(1)}) custom-call(s32[23]{0:T(128)S(1)} %concatenate.3.place, f32[576]{0:T(1024)S(1)} %reshape.3.weights, ...), custom_call_target="tpu_custom_call", output_to_operand_aliasing={{2}: (4, {}), {3}: (5, {})} | custom-call | flops 2038431744 | bytes 7077888 | tf_op jit(solution)/shard_map/pallas_call | solution.py:255
  19.4 4.8 %shard_map.75 = (f32[3,384,384]{2,1,0:T(8,128)S(1)}, bf16[4,1152,384]{2,1,0:T(8,128)(2,1)S(1)}, bf16[4,384,1152]{2,1,0:T(8,128)(2,1)S(1)}) custom-call(s32[23]{0:T(128)S(1)} %concatenate.3.place, f32[576]{0:T(1024)S(1)} %reshape.3.weights, f32[3,384,384]{2,1,0:T(8,128)S(1)} %bitcast.10, ...), custom_call_target="tpu_custom_call", output_to_operand_aliasing={{1}: (4, {}), {2}: (5, {})} | custom-call | flops 2038431744 | bytes 7077888 | tf_op jit(solution)/shard_map/pallas_call | solution.py:255
  24.2 4.6 %collective-permute-start = (f32[3,384,384]{2,1,0:T(8,128)S(1)}, f32[3,384,384]{2,1,0:T(8,128)S(1)}, u32[]{:S(2)}, u32[]{:S(2)}) collective-permute-start(f32[3,384,384]{2,1,0:T(8,128)S(1)} %get-tuple-element.45), channel_id=1, source_target_pairs={{0,16},{1,17},{2,18},{3,19},{4,20},{5,21},{6,22},{7,23},{8,24},{9,... | collective-permute-start | bytes 5308424 | tf_op jit(solution)/shard_map/ppermute | solution.py:301
  28.8 4.1 %collective-permute-start.4 = (f32[3,128,384]{2,1,0:T(8,128)S(1)}, f32[3,128,384]{2,1,0:T(8,128)S(1)}, u32[]{:S(2)}, u32[]{:S(2)}) collective-permute-start(f32[3,128,384]{2,1,0:T(8,128)S(1)} %get-tuple-element.49), channel_id=1, source_target_pairs={{0,19},{1,16},{2,21},{3,22},{4,23},{5,20},{6,25},{7,26},{8,27},{9,... | collective-permute-start | bytes 1769480 | tf_op jit(solution)/shard_map/ppermute | solution.py:277
  32.9 5.4 %collective-permute-start.6 = (f32[3,128,384]{2,1,0:T(8,128)S(1)}, f32[3,128,384]{2,1,0:T(8,128)S(1)}, u32[]{:S(2)}, u32[]{:S(2)}) collective-permute-start(f32[3,128,384]{2,1,0:T(8,128)S(1)} %get-tuple-element.50), channel_id=1, source_target_pairs={{0,19},{1,16},{2,21},{3,22},{4,23},{5,20},{6,25},{7,26},{8,27},{9,... | collective-permute-start | bytes 1769480 | tf_op jit(solution)/shard_map/ppermute | solution.py:279
  38.3 1.9 collective-permute-start.3
  40.2 1.9 collective-permute-start.1
  42.1 4.2 %collective-permute-done.4 = f32[3,128,384]{2,1,0:T(8,128)S(1)} collective-permute-done((f32[3,128,384]{2,1,0:T(8,128)S(1)}, f32[3,128,384]{2,1,0:T(8,128)S(1)}, u32[]{:S(2)}, u32[]{:S(2)}) %collective-permute-start.4) | collective-permute-done | bytes 589856 | tf_op jit(solution)/shard_map/ppermute | solution.py:277
  46.3 5.6 %collective-permute-start.5 = (f32[3,128,384]{2,1,0:T(8,128)S(1)}, f32[3,128,384]{2,1,0:T(8,128)S(1)}, u32[]{:S(2)}, u32[]{:S(2)}) collective-permute-start(f32[3,128,384]{2,1,0:T(8,128)S(1)} %collective-permute-done.4), channel_id=1, source_target_pairs={{19,18},{16,19},{21,20},{22,21},{23,22},{20,23},{25,24},{26,25},{2... | collective-permute-start | bytes 1769480 | tf_op jit(solution)/shard_map/ppermute | solution.py:303
  51.9 7.0 %collective-permute-done.6 = f32[3,128,384]{2,1,0:T(8,128)S(1)} collective-permute-done((f32[3,128,384]{2,1,0:T(8,128)S(1)}, f32[3,128,384]{2,1,0:T(8,128)S(1)}, u32[]{:S(2)}, u32[]{:S(2)}) %collective-permute-start.6) | collective-permute-done | bytes 589856 | tf_op jit(solution)/shard_map/ppermute | solution.py:279
  58.9 5.6 %collective-permute-start.7 = (f32[3,128,384]{2,1,0:T(8,128)S(1)}, f32[3,128,384]{2,1,0:T(8,128)S(1)}, u32[]{:S(2)}, u32[]{:S(2)}) collective-permute-start(f32[3,128,384]{2,1,0:T(8,128)S(1)} %collective-permute-done.6), channel_id=1, source_target_pairs={{19,18},{16,19},{21,20},{22,21},{23,22},{20,23},{25,24},{26,25},{2... | collective-permute-start | bytes 1769480 | tf_op jit(solution)/shard_map/ppermute | solution.py:304
  64.5 17.2 %collective-permute-done.1 = f32[3,128,384]{2,1,0:T(8,128)S(1)} collective-permute-done((f32[3,128,384]{2,1,0:T(8,128)S(1)}, f32[3,128,384]{2,1,0:T(8,128)S(1)}, u32[]{:S(2)}, u32[]{:S(2)}) %collective-permute-start.1) | collective-permute-done | bytes 589856 | tf_op jit(solution)/shard_map/ppermute | solution.py:278
  81.8 1.9 collective-permute-start.2
  83.8 3.7 %shard_map.76 = (f32[3,256,384]{2,1,0:T(8,128)S(1)}, f32[3,384,384]{2,1,0:T(8,128)S(1)}) custom-call(s32[23]{0:T(128)S(1)} %concatenate.3.place, f32[576]{0:T(1024)S(1)} %reshape.3.weights, f32[3,384,384]{2,1,0:T(8,128)S(1)} %collective-permute-done.stay, f32[3,256,384]{2,1,0:T(8,128)S(1)} %collective-permute-done.3.high, ...), custom_call_target="tpu_custom_call" | custom-call | flops 2038431744 | bytes 7077888 | tf_op jit(solution)/shard_map/pallas_call | solution.py:255
  87.5 14.3 %collective-permute-done.2.low = f32[3,128,384]{2,1,0:T(8,128)S(1)} collective-permute-done((f32[3,128,384]{2,1,0:T(8,128)S(1)}, f32[3,128,384]{2,1,0:T(8,128)S(1)}, u32[]{:S(2)}, u32[]{:S(2)}) %collective-permute-start.2) | collective-permute-done | bytes 589856 | tf_op jit(solution)/shard_map/ppermute | solution.py:302
  101.8 2.7 shard_map.77
  104.5 4.5 %shard_map.78 = f32[3,384,384]{2,1,0:T(8,128)S(1)} custom-call(s32[23]{0:T(128)S(1)} %concatenate.3.place, f32[576]{0:T(1024)S(1)} %reshape.3.weights, f32[3,128,384]{2,1,0:T(8,128)S(1)} %get-tuple-element.54.env_low, f32[3,256,384]{2,1,0:T(8,128)S(1)} %get-tuple-element.55.env_high, bf16[4,1152,384]{2,1,0:T(8,128)(2,1)S(1)} %get-tuple-element.51.plain, ...), custom_call_target="tpu_custom_call" | custom-call | flops 2038431744 | bytes 7077888 | tf_op jit(solution)/shard_map/pallas_call | solution.py:255
  109.1 4.5 %collective-permute-start.8 = (f32[3,384,384]{2,1,0:T(8,128)S(1)}, f32[3,384,384]{2,1,0:T(8,128)S(1)}, u32[]{:S(2)}, u32[]{:S(2)}) collective-permute-start(f32[3,384,384]{2,1,0:T(8,128)S(1)} %shard_map.78), channel_id=1, source_target_pairs={{0,16},{1,17},{2,18},{3,19},{4,20},{5,21},{6,22},{7,23},{8,24},{9,... | collective-permute-start | bytes 5308424 | tf_op jit(solution)/shard_map/ppermute | solution.py:301
  113.6 1.9 collective-permute-start.12
  115.5 8.4 %shard_map.79 = (f32[3,128,384]{2,1,0:T(8,128)S(1)}, f32[3,256,384]{2,1,0:T(8,128)S(1)}) custom-call(s32[23]{0:T(128)S(1)} %concatenate.3.place, f32[576]{0:T(1024)S(1)} %reshape.3.weights, f32[3,128,384]{2,1,0:T(8,128)S(1)} %get-tuple-element.54.env_low, f32[3,256,384]{2,1,0:T(8,128)S(1)} %get-tuple-element.55.env_high, ...), custom_call_target="tpu_custom_call" | custom-call | flops 2038431744 | bytes 7077888 | tf_op jit(solution)/shard_map/pallas_call | solution.py:255
  123.9 1.9 collective-permute-start.14
  125.9 1.9 collective-permute-start.11
  127.8 3.1 collective-permute-start.9
  131.1 2.1 collective-permute-start.13
  133.2 10.5 %collective-permute-done.14 = f32[3,128,384]{2,1,0:T(8,128)S(1)} collective-permute-done((f32[3,128,384]{2,1,0:T(8,128)S(1)}, f32[3,128,384]{2,1,0:T(8,128)S(1)}, u32[]{:S(2)}, u32[]{:S(2)}) %collective-permute-start.14) | collective-permute-done | bytes 589856 | tf_op jit(solution)/shard_map/ppermute | solution.py:279
  143.7 1.9 collective-permute-start.15
  145.7 24.9 %collective-permute-done.9 = f32[3,128,384]{2,1,0:T(8,128)S(1)} collective-permute-done((f32[3,128,384]{2,1,0:T(8,128)S(1)}, f32[3,128,384]{2,1,0:T(8,128)S(1)}, u32[]{:S(2)}, u32[]{:S(2)}) %collective-permute-start.9) | collective-permute-done | bytes 589856 | tf_op jit(solution)/shard_map/ppermute | solution.py:278
  170.6 1.9 collective-permute-start.10
  172.6 3.7 %shard_map.80 = (f32[3,256,384]{2,1,0:T(8,128)S(1)}, f32[3,384,384]{2,1,0:T(8,128)S(1)}) custom-call(s32[23]{0:T(128)S(1)} %concatenate.3.place, f32[576]{0:T(1024)S(1)} %reshape.3.weights, f32[3,384,384]{2,1,0:T(8,128)S(1)} %collective-permute-done.8.stay, f32[3,256,384]{2,1,0:T(8,128)S(1)} %collective-permute-done.11.high, ...), custom_call_target="tpu_custom_call" | custom-call | flops 2038431744 | bytes 7077888 | tf_op jit(solution)/shard_map/pallas_call | solution.py:255
  176.3 14.1 %collective-permute-done.10.low = f32[3,128,384]{2,1,0:T(8,128)S(1)} collective-permute-done((f32[3,128,384]{2,1,0:T(8,128)S(1)}, f32[3,128,384]{2,1,0:T(8,128)S(1)}, u32[]{:S(2)}, u32[]{:S(2)}) %collective-permute-start.10) | collective-permute-done | bytes 589856 | tf_op jit(solution)/shard_map/ppermute | solution.py:302
  190.4 2.9 shard_map.81
  193.3 4.5 %shard_map.82 = f32[3,384,384]{2,1,0:T(8,128)S(1)} custom-call(s32[23]{0:T(128)S(1)} %concatenate.3.place, f32[576]{0:T(1024)S(1)} %reshape.3.weights, f32[3,128,384]{2,1,0:T(8,128)S(1)} %get-tuple-element.62.env_low, f32[3,256,384]{2,1,0:T(8,128)S(1)} %get-tuple-element.63.env_high, bf16[4,1152,384]{2,1,0:T(8,128)(2,1)S(1)} %get-tuple-element.51.plain, ...), custom_call_target="tpu_custom_call" | custom-call | flops 2038431744 | bytes 7077888 | tf_op jit(solution)/shard_map/pallas_call | solution.py:255
  197.8 4.8 %collective-permute-start.16 = (f32[3,384,384]{2,1,0:T(8,128)S(1)}, f32[3,384,384]{2,1,0:T(8,128)S(1)}, u32[]{:S(2)}, u32[]{:S(2)}) collective-permute-start(f32[3,384,384]{2,1,0:T(8,128)S(1)} %shard_map.82), channel_id=1, source_target_pairs={{0,16},{1,17},{2,18},{3,19},{4,20},{5,21},{6,22},{7,23},{8,24},{9,... | collective-permute-start | bytes 5308424 | tf_op jit(solution)/shard_map/ppermute | solution.py:301
  202.6 8.4 %shard_map.83 = (f32[3,128,384]{2,1,0:T(8,128)S(1)}, f32[3,256,384]{2,1,0:T(8,128)S(1)}) custom-call(s32[23]{0:T(128)S(1)} %concatenate.3.place, f32[576]{0:T(1024)S(1)} %reshape.3.weights, f32[3,128,384]{2,1,0:T(8,128)S(1)} %get-tuple-element.62.env_low, f32[3,256,384]{2,1,0:T(8,128)S(1)} %get-tuple-element.63.env_high, ...), custom_call_target="tpu_custom_call" | custom-call | flops 2038431744 | bytes 7077888 | tf_op jit(solution)/shard_map/pallas_call | solution.py:255
  211.0 1.9 collective-permute-start.20
  213.0 1.9 collective-permute-start.22
  214.9 1.9 collective-permute-start.19
  216.8 3.1 collective-permute-start.17
  219.9 8.6 %collective-permute-done.20 = f32[3,128,384]{2,1,0:T(8,128)S(1)} collective-permute-done((f32[3,128,384]{2,1,0:T(8,128)S(1)}, f32[3,128,384]{2,1,0:T(8,128)S(1)}, u32[]{:S(2)}, u32[]{:S(2)}) %collective-permute-start.20) | collective-permute-done | bytes 589856 | tf_op jit(solution)/shard_map/ppermute | solution.py:277
  228.6 1.9 collective-permute-start.21
  230.5 10.7 %collective-permute-done.22 = f32[3,128,384]{2,1,0:T(8,128)S(1)} collective-permute-done((f32[3,128,384]{2,1,0:T(8,128)S(1)}, f32[3,128,384]{2,1,0:T(8,128)S(1)}, u32[]{:S(2)}, u32[]{:S(2)}) %collective-permute-start.22) | collective-permute-done | bytes 589856 | tf_op jit(solution)/shard_map/ppermute | solution.py:279
  241.2 1.9 collective-permute-start.23
  243.1 16.5 %collective-permute-done.17 = f32[3,128,384]{2,1,0:T(8,128)S(1)} collective-permute-done((f32[3,128,384]{2,1,0:T(8,128)S(1)}, f32[3,128,384]{2,1,0:T(8,128)S(1)}, u32[]{:S(2)}, u32[]{:S(2)}) %collective-permute-start.17) | collective-permute-done | bytes 589856 | tf_op jit(solution)/shard_map/ppermute | solution.py:278
  259.7 1.9 collective-permute-start.18
  261.6 3.7 %shard_map.84 = (f32[3,256,384]{2,1,0:T(8,128)S(1)}, f32[3,384,384]{2,1,0:T(8,128)S(1)}) custom-call(s32[23]{0:T(128)S(1)} %concatenate.3.place, f32[576]{0:T(1024)S(1)} %reshape.3.weights, f32[3,384,384]{2,1,0:T(8,128)S(1)} %collective-permute-done.16.stay, f32[3,256,384]{2,1,0:T(8,128)S(1)} %collective-permute-done.19.high, ...), custom_call_target="tpu_custom_call" | custom-call | flops 2038431744 | bytes 7077888 | tf_op jit(solution)/shard_map/pallas_call | solution.py:255
  265.3 14.2 %collective-permute-done.18.low = f32[3,128,384]{2,1,0:T(8,128)S(1)} collective-permute-done((f32[3,128,384]{2,1,0:T(8,128)S(1)}, f32[3,128,384]{2,1,0:T(8,128)S(1)}, u32[]{:S(2)}, u32[]{:S(2)}) %collective-permute-start.18) | collective-permute-done | bytes 589856 | tf_op jit(solution)/shard_map/ppermute | solution.py:302
  279.5 2.7 shard_map.85
  282.2 4.5 %shard_map.86 = f32[3,384,384]{2,1,0:T(8,128)S(1)} custom-call(s32[23]{0:T(128)S(1)} %concatenate.3.place, f32[576]{0:T(1024)S(1)} %reshape.3.weights, f32[3,128,384]{2,1,0:T(8,128)S(1)} %get-tuple-element.70.env_low, f32[3,256,384]{2,1,0:T(8,128)S(1)} %get-tuple-element.71.env_high, bf16[4,1152,384]{2,1,0:T(8,128)(2,1)S(1)} %get-tuple-element.51.plain, ...), custom_call_target="tpu_custom_call" | custom-call | flops 2038431744 | bytes 7077888 | tf_op jit(solution)/shard_map/pallas_call | solution.py:255
  286.7 2.6 collective-permute-start.24
  289.4 1.9 collective-permute-start.26
  291.3 1.9 collective-permute-start.28
  293.2 3.1 collective-permute-start.30
  296.3 8.4 %shard_map.87 = (f32[3,128,384]{2,1,0:T(8,128)S(1)}, f32[3,256,384]{2,1,0:T(8,128)S(1)}) custom-call(s32[23]{0:T(128)S(1)} %concatenate.3.place, f32[576]{0:T(1024)S(1)} %reshape.3.weights, f32[3,128,384]{2,1,0:T(8,128)S(1)} %get-tuple-element.70.env_low, f32[3,256,384]{2,1,0:T(8,128)S(1)} %get-tuple-element.71.env_high, ...), custom_call_target="tpu_custom_call" | custom-call | flops 2038431744 | bytes 7077888 | tf_op jit(solution)/shard_map/pallas_call | solution.py:255
  304.8 1.9 collective-permute-start.25
  307.2 1.9 collective-permute-start.27
  309.1 10.4 %collective-permute-done.28 = f32[3,128,384]{2,1,0:T(8,128)S(1)} collective-permute-done((f32[3,128,384]{2,1,0:T(8,128)S(1)}, f32[3,128,384]{2,1,0:T(8,128)S(1)}, u32[]{:S(2)}, u32[]{:S(2)}) %collective-permute-start.28) | collective-permute-done | bytes 589856 | tf_op jit(solution)/shard_map/ppermute | solution.py:279
  319.5 1.9 collective-permute-start.29
  321.5 3.7 %collective-permute-start.31 = (f32[3,128,384]{2,1,0:T(8,128)S(1)}, f32[3,128,384]{2,1,0:T(8,128)S(1)}, u32[]{:S(2)}, u32[]{:S(2)}) collective-permute-start(f32[3,128,384]{2,1,0:T(8,128)S(1)} %add.15), channel_id=1, source_target_pairs={{0,17},{1,18},{2,19},{3,20},{4,21},{5,22},{6,23},{7,24},{8,25},{9,... | collective-permute-start | bytes 1769480 | tf_op jit(solution)/shard_map/ppermute | solution.py:302
  325.3 6.0 %collective-permute-done.29.far_b = f32[3,128,384]{2,1,0:T(8,128)S(1)} collective-permute-done((f32[3,128,384]{2,1,0:T(8,128)S(1)}, f32[3,128,384]{2,1,0:T(8,128)S(1)}, u32[]{:S(2)}, u32[]{:S(2)}) %collective-permute-start.29) | collective-permute-done | bytes 589856 | tf_op jit(solution)/shard_map/ppermute | solution.py:304
  331.3 19.3 %collective-permute-done.31.low = f32[3,128,384]{2,1,0:T(8,128)S(1)} collective-permute-done((f32[3,128,384]{2,1,0:T(8,128)S(1)}, f32[3,128,384]{2,1,0:T(8,128)S(1)}, u32[]{:S(2)}, u32[]{:S(2)}) %collective-permute-start.31) | collective-permute-done | bytes 589856 | tf_op jit(solution)/shard_map/ppermute | solution.py:302
  350.6 2.0 shard_map.88
  (32 shorter events, 2.9 us)
Async XLA Ops:
  2.5 1.7 copy-start
  4.2 1.5 copy-start.1
  19.4 64.4 %slice-start = ((s8[7077888]{0:T(1024)(128)(4,1)}), s8[4194304]{0:T(1024)(128)(4,1)S(1)}, s32[]{:S(2)}) async-start(s8[7077888]{0:T(1024)(128)(4,1)} %bitcast.6), calls=%async_computation | async-start | bytes 8388608
  19.4 64.4 %slice-start.1 = ((s8[7077888]{0:T(1024)(128)(4,1)}), s8[2883584]{0:T(1024)(128)(4,1)S(1)}, s32[]{:S(2)}) async-start(s8[7077888]{0:T(1024)(128)(4,1)} %bitcast.6), calls=%async_computation.1 | async-start | bytes 5767168
  24.2 59.6 %collective-permute-start = (f32[3,384,384]{2,1,0:T(8,128)S(1)}, f32[3,384,384]{2,1,0:T(8,128)S(1)}, u32[]{:S(2)}, u32[]{:S(2)}) collective-permute-start(f32[3,384,384]{2,1,0:T(8,128)S(1)} %get-tuple-element.45), channel_id=1, source_target_pairs={{0,16},{1,17},{2,18},{3,19},{4,20},{5,21},{6,22},{7,23},{8,24},{9,... | collective-permute-start | bytes 5308424 | tf_op jit(solution)/shard_map/ppermute | solution.py:301
  28.8 17.5 %collective-permute-start.4 = (f32[3,128,384]{2,1,0:T(8,128)S(1)}, f32[3,128,384]{2,1,0:T(8,128)S(1)}, u32[]{:S(2)}, u32[]{:S(2)}) collective-permute-start(f32[3,128,384]{2,1,0:T(8,128)S(1)} %get-tuple-element.49), channel_id=1, source_target_pairs={{0,19},{1,16},{2,21},{3,22},{4,23},{5,20},{6,25},{7,26},{8,27},{9,... | collective-permute-start | bytes 1769480 | tf_op jit(solution)/shard_map/ppermute | solution.py:277
  32.9 26.0 %collective-permute-start.6 = (f32[3,128,384]{2,1,0:T(8,128)S(1)}, f32[3,128,384]{2,1,0:T(8,128)S(1)}, u32[]{:S(2)}, u32[]{:S(2)}) collective-permute-start(f32[3,128,384]{2,1,0:T(8,128)S(1)} %get-tuple-element.50), channel_id=1, source_target_pairs={{0,19},{1,16},{2,21},{3,22},{4,23},{5,20},{6,25},{7,26},{8,27},{9,... | collective-permute-start | bytes 1769480 | tf_op jit(solution)/shard_map/ppermute | solution.py:279
  38.3 45.5 %collective-permute-start.3 = (f32[3,256,384]{2,1,0:T(8,128)S(1)}, f32[3,256,384]{2,1,0:T(8,128)S(1)}, u32[]{:S(2)}, u32[]{:S(2)}) collective-permute-start(f32[3,256,384]{2,1,0:T(8,128)S(1)} %get-tuple-element.48), channel_id=1, source_target_pairs={{0,17},{1,18},{2,19},{3,20},{4,21},{5,22},{6,23},{7,24},{8,25},{9,... | collective-permute-start | bytes 3538952 | tf_op jit(solution)/shard_map/ppermute | solution.py:291
  40.2 41.5 %collective-permute-start.1 = (f32[3,128,384]{2,1,0:T(8,128)S(1)}, f32[3,128,384]{2,1,0:T(8,128)S(1)}, u32[]{:S(2)}, u32[]{:S(2)}) collective-permute-start(f32[3,128,384]{2,1,0:T(8,128)S(1)} %get-tuple-element.47), channel_id=1, source_target_pairs={{0,1},{1,2},{2,3},{3,4},{4,5},{5,6},{6,7},{7,8},{8,9},{9,10},{10,1... | collective-permute-start | bytes 1769480 | tf_op jit(solution)/shard_map/ppermute | solution.py:278
  46.3 37.4 %collective-permute-start.5 = (f32[3,128,384]{2,1,0:T(8,128)S(1)}, f32[3,128,384]{2,1,0:T(8,128)S(1)}, u32[]{:S(2)}, u32[]{:S(2)}) collective-permute-start(f32[3,128,384]{2,1,0:T(8,128)S(1)} %collective-permute-done.4), channel_id=1, source_target_pairs={{19,18},{16,19},{21,20},{22,21},{23,22},{20,23},{25,24},{26,25},{2... | collective-permute-start | bytes 1769480 | tf_op jit(solution)/shard_map/ppermute | solution.py:303
  58.9 24.8 %collective-permute-start.7 = (f32[3,128,384]{2,1,0:T(8,128)S(1)}, f32[3,128,384]{2,1,0:T(8,128)S(1)}, u32[]{:S(2)}, u32[]{:S(2)}) collective-permute-start(f32[3,128,384]{2,1,0:T(8,128)S(1)} %collective-permute-done.6), channel_id=1, source_target_pairs={{19,18},{16,19},{21,20},{22,21},{23,22},{20,23},{25,24},{26,25},{2... | collective-permute-start | bytes 1769480 | tf_op jit(solution)/shard_map/ppermute | solution.py:304
  81.8 20.0 %collective-permute-start.2 = (f32[3,128,384]{2,1,0:T(8,128)S(1)}, f32[3,128,384]{2,1,0:T(8,128)S(1)}, u32[]{:S(2)}, u32[]{:S(2)}) collective-permute-start(f32[3,128,384]{2,1,0:T(8,128)S(1)} %add.12), channel_id=1, source_target_pairs={{0,17},{1,18},{2,19},{3,20},{4,21},{5,22},{6,23},{7,24},{8,25},{9,... | collective-permute-start | bytes 1769480 | tf_op jit(solution)/shard_map/ppermute | solution.py:302
  109.1 63.5 %collective-permute-start.8 = (f32[3,384,384]{2,1,0:T(8,128)S(1)}, f32[3,384,384]{2,1,0:T(8,128)S(1)}, u32[]{:S(2)}, u32[]{:S(2)}) collective-permute-start(f32[3,384,384]{2,1,0:T(8,128)S(1)} %shard_map.78), channel_id=1, source_target_pairs={{0,16},{1,17},{2,18},{3,19},{4,20},{5,21},{6,22},{7,23},{8,24},{9,... | collective-permute-start | bytes 5308424 | tf_op jit(solution)/shard_map/ppermute | solution.py:301
  113.6 17.5 %collective-permute-start.12 = (f32[3,128,384]{2,1,0:T(8,128)S(1)}, f32[3,128,384]{2,1,0:T(8,128)S(1)}, u32[]{:S(2)}, u32[]{:S(2)}) collective-permute-start(f32[3,128,384]{2,1,0:T(8,128)S(1)} %get-tuple-element.59), channel_id=1, source_target_pairs={{0,19},{1,16},{2,21},{3,22},{4,23},{5,20},{6,25},{7,26},{8,27},{9,... | collective-permute-start | bytes 1769480 | tf_op jit(solution)/shard_map/ppermute | solution.py:277
  123.9 19.8 %collective-permute-start.14 = (f32[3,128,384]{2,1,0:T(8,128)S(1)}, f32[3,128,384]{2,1,0:T(8,128)S(1)}, u32[]{:S(2)}, u32[]{:S(2)}) collective-permute-start(f32[3,128,384]{2,1,0:T(8,128)S(1)} %get-tuple-element.60), channel_id=1, source_target_pairs={{0,19},{1,16},{2,21},{3,22},{4,23},{5,20},{6,25},{7,26},{8,27},{9,... | collective-permute-start | bytes 1769480 | tf_op jit(solution)/shard_map/ppermute | solution.py:279
  125.9 46.7 %collective-permute-start.11 = (f32[3,256,384]{2,1,0:T(8,128)S(1)}, f32[3,256,384]{2,1,0:T(8,128)S(1)}, u32[]{:S(2)}, u32[]{:S(2)}) collective-permute-start(f32[3,256,384]{2,1,0:T(8,128)S(1)} %get-tuple-element.58), channel_id=1, source_target_pairs={{0,17},{1,18},{2,19},{3,20},{4,21},{5,22},{6,23},{7,24},{8,25},{9,... | collective-permute-start | bytes 3538952 | tf_op jit(solution)/shard_map/ppermute | solution.py:291
  127.8 42.8 %collective-permute-start.9 = (f32[3,128,384]{2,1,0:T(8,128)S(1)}, f32[3,128,384]{2,1,0:T(8,128)S(1)}, u32[]{:S(2)}, u32[]{:S(2)}) collective-permute-start(f32[3,128,384]{2,1,0:T(8,128)S(1)} %get-tuple-element.57), channel_id=1, source_target_pairs={{0,1},{1,2},{2,3},{3,4},{4,5},{5,6},{6,7},{7,8},{8,9},{9,10},{10,1... | collective-permute-start | bytes 1769480 | tf_op jit(solution)/shard_map/ppermute | solution.py:278
  131.1 41.5 %collective-permute-start.13 = (f32[3,128,384]{2,1,0:T(8,128)S(1)}, f32[3,128,384]{2,1,0:T(8,128)S(1)}, u32[]{:S(2)}, u32[]{:S(2)}) collective-permute-start(f32[3,128,384]{2,1,0:T(8,128)S(1)} %collective-permute-done.12), channel_id=1, source_target_pairs={{19,18},{16,19},{21,20},{22,21},{23,22},{20,23},{25,24},{26,25},{2... | collective-permute-start | bytes 1769480 | tf_op jit(solution)/shard_map/ppermute | solution.py:303
  143.7 28.8 %collective-permute-start.15 = (f32[3,128,384]{2,1,0:T(8,128)S(1)}, f32[3,128,384]{2,1,0:T(8,128)S(1)}, u32[]{:S(2)}, u32[]{:S(2)}) collective-permute-start(f32[3,128,384]{2,1,0:T(8,128)S(1)} %collective-permute-done.14), channel_id=1, source_target_pairs={{19,18},{16,19},{21,20},{22,21},{23,22},{20,23},{25,24},{26,25},{2... | collective-permute-start | bytes 1769480 | tf_op jit(solution)/shard_map/ppermute | solution.py:304
  170.6 19.7 %collective-permute-start.10 = (f32[3,128,384]{2,1,0:T(8,128)S(1)}, f32[3,128,384]{2,1,0:T(8,128)S(1)}, u32[]{:S(2)}, u32[]{:S(2)}) collective-permute-start(f32[3,128,384]{2,1,0:T(8,128)S(1)} %add.13), channel_id=1, source_target_pairs={{0,17},{1,18},{2,19},{3,20},{4,21},{5,22},{6,23},{7,24},{8,25},{9,... | collective-permute-start | bytes 1769480 | tf_op jit(solution)/shard_map/ppermute | solution.py:302
  197.8 63.8 %collective-permute-start.16 = (f32[3,384,384]{2,1,0:T(8,128)S(1)}, f32[3,384,384]{2,1,0:T(8,128)S(1)}, u32[]{:S(2)}, u32[]{:S(2)}) collective-permute-start(f32[3,384,384]{2,1,0:T(8,128)S(1)} %shard_map.82), channel_id=1, source_target_pairs={{0,16},{1,17},{2,18},{3,19},{4,20},{5,21},{6,22},{7,23},{8,24},{9,... | collective-permute-start | bytes 5308424 | tf_op jit(solution)/shard_map/ppermute | solution.py:301
  211.0 17.5 %collective-permute-start.20 = (f32[3,128,384]{2,1,0:T(8,128)S(1)}, f32[3,128,384]{2,1,0:T(8,128)S(1)}, u32[]{:S(2)}, u32[]{:S(2)}) collective-permute-start(f32[3,128,384]{2,1,0:T(8,128)S(1)} %get-tuple-element.67), channel_id=1, source_target_pairs={{0,19},{1,16},{2,21},{3,22},{4,23},{5,20},{6,25},{7,26},{8,27},{9,... | collective-permute-start | bytes 1769480 | tf_op jit(solution)/shard_map/ppermute | solution.py:277
  213.0 28.2 %collective-permute-start.22 = (f32[3,128,384]{2,1,0:T(8,128)S(1)}, f32[3,128,384]{2,1,0:T(8,128)S(1)}, u32[]{:S(2)}, u32[]{:S(2)}) collective-permute-start(f32[3,128,384]{2,1,0:T(8,128)S(1)} %get-tuple-element.68), channel_id=1, source_target_pairs={{0,19},{1,16},{2,21},{3,22},{4,23},{5,20},{6,25},{7,26},{8,27},{9,... | collective-permute-start | bytes 1769480 | tf_op jit(solution)/shard_map/ppermute | solution.py:279
  214.9 46.7 %collective-permute-start.19 = (f32[3,256,384]{2,1,0:T(8,128)S(1)}, f32[3,256,384]{2,1,0:T(8,128)S(1)}, u32[]{:S(2)}, u32[]{:S(2)}) collective-permute-start(f32[3,256,384]{2,1,0:T(8,128)S(1)} %get-tuple-element.66), channel_id=1, source_target_pairs={{0,17},{1,18},{2,19},{3,20},{4,21},{5,22},{6,23},{7,24},{8,25},{9,... | collective-permute-start | bytes 3538952 | tf_op jit(solution)/shard_map/ppermute | solution.py:291
  216.8 42.8 %collective-permute-start.17 = (f32[3,128,384]{2,1,0:T(8,128)S(1)}, f32[3,128,384]{2,1,0:T(8,128)S(1)}, u32[]{:S(2)}, u32[]{:S(2)}) collective-permute-start(f32[3,128,384]{2,1,0:T(8,128)S(1)} %get-tuple-element.65), channel_id=1, source_target_pairs={{0,1},{1,2},{2,3},{3,4},{4,5},{5,6},{6,7},{7,8},{8,9},{9,10},{10,1... | collective-permute-start | bytes 1769480 | tf_op jit(solution)/shard_map/ppermute | solution.py:278
  228.6 33.1 %collective-permute-start.21 = (f32[3,128,384]{2,1,0:T(8,128)S(1)}, f32[3,128,384]{2,1,0:T(8,128)S(1)}, u32[]{:S(2)}, u32[]{:S(2)}) collective-permute-start(f32[3,128,384]{2,1,0:T(8,128)S(1)} %collective-permute-done.20), channel_id=1, source_target_pairs={{19,18},{16,19},{21,20},{22,21},{23,22},{20,23},{25,24},{26,25},{2... | collective-permute-start | bytes 1769480 | tf_op jit(solution)/shard_map/ppermute | solution.py:303
  241.2 20.4 %collective-permute-start.23 = (f32[3,128,384]{2,1,0:T(8,128)S(1)}, f32[3,128,384]{2,1,0:T(8,128)S(1)}, u32[]{:S(2)}, u32[]{:S(2)}) collective-permute-start(f32[3,128,384]{2,1,0:T(8,128)S(1)} %collective-permute-done.22), channel_id=1, source_target_pairs={{19,18},{16,19},{21,20},{22,21},{23,22},{20,23},{25,24},{26,25},{2... | collective-permute-start | bytes 1769480 | tf_op jit(solution)/shard_map/ppermute | solution.py:304
  259.7 19.8 %collective-permute-start.18 = (f32[3,128,384]{2,1,0:T(8,128)S(1)}, f32[3,128,384]{2,1,0:T(8,128)S(1)}, u32[]{:S(2)}, u32[]{:S(2)}) collective-permute-start(f32[3,128,384]{2,1,0:T(8,128)S(1)} %add.14), channel_id=1, source_target_pairs={{0,17},{1,18},{2,19},{3,20},{4,21},{5,22},{6,23},{7,24},{8,25},{9,... | collective-permute-start | bytes 1769480 | tf_op jit(solution)/shard_map/ppermute | solution.py:302
  286.7 63.9 %collective-permute-start.24 = (f32[3,384,384]{2,1,0:T(8,128)S(1)}, f32[3,384,384]{2,1,0:T(8,128)S(1)}, u32[]{:S(2)}, u32[]{:S(2)}) collective-permute-start(f32[3,384,384]{2,1,0:T(8,128)S(1)} %shard_map.86), channel_id=1, source_target_pairs={{0,16},{1,17},{2,18},{3,19},{4,20},{5,21},{6,22},{7,23},{8,24},{9,... | collective-permute-start | bytes 5308424 | tf_op jit(solution)/shard_map/ppermute | solution.py:301
  289.4 17.8 %collective-permute-start.26 = (f32[3,128,384]{2,1,0:T(8,128)S(1)}, f32[3,128,384]{2,1,0:T(8,128)S(1)}, u32[]{:S(2)}, u32[]{:S(2)}) collective-permute-start(f32[3,128,384]{2,1,0:T(8,128)S(1)} %get-tuple-element.73), channel_id=1, source_target_pairs={{0,19},{1,16},{2,21},{3,22},{4,23},{5,20},{6,25},{7,26},{8,27},{9,... | collective-permute-start | bytes 1769480 | tf_op jit(solution)/shard_map/ppermute | solution.py:277
  291.3 28.2 %collective-permute-start.28 = (f32[3,128,384]{2,1,0:T(8,128)S(1)}, f32[3,128,384]{2,1,0:T(8,128)S(1)}, u32[]{:S(2)}, u32[]{:S(2)}) collective-permute-start(f32[3,128,384]{2,1,0:T(8,128)S(1)} %get-tuple-element.74), channel_id=1, source_target_pairs={{0,19},{1,16},{2,21},{3,22},{4,23},{5,20},{6,25},{7,26},{8,27},{9,... | collective-permute-start | bytes 1769480 | tf_op jit(solution)/shard_map/ppermute | solution.py:279
  293.2 28.2 %collective-permute-start.30 = (f32[3,128,384]{2,1,0:T(8,128)S(1)}, f32[3,128,384]{2,1,0:T(8,128)S(1)}, u32[]{:S(2)}, u32[]{:S(2)}) collective-permute-start(f32[3,128,384]{2,1,0:T(8,128)S(1)} %get-tuple-element.76), channel_id=1, source_target_pairs={{0,1},{1,2},{2,3},{3,4},{4,5},{5,6},{6,7},{7,8},{8,9},{9,10},{10,1... | collective-permute-start | bytes 1769480 | tf_op jit(solution)/shard_map/ppermute | solution.py:278
  304.8 45.8 %collective-permute-start.25 = (f32[3,256,384]{2,1,0:T(8,128)S(1)}, f32[3,256,384]{2,1,0:T(8,128)S(1)}, u32[]{:S(2)}, u32[]{:S(2)}) collective-permute-start(f32[3,256,384]{2,1,0:T(8,128)S(1)} %get-tuple-element.72), channel_id=1, source_target_pairs={{0,17},{1,18},{2,19},{3,20},{4,21},{5,22},{6,23},{7,24},{8,25},{9,... | collective-permute-start | bytes 3538952 | tf_op jit(solution)/shard_map/ppermute | solution.py:291
  307.2 18.1 %collective-permute-start.27 = (f32[3,128,384]{2,1,0:T(8,128)S(1)}, f32[3,128,384]{2,1,0:T(8,128)S(1)}, u32[]{:S(2)}, u32[]{:S(2)}) collective-permute-start(f32[3,128,384]{2,1,0:T(8,128)S(1)} %collective-permute-done.26), channel_id=1, source_target_pairs={{19,18},{16,19},{21,20},{22,21},{23,22},{20,23},{25,24},{26,25},{2... | collective-permute-start | bytes 1769480 | tf_op jit(solution)/shard_map/ppermute | solution.py:303
  319.5 11.8 %collective-permute-start.29 = (f32[3,128,384]{2,1,0:T(8,128)S(1)}, f32[3,128,384]{2,1,0:T(8,128)S(1)}, u32[]{:S(2)}, u32[]{:S(2)}) collective-permute-start(f32[3,128,384]{2,1,0:T(8,128)S(1)} %collective-permute-done.28), channel_id=1, source_target_pairs={{19,18},{16,19},{21,20},{22,21},{23,22},{20,23},{25,24},{26,25},{2... | collective-permute-start | bytes 1769480 | tf_op jit(solution)/shard_map/ppermute | solution.py:304
  321.5 29.1 %collective-permute-start.31 = (f32[3,128,384]{2,1,0:T(8,128)S(1)}, f32[3,128,384]{2,1,0:T(8,128)S(1)}, u32[]{:S(2)}, u32[]{:S(2)}) collective-permute-start(f32[3,128,384]{2,1,0:T(8,128)S(1)} %add.15), channel_id=1, source_target_pairs={{0,17},{1,18},{2,19},{3,20},{4,21},{5,22},{6,23},{7,24},{8,25},{9,... | collective-permute-start | bytes 1769480 | tf_op jit(solution)/shard_map/ppermute | solution.py:302

commit v3 on v2

--- a/solution.py
+++ b/solution.py
@@ -75,7 +75,40 @@
     return pieces[0] if len(pieces) == 1 else jnp.concatenate(pieces, axis=0)
 
 
-def products(offset, place, weights, env_refs, plain_ref, turned_ref, stores, ready=None):
+def products(offset, place, weights, env_refs, plain_ref, turned_ref, stores, scratch, ready=None):
+    count = plain_ref.shape[0]
+    terms, block = env_refs[0].shape[0], plain_ref.shape[2]
+    wide, tall = scratch
+
+    def body(state, first):
+        if ready is not None:
+            ready(state)
+        for term in range(terms):
+            columns = slice(term * block, (term + 1) * block)
+            high, low = halves(mix(place, weights, count, state, term, env_refs))
+            wide[0:block, columns] = high
+            wide[block : 2 * block, columns] = low
+            wide[2 * block :, columns] = high
+        right = dot(turned_ref[state], wide[...])
+        for term in range(terms):
+            lines = slice(term * block, (term + 1) * block)
+            high, low = halves(right[:, lines])
+            tall[lines, 0:block] = high
+            tall[lines, block : 2 * block] = high
+            tall[lines, 2 * block :] = low
+        triple = dot(tall[...], plain_ref[state])
+        for term in range(terms):
+            row = term * block
+            for ref in stores:
+                rows = ref.shape[1]
+                before = jnp.where(first, jnp.float32(0.0), ref[term])
+                ref[term] = before + triple[row : row + rows]
+                row += rows
+
+    each_state(offset, place, count, body)
+
+
+def looped(offset, place, weights, env_refs, plain_ref, turned_ref, stores, ready=None):
     count = plain_ref.shape[0]
 
     def body(state, first):
@@ -121,7 +154,7 @@
 
 
 def early_kernel(tick, place, weights, stay, high, far_a, far_b, incoming, plain, turned,
-                 env_high, part):
+                 env_high, part, *scratch):
     @pl.when(place[0] == 0)
     def _():
         pltpu.sync_copy(incoming.at[tick, :, 0, LOW:], env_high)
@@ -129,8 +162,8 @@
     @pl.when(place[0] != 0)
     def _():
         half = far_a.shape[1]
-        env_high[:, :half] = stay[:, LOW : LOW + half] + high[:, :half] + far_a[...]
-        env_high[:, half:] = stay[:, LOW + half :] + high[:, half:] + far_b[...]
+        env_high[:, :half] = stay[:, :half] + high[:, :half] + far_a[...]
+        env_high[:, half:] = stay[:, half:] + high[:, half:] + far_b[...]
 
     def combine(term, value, first):
         part[term] = jnp.where(first, jnp.float32(0.0), part[term]) + value
@@ -139,14 +172,14 @@
 
 
 def late_kernel(tick, place, weights, stay, low, part, incoming, plain, turned,
-                out_low, out_a, out_b, env_low):
+                out_low, out_a, out_b, env_low, *scratch):
     @pl.when(place[0] == 0)
     def _():
         pltpu.sync_copy(incoming.at[tick, :, 0, :LOW], env_low)
 
     @pl.when(place[0] != 0)
     def _():
-        env_low[...] = stay[:, :LOW] + low[...]
+        env_low[...] = stay[...] + low[...]
 
     def combine(term, value, first):
         row = 0
@@ -159,37 +192,41 @@
     row_products(place, weights, env_low, 0, plain, turned, combine)
 
 
-def first_kernel(place, weights, env, states, out_low, out_a, out_b, plain, turned):
+def first_kernel(place, weights, env, states, out_low, out_a, out_b, plain, turned,
+                 *scratch):
     def ready(state):
         fill(state, place, plain.shape[0], states, plain, turned)
 
-    products(2, place, weights, [env], plain, turned, [out_low, out_a, out_b], ready)
+    products(2, place, weights, [env], plain, turned, [out_low, out_a, out_b], scratch,
+             ready)
 
 
 def first_one_kernel(place, weights, env, states, plain_in, turned_in,
-                     out_low, out_high, plain, turned):
+                     out_low, out_high, plain, turned, *scratch):
     def ready(state):
         fill(state, place, plain.shape[0], states, plain, turned)
 
-    products(1, place, weights, [env], plain, turned, [out_low, out_high], ready)
-
-
-def first_zero_kernel(place, weights, env, states, plain_in, turned_in, out, plain, turned):
+    products(1, place, weights, [env], plain, turned, [out_low, out_high], scratch, ready)
+
+
+def first_zero_kernel(place, weights, env, states, plain_in, turned_in,
+                      out_low, out_high, plain, turned, *scratch):
     def ready(state):
         fill(state, place, plain.shape[0], states, plain, turned)
 
-    products(0, place, weights, [env], plain, turned, [out], ready)
-
-
-def one_kernel(place, weights, env_low, env_high, plain, turned, out_low, out_high):
-    products(1, place, weights, [env_low, env_high], plain, turned, [out_low, out_high])
-
-
-def zero_kernel(place, weights, env_low, env_high, plain, turned, out):
-    products(0, place, weights, [env_low, env_high], plain, turned, [out])
-
-
-def final_kernel(tick, place, stay, high, far_a, far_b, low, incoming, env):
+    looped(0, place, weights, [env], plain, turned, [out_low, out_high], ready)
+
+
+def one_kernel(place, weights, env_low, env_high, plain, turned, out_low, out_high, *scratch):
+    products(1, place, weights, [env_low, env_high], plain, turned, [out_low, out_high], scratch)
+
+
+def zero_kernel(place, weights, env_low, env_high, plain, turned, out_low, out_high, *scratch):
+    looped(0, place, weights, [env_low, env_high], plain, turned, [out_low, out_high])
+
+
+def final_kernel(tick, place, stay_low, stay_high, high, far_a, far_b, low, incoming, env,
+                 *scratch):
     @pl.when(place[0] == 0)
     def _():
         pltpu.sync_copy(incoming.at[tick, :, 0], env)
@@ -197,9 +234,9 @@
     @pl.when(place[0] != 0)
     def _():
         half = far_a.shape[1]
-        env[:, :LOW] = stay[:, :LOW] + low[...]
-        env[:, LOW : LOW + half] = stay[:, LOW : LOW + half] + high[:, :half] + far_a[...]
-        env[:, LOW + half :] = stay[:, LOW + half :] + high[:, half:] + far_b[...]
+        env[:, :LOW] = stay_low[...] + low[...]
+        env[:, LOW : LOW + half] = stay_high[:, :half] + high[:, :half] + far_a[...]
+        env[:, LOW + half :] = stay_high[:, half:] + high[:, half:] + far_b[...]
 
 
 def shape(*dims):
@@ -249,7 +286,9 @@
     scalars = (place, weights)
     plain, turned = None, None
 
-    def call(kernel, inputs, outputs, aliases={}):
+    def call(kernel, inputs, outputs, aliases={}, rows=None):
+        rows = rows or block
+        scratch = [(3 * rows, terms * block), (terms * rows, 3 * block)]
         specs = [SMEM if value.ndim == 1 else VMEM for value in inputs]
         specs = [HBM if value is incoming else spec for spec, value in zip(specs, inputs)]
         return pl.pallas_call(
@@ -257,6 +296,7 @@
             in_specs=specs,
             out_specs=[VMEM] * len(outputs),
             out_shape=outputs,
+            scratch_shapes=[pltpu.VMEM(dims, jnp.bfloat16) for dims in scratch],
             input_output_aliases=aliases,
             compiler_params=PARAMS,
             cost_estimate=cost,
@@ -271,8 +311,9 @@
         else:
             two_low, far_a, far_b, env_low = call(
                 functools.partial(late_kernel, tick - 1),
-                scalars + (kept, low, part, incoming, plain, turned),
+                scalars + (kept_low, low, part, incoming, plain, turned),
                 thirds + [parts[0]],
+                rows=LOW,
             )
         far_a = lax.ppermute(far_a, AXES, far_one)
         two_low = lax.ppermute(two_low, AXES, relay)
@@ -290,27 +331,31 @@
             )
         high = lax.ppermute(one_high, AXES, lift)
         if tick == 0:
-            zero, plain, turned = call(
+            zero_low, zero_high, plain, turned = call(
                 first_zero_kernel,
                 scalars + (env, states, plain, turned),
-                [whole] + split_states,
-                {4: 1, 5: 2},
+                parts + split_states,
+                {4: 2, 5: 3},
             )
         else:
-            (zero,) = call(zero_kernel, scalars + (env_low, env_high, plain, turned), [whole])
-        kept = lax.ppermute(zero, AXES, stay)
+            zero_low, zero_high = call(
+                zero_kernel, scalars + (env_low, env_high, plain, turned), parts
+            )
+        kept_high = lax.ppermute(zero_high, AXES, stay)
+        kept_low = lax.ppermute(zero_low, AXES, stay)
         low = lax.ppermute(one_low + two_low, AXES, lift)
         far_a = lax.ppermute(far_a, AXES, far_two)
         far_b = lax.ppermute(far_b, AXES, far_two)
         if tick < TICKS - 1:
             env_high, part = call(
                 functools.partial(early_kernel, tick),
-                scalars + (kept, high, far_a, far_b, incoming, plain, turned),
+                scalars + (kept_high, high, far_a, far_b, incoming, plain, turned),
                 [parts[1], whole],
+                rows=block - LOW,
             )
     (env,) = call(
         functools.partial(final_kernel, TICKS - 1),
-        (place, kept, high, far_a, far_b, low, incoming),
+        (place, kept_low, kept_high, high, far_a, far_b, low, incoming),
         [whole],
     )
     return env[None, :, None]

time: 354 us -> 349 us (0.986)
  waiting for transfers between devices: 179 us -> 171 us
  starting transfers between devices: 88.7 us -> 95.4 us
  Pallas kernels: 78.6 us -> 72.7 us
    ppermute x4, waiting for transfers between devices: 58.6 us -> 87 us  [local(): two_low = lax.ppermute(two_low, AXES, relay)]
    ppermute x4, waiting for transfers between devices: 38.7 us -> 15.5 us  [local(): far_b = lax.ppermute(far_b, AXES, far_one)]
    ppermute x4 -> x8, waiting for transfers between devices: 0.01 us -> 15.4 us  [the longest x4 15.4 us: local(): kept_low = lax.ppermute(zero_low, AXES, stay)]
    ppermute x4, waiting for transfers between devices: 13.5 us -> 0.01 us  [local(): far_a = lax.ppermute(far_a, AXES, far_one)]
    ppermute x4, waiting for transfers between devices: 61.8 us -> 48.7 us  [local(): low = lax.ppermute(one_low + two_low, AXES, lift)]
    pallas_call x16, Pallas kernels: 78.6 us -> 72.7 us  [call(): pl.pallas_call(kernel, in_specs=specs, out_specs=[VMEM] * len(outputs), o...]
    ppermute x4 -> x8, starting transfers between devices: 16.5 us -> 18.8 us  [the longest x4 9.51 us: local(): kept_low = lax.ppermute(zero_low, AXES, stay)]
  transfers between devices with their start and end apart: 32 -> 36, of which waited for: 16 -> 15; matrix products, arithmetic and copies ran while one was open for 0% -> 0% of each run, Pallas kernels for 10% -> 17%
where the time goes in v3:
time: 349 us; the launch traced here: 346 us
  waiting for transfers between devices  171 us (49%)
  starting transfers between devices  95.4 us (27%)
  Pallas kernels  72.7 us (21%)
  local copies, waits for them, and re-layouts  4.99 us (1%)
    ppermute x4, waiting for transfers between devices, local(): two_low = lax.ppermute(two_low, AXES, relay)  87 us
    pallas_call x16, Pallas kernels, call(): pl.pallas_call(kernel, in_specs=specs, out_specs=[VMEM] * len(outputs), o...  72.7 us
    ppermute x4, waiting for transfers between devices, local(): low = lax.ppermute(one_low + two_low, AXES, lift)  48.7 us
    ppermute x4, waiting for transfers between devices, local(): far_b = lax.ppermute(far_b, AXES, far_one)  15.5 us
    ppermute x4, waiting for transfers between devices, local(): kept_low = lax.ppermute(zero_low, AXES, stay)  15.4 us
    ppermute x4, starting transfers between devices, local(): low = lax.ppermute(one_low + two_low, AXES, lift)  12.6 us
    ppermute x4, starting transfers between devices, local(): far_a = lax.ppermute(far_a, AXES, far_one)  12.5 us
    ppermute x4, starting transfers between devices, local(): far_a = lax.ppermute(far_a, AXES, far_two)  12.4 us
  transfers between devices with their start and end apart: 36, of which 15 were waited for; matrix products, arithmetic and copies ran while one was open for 0% of the time, Pallas kernels for 17%

profile of v3, /device:TPU:1, one launch (start us, length us, event | category | flops | bytes accessed | tf_op | source)
XLA Modules:
  0.0 346.1 jit_solution(5683099745916494504)
XLA Ops:
  5.6 4.1 %shard_map.73 = (f32[3,128,384]{2,1,0:T(8,128)S(1)}, f32[3,128,384]{2,1,0:T(8,128)S(1)}, f32[3,128,384]{2,1,0:T(8,128)S(1)}, bf16[4,1152,384]{2,1,0:T(8,128)(2,1)S(1)}, bf16[4,384,1152]{2,1,0:T(8,128)(2,1)S(1)}) custom-call(s32[23]{0:T(128)S(1)} %concatenate.3.place, f32[576]{0:T(1024)S(1)} %reshape.3.weights, f32[3,384,384]{2,1,0:T(8,128)S(1)} %bitcast.8, ...), custom_call_target="tpu_custom_call" | custom-call | flops 2038431744 | bytes 7077888 | tf_op jit(solution)/shard_map/pallas_call | solution.py:294
  9.7 6.8 %collective-permute-start.5 = (f32[3,128,384]{2,1,0:T(8,128)S(1)}, f32[3,128,384]{2,1,0:T(8,128)S(1)}, u32[]{:S(2)}, u32[]{:S(2)}) collective-permute-start(f32[3,128,384]{2,1,0:T(8,128)S(1)} %get-tuple-element.57), channel_id=1, source_target_pairs={{0,19},{1,16},{2,21},{3,22},{4,23},{5,20},{6,25},{7,26},{8,27},{9,... | collective-permute-start | bytes 1769480 | tf_op jit(solution)/shard_map/ppermute | solution.py:318
  16.5 3.5 %collective-permute-start.7 = (f32[3,128,384]{2,1,0:T(8,128)S(1)}, f32[3,128,384]{2,1,0:T(8,128)S(1)}, u32[]{:S(2)}, u32[]{:S(2)}) collective-permute-start(f32[3,128,384]{2,1,0:T(8,128)S(1)} %get-tuple-element.58), channel_id=1, source_target_pairs={{0,19},{1,16},{2,21},{3,22},{4,23},{5,20},{6,25},{7,26},{8,27},{9,... | collective-permute-start | bytes 1769480 | tf_op jit(solution)/shard_map/ppermute | solution.py:320
  20.0 7.5 %shard_map.74 = (f32[3,128,384]{2,1,0:T(8,128)S(1)}, f32[3,256,384]{2,1,0:T(8,128)S(1)}, bf16[4,1152,384]{2,1,0:T(8,128)(2,1)S(1)}, bf16[4,384,1152]{2,1,0:T(8,128)(2,1)S(1)}) custom-call(s32[23]{0:T(128)S(1)} %concatenate.3.place, f32[576]{0:T(1024)S(1)} %reshape.3.weights, ...), custom_call_target="tpu_custom_call", output_to_operand_aliasing={{2}: (4, {}), {3}: (5, {})} | custom-call | flops 2038431744 | bytes 7077888 | tf_op jit(solution)/shard_map/pallas_call | solution.py:294
  27.6 3.0 collective-permute-start.4
  30.6 4.8 %shard_map.75 = (f32[3,128,384]{2,1,0:T(8,128)S(1)}, f32[3,256,384]{2,1,0:T(8,128)S(1)}, bf16[4,1152,384]{2,1,0:T(8,128)(2,1)S(1)}, bf16[4,384,1152]{2,1,0:T(8,128)(2,1)S(1)}) custom-call(s32[23]{0:T(128)S(1)} %concatenate.3.place, f32[576]{0:T(1024)S(1)} %reshape.3.weights, ...), custom_call_target="tpu_custom_call", output_to_operand_aliasing={{2}: (4, {}), {3}: (5, {})} | custom-call | flops 2038431744 | bytes 7077888 | tf_op jit(solution)/shard_map/pallas_call | solution.py:294
  35.4 2.6 collective-permute-start.3
  38.1 1.9 collective-permute-start.1
  40.0 5.9 %collective-permute-start.6 = (f32[3,128,384]{2,1,0:T(8,128)S(1)}, f32[3,128,384]{2,1,0:T(8,128)S(1)}, u32[]{:S(2)}, u32[]{:S(2)}) collective-permute-start(f32[3,128,384]{2,1,0:T(8,128)S(1)} %collective-permute-done.5), channel_id=1, source_target_pairs={{19,18},{16,19},{21,20},{22,21},{23,22},{20,23},{25,24},{26,25},{2... | collective-permute-start | bytes 1769480 | tf_op jit(solution)/shard_map/ppermute | solution.py:347
  45.9 3.1 collective-permute-start.8
  49.0 24.6 %collective-permute-done.1 = f32[3,128,384]{2,1,0:T(8,128)S(1)} collective-permute-done((f32[3,128,384]{2,1,0:T(8,128)S(1)}, f32[3,128,384]{2,1,0:T(8,128)S(1)}, u32[]{:S(2)}, u32[]{:S(2)}) %collective-permute-start.1) | collective-permute-done | bytes 589856 | tf_op jit(solution)/shard_map/ppermute | solution.py:319
  73.7 3.7 %collective-permute-start = (f32[3,128,384]{2,1,0:T(8,128)S(1)}, f32[3,128,384]{2,1,0:T(8,128)S(1)}, u32[]{:S(2)}, u32[]{:S(2)}) collective-permute-start(f32[3,128,384]{2,1,0:T(8,128)S(1)} %get-tuple-element.52), channel_id=1, source_target_pairs={{0,16},{1,17},{2,18},{3,19},{4,20},{5,21},{6,22},{7,23},{8,24},{9,... | collective-permute-start | bytes 1769480 | tf_op jit(solution)/shard_map/ppermute | solution.py:345
  77.5 1.9 collective-permute-start.2
  79.4 3.7 %shard_map.76 = (f32[3,256,384]{2,1,0:T(8,128)S(1)}, f32[3,384,384]{2,1,0:T(8,128)S(1)}) custom-call(s32[23]{0:T(128)S(1)} %concatenate.3.place, f32[576]{0:T(1024)S(1)} %reshape.3.weights, f32[3,256,384]{2,1,0:T(8,128)S(1)} %collective-permute-done.3.stay, f32[3,256,384]{2,1,0:T(8,128)S(1)} %collective-permute-done.4.high, ...), custom_call_target="tpu_custom_call" | custom-call | flops 2038431744 | bytes 7077888 | tf_op jit(solution)/shard_map/pallas_call | solution.py:294
  83.1 3.4 collective-permute-done.stay
  86.5 10.9 %collective-permute-done.2.low = f32[3,128,384]{2,1,0:T(8,128)S(1)} collective-permute-done((f32[3,128,384]{2,1,0:T(8,128)S(1)}, f32[3,128,384]{2,1,0:T(8,128)S(1)}, u32[]{:S(2)}, u32[]{:S(2)}) %collective-permute-start.2) | collective-permute-done | bytes 589856 | tf_op jit(solution)/shard_map/ppermute | solution.py:346
  97.5 2.7 shard_map.77
  100.2 1.9 collective-permute-start.14
  102.1 2.1 collective-permute-start.16
  104.2 7.1 %shard_map.79 = (f32[3,128,384]{2,1,0:T(8,128)S(1)}, f32[3,256,384]{2,1,0:T(8,128)S(1)}) custom-call(s32[23]{0:T(128)S(1)} %concatenate.3.place, f32[576]{0:T(1024)S(1)} %reshape.3.weights, f32[3,128,384]{2,1,0:T(8,128)S(1)} %get-tuple-element.62.env_low, f32[3,256,384]{2,1,0:T(8,128)S(1)} %get-tuple-element.63.env_high, ...), custom_call_target="tpu_custom_call" | custom-call | flops 2038431744 | bytes 7077888 | tf_op jit(solution)/shard_map/pallas_call | solution.py:294
  111.4 4.5 %shard_map.78 = (f32[3,128,384]{2,1,0:T(8,128)S(1)}, f32[3,256,384]{2,1,0:T(8,128)S(1)}) custom-call(s32[23]{0:T(128)S(1)} %concatenate.3.place, f32[576]{0:T(1024)S(1)} %reshape.3.weights, f32[3,128,384]{2,1,0:T(8,128)S(1)} %get-tuple-element.62.env_low, f32[3,256,384]{2,1,0:T(8,128)S(1)} %get-tuple-element.63.env_high, ...), custom_call_target="tpu_custom_call" | custom-call | flops 2038431744 | bytes 7077888 | tf_op jit(solution)/shard_map/pallas_call | solution.py:294
  115.9 2.8 collective-permute-start.12
  118.7 1.9 collective-permute-start.13
  120.6 3.1 collective-permute-start.10
  123.8 2.4 collective-permute-start.15
  126.2 4.1 %collective-permute-done.16 = f32[3,128,384]{2,1,0:T(8,128)S(1)} collective-permute-done((f32[3,128,384]{2,1,0:T(8,128)S(1)}, f32[3,128,384]{2,1,0:T(8,128)S(1)}, u32[]{:S(2)}, u32[]{:S(2)}) %collective-permute-start.16) | collective-permute-done | bytes 589856 | tf_op jit(solution)/shard_map/ppermute | solution.py:320
  130.3 1.9 collective-permute-start.17
  132.2 31.2 %collective-permute-done.10 = f32[3,128,384]{2,1,0:T(8,128)S(1)} collective-permute-done((f32[3,128,384]{2,1,0:T(8,128)S(1)}, f32[3,128,384]{2,1,0:T(8,128)S(1)}, u32[]{:S(2)}, u32[]{:S(2)}) %collective-permute-start.10) | collective-permute-done | bytes 589856 | tf_op jit(solution)/shard_map/ppermute | solution.py:319
  163.4 1.9 collective-permute-start.9
  165.4 1.9 collective-permute-start.11
  167.4 3.7 %shard_map.80 = (f32[3,256,384]{2,1,0:T(8,128)S(1)}, f32[3,384,384]{2,1,0:T(8,128)S(1)}) custom-call(s32[23]{0:T(128)S(1)} %concatenate.3.place, f32[576]{0:T(1024)S(1)} %reshape.3.weights, f32[3,256,384]{2,1,0:T(8,128)S(1)} %collective-permute-done.12.stay, f32[3,256,384]{2,1,0:T(8,128)S(1)} %collective-permute-done.13.high, ...), custom_call_target="tpu_custom_call" | custom-call | flops 2038431744 | bytes 7077888 | tf_op jit(solution)/shard_map/pallas_call | solution.py:294
  171.1 6.2 %collective-permute-done.9.stay = f32[3,128,384]{2,1,0:T(8,128)S(1)} collective-permute-done((f32[3,128,384]{2,1,0:T(8,128)S(1)}, f32[3,128,384]{2,1,0:T(8,128)S(1)}, u32[]{:S(2)}, u32[]{:S(2)}) %collective-permute-start.9) | collective-permute-done | bytes 589856 | tf_op jit(solution)/shard_map/ppermute | solution.py:345
  177.3 7.1 %collective-permute-done.11.low = f32[3,128,384]{2,1,0:T(8,128)S(1)} collective-permute-done((f32[3,128,384]{2,1,0:T(8,128)S(1)}, f32[3,128,384]{2,1,0:T(8,128)S(1)}, u32[]{:S(2)}, u32[]{:S(2)}) %collective-permute-start.11) | collective-permute-done | bytes 589856 | tf_op jit(solution)/shard_map/ppermute | solution.py:346
  184.4 2.7 shard_map.81
  187.1 1.9 collective-permute-start.23
  189.0 1.9 collective-permute-start.25
  190.9 7.1 %shard_map.83 = (f32[3,128,384]{2,1,0:T(8,128)S(1)}, f32[3,256,384]{2,1,0:T(8,128)S(1)}) custom-call(s32[23]{0:T(128)S(1)} %concatenate.3.place, f32[576]{0:T(1024)S(1)} %reshape.3.weights, f32[3,128,384]{2,1,0:T(8,128)S(1)} %get-tuple-element.72.env_low, f32[3,256,384]{2,1,0:T(8,128)S(1)} %get-tuple-element.73.env_high, ...), custom_call_target="tpu_custom_call" | custom-call | flops 2038431744 | bytes 7077888 | tf_op jit(solution)/shard_map/pallas_call | solution.py:294
  198.1 4.5 %shard_map.82 = (f32[3,128,384]{2,1,0:T(8,128)S(1)}, f32[3,256,384]{2,1,0:T(8,128)S(1)}) custom-call(s32[23]{0:T(128)S(1)} %concatenate.3.place, f32[576]{0:T(1024)S(1)} %reshape.3.weights, f32[3,128,384]{2,1,0:T(8,128)S(1)} %get-tuple-element.72.env_low, f32[3,256,384]{2,1,0:T(8,128)S(1)} %get-tuple-element.73.env_high, ...), custom_call_target="tpu_custom_call" | custom-call | flops 2038431744 | bytes 7077888 | tf_op jit(solution)/shard_map/pallas_call | solution.py:294
  202.6 1.9 collective-permute-start.21
  204.6 1.9 collective-permute-start.22
  206.5 2.9 collective-permute-start.19
  209.4 2.1 collective-permute-start.24
  211.6 5.7 %collective-permute-done.25 = f32[3,128,384]{2,1,0:T(8,128)S(1)} collective-permute-done((f32[3,128,384]{2,1,0:T(8,128)S(1)}, f32[3,128,384]{2,1,0:T(8,128)S(1)}, u32[]{:S(2)}, u32[]{:S(2)}) %collective-permute-start.25) | collective-permute-done | bytes 589856 | tf_op jit(solution)/shard_map/ppermute | solution.py:320
  217.2 1.9 collective-permute-start.26
  219.2 29.8 %collective-permute-done.19 = f32[3,128,384]{2,1,0:T(8,128)S(1)} collective-permute-done((f32[3,128,384]{2,1,0:T(8,128)S(1)}, f32[3,128,384]{2,1,0:T(8,128)S(1)}, u32[]{:S(2)}, u32[]{:S(2)}) %collective-permute-start.19) | collective-permute-done | bytes 589856 | tf_op jit(solution)/shard_map/ppermute | solution.py:319
  248.9 2.0 collective-permute-start.18
  251.0 1.9 collective-permute-start.20
  253.0 3.9 %shard_map.84 = (f32[3,256,384]{2,1,0:T(8,128)S(1)}, f32[3,384,384]{2,1,0:T(8,128)S(1)}) custom-call(s32[23]{0:T(128)S(1)} %concatenate.3.place, f32[576]{0:T(1024)S(1)} %reshape.3.weights, f32[3,256,384]{2,1,0:T(8,128)S(1)} %collective-permute-done.21.stay, f32[3,256,384]{2,1,0:T(8,128)S(1)} %collective-permute-done.22.high, ...), custom_call_target="tpu_custom_call" | custom-call | flops 2038431744 | bytes 7077888 | tf_op jit(solution)/shard_map/pallas_call | solution.py:294
  256.9 5.8 %collective-permute-done.18.stay = f32[3,128,384]{2,1,0:T(8,128)S(1)} collective-permute-done((f32[3,128,384]{2,1,0:T(8,128)S(1)}, f32[3,128,384]{2,1,0:T(8,128)S(1)}, u32[]{:S(2)}, u32[]{:S(2)}) %collective-permute-start.18) | collective-permute-done | bytes 589856 | tf_op jit(solution)/shard_map/ppermute | solution.py:345
  262.7 8.3 %collective-permute-done.20.low = f32[3,128,384]{2,1,0:T(8,128)S(1)} collective-permute-done((f32[3,128,384]{2,1,0:T(8,128)S(1)}, f32[3,128,384]{2,1,0:T(8,128)S(1)}, u32[]{:S(2)}, u32[]{:S(2)}) %collective-permute-start.20) | collective-permute-done | bytes 589856 | tf_op jit(solution)/shard_map/ppermute | solution.py:346
  271.0 2.7 shard_map.85
  273.7 1.9 collective-permute-start.30
  275.7 7.1 %shard_map.87 = (f32[3,128,384]{2,1,0:T(8,128)S(1)}, f32[3,256,384]{2,1,0:T(8,128)S(1)}) custom-call(s32[23]{0:T(128)S(1)} %concatenate.3.place, f32[576]{0:T(1024)S(1)} %reshape.3.weights, f32[3,128,384]{2,1,0:T(8,128)S(1)} %get-tuple-element.82.env_low, f32[3,256,384]{2,1,0:T(8,128)S(1)} %get-tuple-element.83.env_high, ...), custom_call_target="tpu_custom_call" | custom-call | flops 2038431744 | bytes 7077888 | tf_op jit(solution)/shard_map/pallas_call | solution.py:294
  282.8 4.5 %shard_map.86 = (f32[3,128,384]{2,1,0:T(8,128)S(1)}, f32[3,256,384]{2,1,0:T(8,128)S(1)}) custom-call(s32[23]{0:T(128)S(1)} %concatenate.3.place, f32[576]{0:T(1024)S(1)} %reshape.3.weights, f32[3,128,384]{2,1,0:T(8,128)S(1)} %get-tuple-element.82.env_low, f32[3,256,384]{2,1,0:T(8,128)S(1)} %get-tuple-element.83.env_high, ...), custom_call_target="tpu_custom_call" | custom-call | flops 2038431744 | bytes 7077888 | tf_op jit(solution)/shard_map/pallas_call | solution.py:294
  287.4 1.9 collective-permute-start.32
  289.3 4.0 %collective-permute-start.34 = (f32[3,128,384]{2,1,0:T(8,128)S(1)}, f32[3,128,384]{2,1,0:T(8,128)S(1)}, u32[]{:S(2)}, u32[]{:S(2)}) collective-permute-start(f32[3,128,384]{2,1,0:T(8,128)S(1)} %get-tuple-element.90), channel_id=1, source_target_pairs={{0,1},{1,2},{2,3},{3,4},{4,5},{5,6},{6,7},{7,8},{8,9},{9,10},{10,1... | collective-permute-start | bytes 1769480 | tf_op jit(solution)/shard_map/ppermute | solution.py:319
  293.3 1.9 collective-permute-start.27
  295.2 1.9 collective-permute-start.29
  297.2 1.9 collective-permute-start.28
  299.1 5.7 %collective-permute-done.32 = f32[3,128,384]{2,1,0:T(8,128)S(1)} collective-permute-done((f32[3,128,384]{2,1,0:T(8,128)S(1)}, f32[3,128,384]{2,1,0:T(8,128)S(1)}, u32[]{:S(2)}, u32[]{:S(2)}) %collective-permute-start.32) | collective-permute-done | bytes 589856 | tf_op jit(solution)/shard_map/ppermute | solution.py:320
  310.1 6.8 %collective-permute-start.35 = (f32[3,128,384]{2,1,0:T(8,128)S(1)}, f32[3,128,384]{2,1,0:T(8,128)S(1)}, u32[]{:S(2)}, u32[]{:S(2)}) collective-permute-start(f32[3,128,384]{2,1,0:T(8,128)S(1)} %add.15), channel_id=1, source_target_pairs={{0,17},{1,18},{2,19},{3,20},{4,21},{5,22},{6,23},{7,24},{8,25},{9,... | collective-permute-start | bytes 1769480 | tf_op jit(solution)/shard_map/ppermute | solution.py:346
  317.0 4.8 %collective-permute-done.33.far_b = f32[3,128,384]{2,1,0:T(8,128)S(1)} collective-permute-done((f32[3,128,384]{2,1,0:T(8,128)S(1)}, f32[3,128,384]{2,1,0:T(8,128)S(1)}, u32[]{:S(2)}, u32[]{:S(2)}) %collective-permute-start.33) | collective-permute-done | bytes 589856 | tf_op jit(solution)/shard_map/ppermute | solution.py:348
  321.8 22.3 %collective-permute-done.35.low = f32[3,128,384]{2,1,0:T(8,128)S(1)} collective-permute-done((f32[3,128,384]{2,1,0:T(8,128)S(1)}, f32[3,128,384]{2,1,0:T(8,128)S(1)}, u32[]{:S(2)}, u32[]{:S(2)}) %collective-permute-start.35) | collective-permute-done | bytes 589856 | tf_op jit(solution)/shard_map/ppermute | solution.py:346
  344.1 2.0 shard_map.88
  (40 shorter events, 10.5 us)
Async XLA Ops:
  2.5 1.7 copy-start
  4.2 1.5 copy-start.1
  9.7 30.3 %collective-permute-start.5 = (f32[3,128,384]{2,1,0:T(8,128)S(1)}, f32[3,128,384]{2,1,0:T(8,128)S(1)}, u32[]{:S(2)}, u32[]{:S(2)}) collective-permute-start(f32[3,128,384]{2,1,0:T(8,128)S(1)} %get-tuple-element.57), channel_id=1, source_target_pairs={{0,19},{1,16},{2,21},{3,22},{4,23},{5,20},{6,25},{7,26},{8,27},{9,... | collective-permute-start | bytes 1769480 | tf_op jit(solution)/shard_map/ppermute | solution.py:318
  16.5 29.4 %collective-permute-start.7 = (f32[3,128,384]{2,1,0:T(8,128)S(1)}, f32[3,128,384]{2,1,0:T(8,128)S(1)}, u32[]{:S(2)}, u32[]{:S(2)}) collective-permute-start(f32[3,128,384]{2,1,0:T(8,128)S(1)} %get-tuple-element.58), channel_id=1, source_target_pairs={{0,19},{1,16},{2,21},{3,22},{4,23},{5,20},{6,25},{7,26},{8,27},{9,... | collective-permute-start | bytes 1769480 | tf_op jit(solution)/shard_map/ppermute | solution.py:320
  27.6 51.8 %collective-permute-start.4 = (f32[3,256,384]{2,1,0:T(8,128)S(1)}, f32[3,256,384]{2,1,0:T(8,128)S(1)}, u32[]{:S(2)}, u32[]{:S(2)}) collective-permute-start(f32[3,256,384]{2,1,0:T(8,128)S(1)} %get-tuple-element.56), channel_id=1, source_target_pairs={{0,17},{1,18},{2,19},{3,20},{4,21},{5,22},{6,23},{7,24},{8,25},{9,... | collective-permute-start | bytes 3538952 | tf_op jit(solution)/shard_map/ppermute | solution.py:332
  30.6 48.8 %slice-start = ((s8[7077888]{0:T(1024)(128)(4,1)}), s8[4194304]{0:T(1024)(128)(4,1)S(1)}, s32[]{:S(2)}) async-start(s8[7077888]{0:T(1024)(128)(4,1)} %bitcast.6), calls=%async_computation | async-start | bytes 8388608
  30.6 48.8 %slice-start.1 = ((s8[7077888]{0:T(1024)(128)(4,1)}), s8[2883584]{0:T(1024)(128)(4,1)S(1)}, s32[]{:S(2)}) async-start(s8[7077888]{0:T(1024)(128)(4,1)} %bitcast.6), calls=%async_computation.1 | async-start | bytes 5767168
  35.4 44.0 %collective-permute-start.3 = (f32[3,256,384]{2,1,0:T(8,128)S(1)}, f32[3,256,384]{2,1,0:T(8,128)S(1)}, u32[]{:S(2)}, u32[]{:S(2)}) collective-permute-start(f32[3,256,384]{2,1,0:T(8,128)S(1)} %get-tuple-element.55), channel_id=1, source_target_pairs={{0,16},{1,17},{2,18},{3,19},{4,20},{5,21},{6,22},{7,23},{8,24},{9,... | collective-permute-start | bytes 3538952 | tf_op jit(solution)/shard_map/ppermute | solution.py:344
  38.1 35.6 %collective-permute-start.1 = (f32[3,128,384]{2,1,0:T(8,128)S(1)}, f32[3,128,384]{2,1,0:T(8,128)S(1)}, u32[]{:S(2)}, u32[]{:S(2)}) collective-permute-start(f32[3,128,384]{2,1,0:T(8,128)S(1)} %get-tuple-element.54), channel_id=1, source_target_pairs={{0,1},{1,2},{2,3},{3,4},{4,5},{5,6},{6,7},{7,8},{8,9},{9,10},{10,1... | collective-permute-start | bytes 1769480 | tf_op jit(solution)/shard_map/ppermute | solution.py:319
  40.0 37.4 %collective-permute-start.6 = (f32[3,128,384]{2,1,0:T(8,128)S(1)}, f32[3,128,384]{2,1,0:T(8,128)S(1)}, u32[]{:S(2)}, u32[]{:S(2)}) collective-permute-start(f32[3,128,384]{2,1,0:T(8,128)S(1)} %collective-permute-done.5), channel_id=1, source_target_pairs={{19,18},{16,19},{21,20},{22,21},{23,22},{20,23},{25,24},{26,25},{2... | collective-permute-start | bytes 1769480 | tf_op jit(solution)/shard_map/ppermute | solution.py:347
  45.9 33.4 %collective-permute-start.8 = (f32[3,128,384]{2,1,0:T(8,128)S(1)}, f32[3,128,384]{2,1,0:T(8,128)S(1)}, u32[]{:S(2)}, u32[]{:S(2)}) collective-permute-start(f32[3,128,384]{2,1,0:T(8,128)S(1)} %collective-permute-done.7), channel_id=1, source_target_pairs={{19,18},{16,19},{21,20},{22,21},{23,22},{20,23},{25,24},{26,25},{2... | collective-permute-start | bytes 1769480 | tf_op jit(solution)/shard_map/ppermute | solution.py:348
  73.7 12.8 %collective-permute-start = (f32[3,128,384]{2,1,0:T(8,128)S(1)}, f32[3,128,384]{2,1,0:T(8,128)S(1)}, u32[]{:S(2)}, u32[]{:S(2)}) collective-permute-start(f32[3,128,384]{2,1,0:T(8,128)S(1)} %get-tuple-element.52), channel_id=1, source_target_pairs={{0,16},{1,17},{2,18},{3,19},{4,20},{5,21},{6,22},{7,23},{8,24},{9,... | collective-permute-start | bytes 1769480 | tf_op jit(solution)/shard_map/ppermute | solution.py:345
  77.5 20.0 %collective-permute-start.2 = (f32[3,128,384]{2,1,0:T(8,128)S(1)}, f32[3,128,384]{2,1,0:T(8,128)S(1)}, u32[]{:S(2)}, u32[]{:S(2)}) collective-permute-start(f32[3,128,384]{2,1,0:T(8,128)S(1)} %add.12), channel_id=1, source_target_pairs={{0,17},{1,18},{2,19},{3,20},{4,21},{5,22},{6,23},{7,24},{8,25},{9,... | collective-permute-start | bytes 1769480 | tf_op jit(solution)/shard_map/ppermute | solution.py:346
  100.2 23.6 %collective-permute-start.14 = (f32[3,128,384]{2,1,0:T(8,128)S(1)}, f32[3,128,384]{2,1,0:T(8,128)S(1)}, u32[]{:S(2)}, u32[]{:S(2)}) collective-permute-start(f32[3,128,384]{2,1,0:T(8,128)S(1)} %get-tuple-element.69), channel_id=1, source_target_pairs={{0,19},{1,16},{2,21},{3,22},{4,23},{5,20},{6,25},{7,26},{8,27},{9,... | collective-permute-start | bytes 1769480 | tf_op jit(solution)/shard_map/ppermute | solution.py:318
  102.1 28.2 %collective-permute-start.16 = (f32[3,128,384]{2,1,0:T(8,128)S(1)}, f32[3,128,384]{2,1,0:T(8,128)S(1)}, u32[]{:S(2)}, u32[]{:S(2)}) collective-permute-start(f32[3,128,384]{2,1,0:T(8,128)S(1)} %get-tuple-element.70), channel_id=1, source_target_pairs={{0,19},{1,16},{2,21},{3,22},{4,23},{5,20},{6,25},{7,26},{8,27},{9,... | collective-permute-start | bytes 1769480 | tf_op jit(solution)/shard_map/ppermute | solution.py:320
  115.9 51.5 %collective-permute-start.12 = (f32[3,256,384]{2,1,0:T(8,128)S(1)}, f32[3,256,384]{2,1,0:T(8,128)S(1)}, u32[]{:S(2)}, u32[]{:S(2)}) collective-permute-start(f32[3,256,384]{2,1,0:T(8,128)S(1)} %get-tuple-element.67), channel_id=1, source_target_pairs={{0,16},{1,17},{2,18},{3,19},{4,20},{5,21},{6,22},{7,23},{8,24},{9,... | collective-permute-start | bytes 3538952 | tf_op jit(solution)/shard_map/ppermute | solution.py:344
  118.7 48.7 %collective-permute-start.13 = (f32[3,256,384]{2,1,0:T(8,128)S(1)}, f32[3,256,384]{2,1,0:T(8,128)S(1)}, u32[]{:S(2)}, u32[]{:S(2)}) collective-permute-start(f32[3,256,384]{2,1,0:T(8,128)S(1)} %get-tuple-element.68), channel_id=1, source_target_pairs={{0,17},{1,18},{2,19},{3,20},{4,21},{5,22},{6,23},{7,24},{8,25},{9,... | collective-permute-start | bytes 3538952 | tf_op jit(solution)/shard_map/ppermute | solution.py:332
  120.6 42.8 %collective-permute-start.10 = (f32[3,128,384]{2,1,0:T(8,128)S(1)}, f32[3,128,384]{2,1,0:T(8,128)S(1)}, u32[]{:S(2)}, u32[]{:S(2)}) collective-permute-start(f32[3,128,384]{2,1,0:T(8,128)S(1)} %get-tuple-element.66), channel_id=1, source_target_pairs={{0,1},{1,2},{2,3},{3,4},{4,5},{5,6},{6,7},{7,8},{8,9},{9,10},{10,1... | collective-permute-start | bytes 1769480 | tf_op jit(solution)/shard_map/ppermute | solution.py:319
  123.8 41.7 %collective-permute-start.15 = (f32[3,128,384]{2,1,0:T(8,128)S(1)}, f32[3,128,384]{2,1,0:T(8,128)S(1)}, u32[]{:S(2)}, u32[]{:S(2)}) collective-permute-start(f32[3,128,384]{2,1,0:T(8,128)S(1)} %collective-permute-done.14), channel_id=1, source_target_pairs={{19,18},{16,19},{21,20},{22,21},{23,22},{20,23},{25,24},{26,25},{2... | collective-permute-start | bytes 1769480 | tf_op jit(solution)/shard_map/ppermute | solution.py:347
  130.3 37.1 %collective-permute-start.17 = (f32[3,128,384]{2,1,0:T(8,128)S(1)}, f32[3,128,384]{2,1,0:T(8,128)S(1)}, u32[]{:S(2)}, u32[]{:S(2)}) collective-permute-start(f32[3,128,384]{2,1,0:T(8,128)S(1)} %collective-permute-done.16), channel_id=1, source_target_pairs={{19,18},{16,19},{21,20},{22,21},{23,22},{20,23},{25,24},{26,25},{2... | collective-permute-start | bytes 1769480 | tf_op jit(solution)/shard_map/ppermute | solution.py:348
  163.4 13.8 %collective-permute-start.9 = (f32[3,128,384]{2,1,0:T(8,128)S(1)}, f32[3,128,384]{2,1,0:T(8,128)S(1)}, u32[]{:S(2)}, u32[]{:S(2)}) collective-permute-start(f32[3,128,384]{2,1,0:T(8,128)S(1)} %get-tuple-element.64), channel_id=1, source_target_pairs={{0,16},{1,17},{2,18},{3,19},{4,20},{5,21},{6,22},{7,23},{8,24},{9,... | collective-permute-start | bytes 1769480 | tf_op jit(solution)/shard_map/ppermute | solution.py:345
  165.4 18.9 %collective-permute-start.11 = (f32[3,128,384]{2,1,0:T(8,128)S(1)}, f32[3,128,384]{2,1,0:T(8,128)S(1)}, u32[]{:S(2)}, u32[]{:S(2)}) collective-permute-start(f32[3,128,384]{2,1,0:T(8,128)S(1)} %add.13), channel_id=1, source_target_pairs={{0,17},{1,18},{2,19},{3,20},{4,21},{5,22},{6,23},{7,24},{8,25},{9,... | collective-permute-start | bytes 1769480 | tf_op jit(solution)/shard_map/ppermute | solution.py:346
  187.1 22.3 %collective-permute-start.23 = (f32[3,128,384]{2,1,0:T(8,128)S(1)}, f32[3,128,384]{2,1,0:T(8,128)S(1)}, u32[]{:S(2)}, u32[]{:S(2)}) collective-permute-start(f32[3,128,384]{2,1,0:T(8,128)S(1)} %get-tuple-element.79), channel_id=1, source_target_pairs={{0,19},{1,16},{2,21},{3,22},{4,23},{5,20},{6,25},{7,26},{8,27},{9,... | collective-permute-start | bytes 1769480 | tf_op jit(solution)/shard_map/ppermute | solution.py:318
  189.0 28.2 %collective-permute-start.25 = (f32[3,128,384]{2,1,0:T(8,128)S(1)}, f32[3,128,384]{2,1,0:T(8,128)S(1)}, u32[]{:S(2)}, u32[]{:S(2)}) collective-permute-start(f32[3,128,384]{2,1,0:T(8,128)S(1)} %get-tuple-element.80), channel_id=1, source_target_pairs={{0,19},{1,16},{2,21},{3,22},{4,23},{5,20},{6,25},{7,26},{8,27},{9,... | collective-permute-start | bytes 1769480 | tf_op jit(solution)/shard_map/ppermute | solution.py:320
  202.6 50.3 %collective-permute-start.21 = (f32[3,256,384]{2,1,0:T(8,128)S(1)}, f32[3,256,384]{2,1,0:T(8,128)S(1)}, u32[]{:S(2)}, u32[]{:S(2)}) collective-permute-start(f32[3,256,384]{2,1,0:T(8,128)S(1)} %get-tuple-element.77), channel_id=1, source_target_pairs={{0,16},{1,17},{2,18},{3,19},{4,20},{5,21},{6,22},{7,23},{8,24},{9,... | collective-permute-start | bytes 3538952 | tf_op jit(solution)/shard_map/ppermute | solution.py:344
  204.6 48.4 %collective-permute-start.22 = (f32[3,256,384]{2,1,0:T(8,128)S(1)}, f32[3,256,384]{2,1,0:T(8,128)S(1)}, u32[]{:S(2)}, u32[]{:S(2)}) collective-permute-start(f32[3,256,384]{2,1,0:T(8,128)S(1)} %get-tuple-element.78), channel_id=1, source_target_pairs={{0,17},{1,18},{2,19},{3,20},{4,21},{5,22},{6,23},{7,24},{8,25},{9,... | collective-permute-start | bytes 3538952 | tf_op jit(solution)/shard_map/ppermute | solution.py:332
  206.5 42.5 %collective-permute-start.19 = (f32[3,128,384]{2,1,0:T(8,128)S(1)}, f32[3,128,384]{2,1,0:T(8,128)S(1)}, u32[]{:S(2)}, u32[]{:S(2)}) collective-permute-start(f32[3,128,384]{2,1,0:T(8,128)S(1)} %get-tuple-element.76), channel_id=1, source_target_pairs={{0,1},{1,2},{2,3},{3,4},{4,5},{5,6},{6,7},{7,8},{8,9},{9,10},{10,1... | collective-permute-start | bytes 1769480 | tf_op jit(solution)/shard_map/ppermute | solution.py:319
  209.4 41.6 %collective-permute-start.24 = (f32[3,128,384]{2,1,0:T(8,128)S(1)}, f32[3,128,384]{2,1,0:T(8,128)S(1)}, u32[]{:S(2)}, u32[]{:S(2)}) collective-permute-start(f32[3,128,384]{2,1,0:T(8,128)S(1)} %collective-permute-done.23), channel_id=1, source_target_pairs={{19,18},{16,19},{21,20},{22,21},{23,22},{20,23},{25,24},{26,25},{2... | collective-permute-start | bytes 1769480 | tf_op jit(solution)/shard_map/ppermute | solution.py:347
  217.2 35.7 %collective-permute-start.26 = (f32[3,128,384]{2,1,0:T(8,128)S(1)}, f32[3,128,384]{2,1,0:T(8,128)S(1)}, u32[]{:S(2)}, u32[]{:S(2)}) collective-permute-start(f32[3,128,384]{2,1,0:T(8,128)S(1)} %collective-permute-done.25), channel_id=1, source_target_pairs={{19,18},{16,19},{21,20},{22,21},{23,22},{20,23},{25,24},{26,25},{2... | collective-permute-start | bytes 1769480 | tf_op jit(solution)/shard_map/ppermute | solution.py:348
  248.9 13.7 %collective-permute-start.18 = (f32[3,128,384]{2,1,0:T(8,128)S(1)}, f32[3,128,384]{2,1,0:T(8,128)S(1)}, u32[]{:S(2)}, u32[]{:S(2)}) collective-permute-start(f32[3,128,384]{2,1,0:T(8,128)S(1)} %get-tuple-element.74), channel_id=1, source_target_pairs={{0,16},{1,17},{2,18},{3,19},{4,20},{5,21},{6,22},{7,23},{8,24},{9,... | collective-permute-start | bytes 1769480 | tf_op jit(solution)/shard_map/ppermute | solution.py:345
  251.0 20.0 %collective-permute-start.20 = (f32[3,128,384]{2,1,0:T(8,128)S(1)}, f32[3,128,384]{2,1,0:T(8,128)S(1)}, u32[]{:S(2)}, u32[]{:S(2)}) collective-permute-start(f32[3,128,384]{2,1,0:T(8,128)S(1)} %add.14), channel_id=1, source_target_pairs={{0,17},{1,18},{2,19},{3,20},{4,21},{5,22},{6,23},{7,24},{8,25},{9,... | collective-permute-start | bytes 1769480 | tf_op jit(solution)/shard_map/ppermute | solution.py:346
  273.7 23.4 %collective-permute-start.30 = (f32[3,128,384]{2,1,0:T(8,128)S(1)}, f32[3,128,384]{2,1,0:T(8,128)S(1)}, u32[]{:S(2)}, u32[]{:S(2)}) collective-permute-start(f32[3,128,384]{2,1,0:T(8,128)S(1)} %get-tuple-element.87), channel_id=1, source_target_pairs={{0,19},{1,16},{2,21},{3,22},{4,23},{5,20},{6,25},{7,26},{8,27},{9,... | collective-permute-start | bytes 1769480 | tf_op jit(solution)/shard_map/ppermute | solution.py:318
  287.4 17.5 %collective-permute-start.32 = (f32[3,128,384]{2,1,0:T(8,128)S(1)}, f32[3,128,384]{2,1,0:T(8,128)S(1)}, u32[]{:S(2)}, u32[]{:S(2)}) collective-permute-start(f32[3,128,384]{2,1,0:T(8,128)S(1)} %get-tuple-element.88), channel_id=1, source_target_pairs={{0,19},{1,16},{2,21},{3,22},{4,23},{5,20},{6,25},{7,26},{8,27},{9,... | collective-permute-start | bytes 1769480 | tf_op jit(solution)/shard_map/ppermute | solution.py:320
  289.3 18.8 %collective-permute-start.34 = (f32[3,128,384]{2,1,0:T(8,128)S(1)}, f32[3,128,384]{2,1,0:T(8,128)S(1)}, u32[]{:S(2)}, u32[]{:S(2)}) collective-permute-start(f32[3,128,384]{2,1,0:T(8,128)S(1)} %get-tuple-element.90), channel_id=1, source_target_pairs={{0,1},{1,2},{2,3},{3,4},{4,5},{5,6},{6,7},{7,8},{8,9},{9,10},{10,1... | collective-permute-start | bytes 1769480 | tf_op jit(solution)/shard_map/ppermute | solution.py:319
  293.3 16.9 %collective-permute-start.27 = (f32[3,128,384]{2,1,0:T(8,128)S(1)}, f32[3,128,384]{2,1,0:T(8,128)S(1)}, u32[]{:S(2)}, u32[]{:S(2)}) collective-permute-start(f32[3,128,384]{2,1,0:T(8,128)S(1)} %get-tuple-element.84), channel_id=1, source_target_pairs={{0,16},{1,17},{2,18},{3,19},{4,20},{5,21},{6,22},{7,23},{8,24},{9,... | collective-permute-start | bytes 1769480 | tf_op jit(solution)/shard_map/ppermute | solution.py:345
  295.2 48.9 %collective-permute-start.29 = (f32[3,256,384]{2,1,0:T(8,128)S(1)}, f32[3,256,384]{2,1,0:T(8,128)S(1)}, u32[]{:S(2)}, u32[]{:S(2)}) collective-permute-start(f32[3,256,384]{2,1,0:T(8,128)S(1)} %get-tuple-element.86), channel_id=1, source_target_pairs={{0,17},{1,18},{2,19},{3,20},{4,21},{5,22},{6,23},{7,24},{8,25},{9,... | collective-permute-start | bytes 3538952 | tf_op jit(solution)/shard_map/ppermute | solution.py:332
  297.2 46.9 %collective-permute-start.28 = (f32[3,256,384]{2,1,0:T(8,128)S(1)}, f32[3,256,384]{2,1,0:T(8,128)S(1)}, u32[]{:S(2)}, u32[]{:S(2)}) collective-permute-start(f32[3,256,384]{2,1,0:T(8,128)S(1)} %get-tuple-element.85), channel_id=1, source_target_pairs={{0,16},{1,17},{2,18},{3,19},{4,20},{5,21},{6,22},{7,23},{8,24},{9,... | collective-permute-start | bytes 3538952 | tf_op jit(solution)/shard_map/ppermute | solution.py:344
  304.8 12.2 %collective-permute-start.31 = (f32[3,128,384]{2,1,0:T(8,128)S(1)}, f32[3,128,384]{2,1,0:T(8,128)S(1)}, u32[]{:S(2)}, u32[]{:S(2)}) collective-permute-start(f32[3,128,384]{2,1,0:T(8,128)S(1)} %collective-permute-done.30), channel_id=1, source_target_pairs={{19,18},{16,19},{21,20},{22,21},{23,22},{20,23},{25,24},{26,25},{2... | collective-permute-start | bytes 1769480 | tf_op jit(solution)/shard_map/ppermute | solution.py:347
  308.1 13.6 %collective-permute-start.33 = (f32[3,128,384]{2,1,0:T(8,128)S(1)}, f32[3,128,384]{2,1,0:T(8,128)S(1)}, u32[]{:S(2)}, u32[]{:S(2)}) collective-permute-start(f32[3,128,384]{2,1,0:T(8,128)S(1)} %collective-permute-done.32), channel_id=1, source_target_pairs={{19,18},{16,19},{21,20},{22,21},{23,22},{20,23},{25,24},{26,25},{2... | collective-permute-start | bytes 1769480 | tf_op jit(solution)/shard_map/ppermute | solution.py:348
  310.1 33.9 %collective-permute-start.35 = (f32[3,128,384]{2,1,0:T(8,128)S(1)}, f32[3,128,384]{2,1,0:T(8,128)S(1)}, u32[]{:S(2)}, u32[]{:S(2)}) collective-permute-start(f32[3,128,384]{2,1,0:T(8,128)S(1)} %add.15), channel_id=1, source_target_pairs={{0,17},{1,18},{2,19},{3,20},{4,21},{5,22},{6,23},{7,24},{8,25},{9,... | collective-permute-start | bytes 1769480 | tf_op jit(solution)/shard_map/ppermute | solution.py:346

commit v4 on v3

--- a/solution.py
+++ b/solution.py
@@ -98,12 +98,11 @@
             tall[lines, 2 * block :] = low
         triple = dot(tall[...], plain_ref[state])
         for term in range(terms):
-            row = term * block
-            for ref in stores:
+            base = term * block
+            for row, ref in stores:
                 rows = ref.shape[1]
                 before = jnp.where(first, jnp.float32(0.0), ref[term])
-                ref[term] = before + triple[row : row + rows]
-                row += rows
+                ref[term] = before + triple[base + row : base + row + rows]
 
     each_state(offset, place, count, body)
 
@@ -121,12 +120,10 @@
             right = dot(turned_ref[state], jnp.concatenate([high, low, high], axis=0))
             high, low = halves(right)
             triple = dot(jnp.concatenate([high, high, low], axis=1), plain_ref[state])
-            row = 0
-            for ref in stores:
+            for row, ref in stores:
                 rows = ref.shape[1]
                 before = jnp.where(first, jnp.float32(0.0), ref[out_term])
                 ref[out_term] = before + triple[row : row + rows]
-                row += rows
 
     each_state(offset, place, count, body)
 
@@ -153,7 +150,7 @@
     each_state(2, place, count, body)
 
 
-def early_kernel(tick, place, weights, stay, high, far_a, far_b, incoming, plain, turned,
+def early_kernel(tick, place, weights, rest, kept, high, far_a, far_b, incoming, plain, turned,
                  env_high, part, *scratch):
     @pl.when(place[0] == 0)
     def _():
@@ -162,8 +159,8 @@
     @pl.when(place[0] != 0)
     def _():
         half = far_a.shape[1]
-        env_high[:, :half] = stay[:, :half] + high[:, :half] + far_a[...]
-        env_high[:, half:] = stay[:, half:] + high[:, half:] + far_b[...]
+        env_high[:, :half] = kept[...] + far_a[...]
+        env_high[:, half:] = rest[:, LOW:] + high[...] + far_b[...]
 
     def combine(term, value, first):
         part[term] = jnp.where(first, jnp.float32(0.0), part[term]) + value
@@ -171,7 +168,7 @@
     row_products(place, weights, env_high, LOW, plain, turned, combine)
 
 
-def late_kernel(tick, place, weights, stay, low, part, incoming, plain, turned,
+def late_kernel(tick, place, weights, rest, low, part, incoming, plain, turned,
                 out_low, out_a, out_b, env_low, *scratch):
     @pl.when(place[0] == 0)
     def _():
@@ -179,7 +176,7 @@
 
     @pl.when(place[0] != 0)
     def _():
-        env_low[...] = stay[...] + low[...]
+        env_low[...] = rest[:, :LOW] + low[...]
 
     def combine(term, value, first):
         row = 0
@@ -192,40 +189,55 @@
     row_products(place, weights, env_low, 0, plain, turned, combine)
 
 
+def in_order(*refs):
+    pairs, row = [], 0
+    for ref in refs:
+        pairs.append((row, ref))
+        row += ref.shape[1]
+    return pairs
+
+
+def outer_rows(middle, rest):
+    rows = middle.shape[1]
+    return [(rows, middle), (0, rest.at[:, :rows]), (2 * rows, rest.at[:, rows:])]
+
+
 def first_kernel(place, weights, env, states, out_low, out_a, out_b, plain, turned,
                  *scratch):
     def ready(state):
         fill(state, place, plain.shape[0], states, plain, turned)
 
-    products(2, place, weights, [env], plain, turned, [out_low, out_a, out_b], scratch,
+    products(2, place, weights, [env], plain, turned, in_order(out_low, out_a, out_b), scratch,
              ready)
 
 
 def first_one_kernel(place, weights, env, states, plain_in, turned_in,
-                     out_low, out_high, plain, turned, *scratch):
+                     out_low, out_a, out_b, plain, turned, *scratch):
     def ready(state):
         fill(state, place, plain.shape[0], states, plain, turned)
 
-    products(1, place, weights, [env], plain, turned, [out_low, out_high], scratch, ready)
+    products(1, place, weights, [env], plain, turned, in_order(out_low, out_a, out_b), scratch, ready)
 
 
 def first_zero_kernel(place, weights, env, states, plain_in, turned_in,
-                      out_low, out_high, plain, turned, *scratch):
+                      middle, rest, plain, turned, *scratch):
     def ready(state):
         fill(state, place, plain.shape[0], states, plain, turned)
 
-    looped(0, place, weights, [env], plain, turned, [out_low, out_high], ready)
-
-
-def one_kernel(place, weights, env_low, env_high, plain, turned, out_low, out_high, *scratch):
-    products(1, place, weights, [env_low, env_high], plain, turned, [out_low, out_high], scratch)
-
-
-def zero_kernel(place, weights, env_low, env_high, plain, turned, out_low, out_high, *scratch):
-    looped(0, place, weights, [env_low, env_high], plain, turned, [out_low, out_high])
-
-
-def final_kernel(tick, place, stay_low, stay_high, high, far_a, far_b, low, incoming, env,
+    looped(0, place, weights, [env], plain, turned, outer_rows(middle, rest), ready)
+
+
+def one_kernel(place, weights, env_low, env_high, plain, turned, out_low, out_a, out_b,
+               *scratch):
+    products(1, place, weights, [env_low, env_high], plain, turned,
+             in_order(out_low, out_a, out_b), scratch)
+
+
+def zero_kernel(place, weights, env_low, env_high, plain, turned, middle, rest, *scratch):
+    looped(0, place, weights, [env_low, env_high], plain, turned, outer_rows(middle, rest))
+
+
+def final_kernel(tick, place, rest, kept, high, far_a, far_b, low, incoming, env,
                  *scratch):
     @pl.when(place[0] == 0)
     def _():
@@ -234,9 +246,9 @@
     @pl.when(place[0] != 0)
     def _():
         half = far_a.shape[1]
-        env[:, :LOW] = stay_low[...] + low[...]
-        env[:, LOW : LOW + half] = stay_high[:, :half] + high[:, :half] + far_a[...]
-        env[:, LOW + half :] = stay_high[:, half:] + high[:, half:] + far_b[...]
+        env[:, :LOW] = rest[:, :LOW] + low[...]
+        env[:, LOW : LOW + half] = kept[...] + far_a[...]
+        env[:, LOW + half :] = rest[:, LOW:] + high[...] + far_b[...]
 
 
 def shape(*dims):
@@ -311,7 +323,7 @@
         else:
             two_low, far_a, far_b, env_low = call(
                 functools.partial(late_kernel, tick - 1),
-                scalars + (kept_low, low, part, incoming, plain, turned),
+                scalars + (rest, low, part, incoming, plain, turned),
                 thirds + [parts[0]],
                 rows=LOW,
             )
@@ -319,43 +331,44 @@
         two_low = lax.ppermute(two_low, AXES, relay)
         far_b = lax.ppermute(far_b, AXES, far_one)
         if tick == 0:
-            one_low, one_high, plain, turned = call(
+            one_low, one_mid, one_high, plain, turned = call(
                 first_one_kernel,
                 scalars + (env, states, plain, turned),
-                parts + split_states,
-                {4: 2, 5: 3},
+                thirds + split_states,
+                {4: 3, 5: 4},
             )
         else:
-            one_low, one_high = call(
-                one_kernel, scalars + (env_low, env_high, plain, turned), parts
-            )
+            one_low, one_mid, one_high = call(
+                one_kernel, scalars + (env_low, env_high, plain, turned), thirds
+            )
+        one_mid = lax.ppermute(one_mid, AXES, relay)
         high = lax.ppermute(one_high, AXES, lift)
         if tick == 0:
-            zero_low, zero_high, plain, turned = call(
+            zero_mid, zero_rest, plain, turned = call(
                 first_zero_kernel,
                 scalars + (env, states, plain, turned),
                 parts + split_states,
                 {4: 2, 5: 3},
             )
         else:
-            zero_low, zero_high = call(
+            zero_mid, zero_rest = call(
                 zero_kernel, scalars + (env_low, env_high, plain, turned), parts
             )
-        kept_high = lax.ppermute(zero_high, AXES, stay)
-        kept_low = lax.ppermute(zero_low, AXES, stay)
+        rest = lax.ppermute(zero_rest, AXES, stay)
+        kept = lax.ppermute(zero_mid + one_mid, AXES, stay)
         low = lax.ppermute(one_low + two_low, AXES, lift)
         far_a = lax.ppermute(far_a, AXES, far_two)
         far_b = lax.ppermute(far_b, AXES, far_two)
         if tick < TICKS - 1:
             env_high, part = call(
                 functools.partial(early_kernel, tick),
-                scalars + (kept_high, high, far_a, far_b, incoming, plain, turned),
+                scalars + (rest, kept, high, far_a, far_b, incoming, plain, turned),
                 [parts[1], whole],
                 rows=block - LOW,
             )
     (env,) = call(
         functools.partial(final_kernel, TICKS - 1),
-        (place, kept_low, kept_high, high, far_a, far_b, low, incoming),
+        (place, rest, kept, high, far_a, far_b, low, incoming),
         [whole],
     )
     return env[None, :, None]

time: 349 us -> 326 us (0.934)
  the two profiles are of different devices: /device:TPU:1 before, /device:TPU:16 now
where the time goes in v4:
time: 326 us; the launch traced here: 325 us
  waiting for transfers between devices  130 us (40%)
  starting transfers between devices  115 us (35%)
  Pallas kernels  72.5 us (22%)
  local copies, waits for them, and re-layouts  4.99 us (2%)
    pallas_call x16, Pallas kernels, call(): pl.pallas_call(kernel, in_specs=specs, out_specs=[VMEM] * len(outputs), o...  72.5 us
    ppermute x4, waiting for transfers between devices, local(): high = lax.ppermute(one_high, AXES, lift)  43.7 us
    ppermute x4, waiting for transfers between devices, local(): low = lax.ppermute(one_low + two_low, AXES, lift)  37.6 us
    ppermute x4, starting transfers between devices, local(): far_a = lax.ppermute(far_a, AXES, far_two)  26.9 us
    ppermute x4, waiting for transfers between devices, local(): far_b = lax.ppermute(far_b, AXES, far_one)  23.9 us
    ppermute x4, starting transfers between devices, local(): one_mid = lax.ppermute(one_mid, AXES, relay)  19.8 us
    ppermute x4, starting transfers between devices, local(): far_b = lax.ppermute(far_b, AXES, far_two)  19 us
    ppermute x4, waiting for transfers between devices, local(): kept = lax.ppermute(zero_mid + one_mid, AXES, stay)  14.3 us
  transfers between devices with their start and end apart: 40, of which 17 were waited for; matrix products, arithmetic and copies ran while one was open for 0% of the time, Pallas kernels for 16%

profile of v4, /device:TPU:16, one launch (start us, length us, event | category | flops | bytes accessed | tf_op | source)
XLA Modules:
  0.0 324.8 jit_solution(18310236643235279958)
XLA Ops:
  5.6 4.1 %shard_map.73 = (f32[3,128,384]{2,1,0:T(8,128)S(1)}, f32[3,128,384]{2,1,0:T(8,128)S(1)}, f32[3,128,384]{2,1,0:T(8,128)S(1)}, bf16[4,1152,384]{2,1,0:T(8,128)(2,1)S(1)}, bf16[4,384,1152]{2,1,0:T(8,128)(2,1)S(1)}) custom-call(s32[23]{0:T(128)S(1)} %concatenate.3.place, f32[576]{0:T(1024)S(1)} %reshape.3.weights, f32[3,384,384]{2,1,0:T(8,128)S(1)} %bitcast.8, ...), custom_call_target="tpu_custom_call" | custom-call | flops 2038431744 | bytes 7077888 | tf_op jit(solution)/shard_map/pallas_call | solution.py:306
  13.0 7.5 %shard_map.74 = (f32[3,128,384]{2,1,0:T(8,128)S(1)}, f32[3,128,384]{2,1,0:T(8,128)S(1)}, f32[3,128,384]{2,1,0:T(8,128)S(1)}, bf16[4,1152,384]{2,1,0:T(8,128)(2,1)S(1)}, bf16[4,384,1152]{2,1,0:T(8,128)(2,1)S(1)}) custom-call(s32[23]{0:T(128)S(1)} %concatenate.3.place, f32[576]{0:T(1024)S(1)} %reshape.3.weights, ...), custom_call_target="tpu_custom_call", output_to_operand_aliasing={{3}: (4, {}), {4}: (5, {})} | custom-call | flops 2038431744 | bytes 7077888 | tf_op jit(solution)/shard_map/pallas_call | solution.py:306
  21.3 4.8 %shard_map.75 = (f32[3,128,384]{2,1,0:T(8,128)S(1)}, f32[3,256,384]{2,1,0:T(8,128)S(1)}, bf16[4,1152,384]{2,1,0:T(8,128)(2,1)S(1)}, bf16[4,384,1152]{2,1,0:T(8,128)(2,1)S(1)}) custom-call(s32[23]{0:T(128)S(1)} %concatenate.3.place, f32[576]{0:T(1024)S(1)} %reshape.3.weights, ...), custom_call_target="tpu_custom_call", output_to_operand_aliasing={{2}: (4, {}), {3}: (5, {})} | custom-call | flops 2038431744 | bytes 7077888 | tf_op jit(solution)/shard_map/pallas_call | solution.py:306
  29.4 10.5 %collective-permute-done.8 = f32[3,128,384]{2,1,0:T(8,128)S(1)} collective-permute-done((f32[3,128,384]{2,1,0:T(8,128)S(1)}, f32[3,128,384]{2,1,0:T(8,128)S(1)}, u32[]{:S(2)}, u32[]{:S(2)}) %collective-permute-start.8) | collective-permute-done | bytes 589856 | tf_op jit(solution)/shard_map/ppermute | solution.py:332
  39.9 5.8 %collective-permute-start.7 = (f32[3,128,384]{2,1,0:T(8,128)S(1)}, f32[3,128,384]{2,1,0:T(8,128)S(1)}, u32[]{:S(2)}, u32[]{:S(2)}) collective-permute-start(f32[3,128,384]{2,1,0:T(8,128)S(1)} %collective-permute-done.6), channel_id=1, source_target_pairs={{19,18},{16,19},{21,20},{22,21},{23,22},{20,23},{25,24},{26,25},{2... | collective-permute-start | bytes 1769480 | tf_op jit(solution)/shard_map/ppermute | solution.py:360
  45.8 4.4 %collective-permute-start.9 = (f32[3,128,384]{2,1,0:T(8,128)S(1)}, f32[3,128,384]{2,1,0:T(8,128)S(1)}, u32[]{:S(2)}, u32[]{:S(2)}) collective-permute-start(f32[3,128,384]{2,1,0:T(8,128)S(1)} %collective-permute-done.8), channel_id=1, source_target_pairs={{19,18},{16,19},{21,20},{22,21},{23,22},{20,23},{25,24},{26,25},{2... | collective-permute-start | bytes 1769480 | tf_op jit(solution)/shard_map/ppermute | solution.py:361
  51.6 4.5 %collective-permute-done.5.high = f32[3,128,384]{2,1,0:T(8,128)S(1)} collective-permute-done((f32[3,128,384]{2,1,0:T(8,128)S(1)}, f32[3,128,384]{2,1,0:T(8,128)S(1)}, u32[]{:S(2)}, u32[]{:S(2)}) %collective-permute-start.5) | collective-permute-done | bytes 589856 | tf_op jit(solution)/shard_map/ppermute | solution.py:345
  57.4 2.6 collective-permute-done.9.far_b
  60.0 11.1 %collective-permute-done.4.kept = f32[3,128,384]{2,1,0:T(8,128)S(1)} collective-permute-done((f32[3,128,384]{2,1,0:T(8,128)S(1)}, f32[3,128,384]{2,1,0:T(8,128)S(1)}, u32[]{:S(2)}, u32[]{:S(2)}) %collective-permute-start.4) | collective-permute-done | bytes 589856 | tf_op jit(solution)/shard_map/ppermute | solution.py:358
  71.2 3.6 %shard_map.76 = (f32[3,256,384]{2,1,0:T(8,128)S(1)}, f32[3,384,384]{2,1,0:T(8,128)S(1)}) custom-call(s32[23]{0:T(128)S(1)} %concatenate.3.place, f32[576]{0:T(1024)S(1)} %reshape.3.weights, f32[3,256,384]{2,1,0:T(8,128)S(1)} %collective-permute-done.rest, f32[3,128,384]{2,1,0:T(8,128)S(1)} %collective-permute-done.4.kept, ...), custom_call_target="tpu_custom_call" | custom-call | flops 2038431744 | bytes 7077888 | tf_op jit(solution)/shard_map/pallas_call | solution.py:306
  74.8 2.7 shard_map.77
  77.6 1.9 collective-permute-start.16
  79.5 2.1 collective-permute-start.18
  81.6 7.1 %shard_map.79 = (f32[3,128,384]{2,1,0:T(8,128)S(1)}, f32[3,128,384]{2,1,0:T(8,128)S(1)}, f32[3,128,384]{2,1,0:T(8,128)S(1)}) custom-call(s32[23]{0:T(128)S(1)} %concatenate.3.place, f32[576]{0:T(1024)S(1)} %reshape.3.weights, f32[3,128,384]{2,1,0:T(8,128)S(1)} %get-tuple-element.67.env_low, f32[3,256,384]{2,1,0:T(8,128)S(1)} %get-tuple-element.68.env_high, ...), custom_call_target="tpu_custom_call" | custom-call | flops 2038431744 | bytes 7077888 | tf_op jit(solution)/shard_map/pallas_call | solution.py:306
  88.8 5.6 %collective-permute-start.13 = (f32[3,128,384]{2,1,0:T(8,128)S(1)}, f32[3,128,384]{2,1,0:T(8,128)S(1)}, u32[]{:S(2)}, u32[]{:S(2)}) collective-permute-start(f32[3,128,384]{2,1,0:T(8,128)S(1)} %get-tuple-element.73), channel_id=1, source_target_pairs={{0,1},{1,2},{2,3},{3,4},{4,5},{5,6},{6,7},{7,8},{8,9},{9,10},{10,1... | collective-permute-start | bytes 1769480 | tf_op jit(solution)/shard_map/ppermute | solution.py:344
  94.4 4.5 %shard_map.78 = (f32[3,128,384]{2,1,0:T(8,128)S(1)}, f32[3,256,384]{2,1,0:T(8,128)S(1)}) custom-call(s32[23]{0:T(128)S(1)} %concatenate.3.place, f32[576]{0:T(1024)S(1)} %reshape.3.weights, f32[3,128,384]{2,1,0:T(8,128)S(1)} %get-tuple-element.67.env_low, f32[3,256,384]{2,1,0:T(8,128)S(1)} %get-tuple-element.68.env_high, ...), custom_call_target="tpu_custom_call" | custom-call | flops 2038431744 | bytes 7077888 | tf_op jit(solution)/shard_map/pallas_call | solution.py:306
  98.9 2.3 collective-permute-start.11
  101.2 1.9 collective-permute-start.10
  103.2 1.9 collective-permute-start.15
  105.1 2.7 collective-permute-done.18
  107.8 4.4 %collective-permute-start.17 = (f32[3,128,384]{2,1,0:T(8,128)S(1)}, f32[3,128,384]{2,1,0:T(8,128)S(1)}, u32[]{:S(2)}, u32[]{:S(2)}) collective-permute-start(f32[3,128,384]{2,1,0:T(8,128)S(1)} %collective-permute-done.16), channel_id=1, source_target_pairs={{19,18},{16,19},{21,20},{22,21},{23,22},{20,23},{25,24},{26,25},{2... | collective-permute-start | bytes 1769480 | tf_op jit(solution)/shard_map/ppermute | solution.py:360
  112.2 6.6 %collective-permute-start.19 = (f32[3,128,384]{2,1,0:T(8,128)S(1)}, f32[3,128,384]{2,1,0:T(8,128)S(1)}, u32[]{:S(2)}, u32[]{:S(2)}) collective-permute-start(f32[3,128,384]{2,1,0:T(8,128)S(1)} %collective-permute-done.18), channel_id=1, source_target_pairs={{19,18},{16,19},{21,20},{22,21},{23,22},{20,23},{25,24},{26,25},{2... | collective-permute-start | bytes 1769480 | tf_op jit(solution)/shard_map/ppermute | solution.py:361
  118.9 1.9 collective-permute-start.14
  120.9 14.7 %collective-permute-done.15.high = f32[3,128,384]{2,1,0:T(8,128)S(1)} collective-permute-done((f32[3,128,384]{2,1,0:T(8,128)S(1)}, f32[3,128,384]{2,1,0:T(8,128)S(1)}, u32[]{:S(2)}, u32[]{:S(2)}) %collective-permute-start.15) | collective-permute-done | bytes 589856 | tf_op jit(solution)/shard_map/ppermute | solution.py:345
  135.7 1.9 collective-permute-start.12
  137.6 3.6 %shard_map.80 = (f32[3,256,384]{2,1,0:T(8,128)S(1)}, f32[3,384,384]{2,1,0:T(8,128)S(1)}) custom-call(s32[23]{0:T(128)S(1)} %concatenate.3.place, f32[576]{0:T(1024)S(1)} %reshape.3.weights, f32[3,256,384]{2,1,0:T(8,128)S(1)} %collective-permute-done.10.rest, f32[3,128,384]{2,1,0:T(8,128)S(1)} %collective-permute-done.14.kept, ...), custom_call_target="tpu_custom_call" | custom-call | flops 2038431744 | bytes 7077888 | tf_op jit(solution)/shard_map/pallas_call | solution.py:306
  141.2 12.3 %collective-permute-done.12.low = f32[3,128,384]{2,1,0:T(8,128)S(1)} collective-permute-done((f32[3,128,384]{2,1,0:T(8,128)S(1)}, f32[3,128,384]{2,1,0:T(8,128)S(1)}, u32[]{:S(2)}, u32[]{:S(2)}) %collective-permute-start.12) | collective-permute-done | bytes 589856 | tf_op jit(solution)/shard_map/ppermute | solution.py:359
  153.5 2.7 shard_map.81
  156.2 1.9 collective-permute-start.26
  158.2 1.9 collective-permute-start.28
  160.1 7.1 %shard_map.83 = (f32[3,128,384]{2,1,0:T(8,128)S(1)}, f32[3,128,384]{2,1,0:T(8,128)S(1)}, f32[3,128,384]{2,1,0:T(8,128)S(1)}) custom-call(s32[23]{0:T(128)S(1)} %concatenate.3.place, f32[576]{0:T(1024)S(1)} %reshape.3.weights, f32[3,128,384]{2,1,0:T(8,128)S(1)} %get-tuple-element.78.env_low, f32[3,256,384]{2,1,0:T(8,128)S(1)} %get-tuple-element.79.env_high, ...), custom_call_target="tpu_custom_call" | custom-call | flops 2038431744 | bytes 7077888 | tf_op jit(solution)/shard_map/pallas_call | solution.py:306
  167.2 7.3 %collective-permute-start.23 = (f32[3,128,384]{2,1,0:T(8,128)S(1)}, f32[3,128,384]{2,1,0:T(8,128)S(1)}, u32[]{:S(2)}, u32[]{:S(2)}) collective-permute-start(f32[3,128,384]{2,1,0:T(8,128)S(1)} %get-tuple-element.84), channel_id=1, source_target_pairs={{0,1},{1,2},{2,3},{3,4},{4,5},{5,6},{6,7},{7,8},{8,9},{9,10},{10,1... | collective-permute-start | bytes 1769480 | tf_op jit(solution)/shard_map/ppermute | solution.py:344
  174.6 4.5 %shard_map.82 = (f32[3,128,384]{2,1,0:T(8,128)S(1)}, f32[3,256,384]{2,1,0:T(8,128)S(1)}) custom-call(s32[23]{0:T(128)S(1)} %concatenate.3.place, f32[576]{0:T(1024)S(1)} %reshape.3.weights, f32[3,128,384]{2,1,0:T(8,128)S(1)} %get-tuple-element.78.env_low, f32[3,256,384]{2,1,0:T(8,128)S(1)} %get-tuple-element.79.env_high, ...), custom_call_target="tpu_custom_call" | custom-call | flops 2038431744 | bytes 7077888 | tf_op jit(solution)/shard_map/pallas_call | solution.py:306
  179.1 1.9 collective-permute-start.21
  181.1 1.9 collective-permute-start.20
  183.0 1.9 collective-permute-start.25
  184.9 2.2 collective-permute-done.28
  187.1 7.3 %collective-permute-start.27 = (f32[3,128,384]{2,1,0:T(8,128)S(1)}, f32[3,128,384]{2,1,0:T(8,128)S(1)}, u32[]{:S(2)}, u32[]{:S(2)}) collective-permute-start(f32[3,128,384]{2,1,0:T(8,128)S(1)} %collective-permute-done.26), channel_id=1, source_target_pairs={{19,18},{16,19},{21,20},{22,21},{23,22},{20,23},{25,24},{26,25},{2... | collective-permute-start | bytes 1769480 | tf_op jit(solution)/shard_map/ppermute | solution.py:360
  194.5 1.9 collective-permute-start.29
  196.5 4.3 %collective-permute-done.21 = f32[3,128,384]{2,1,0:T(8,128)S(1)} collective-permute-done((f32[3,128,384]{2,1,0:T(8,128)S(1)}, f32[3,128,384]{2,1,0:T(8,128)S(1)}, u32[]{:S(2)}, u32[]{:S(2)}) %collective-permute-start.21) | collective-permute-done | bytes 589856 | tf_op jit(solution)/shard_map/ppermute | solution.py:331
  200.8 1.9 collective-permute-start.24
  202.8 14.9 %collective-permute-done.25.high = f32[3,128,384]{2,1,0:T(8,128)S(1)} collective-permute-done((f32[3,128,384]{2,1,0:T(8,128)S(1)}, f32[3,128,384]{2,1,0:T(8,128)S(1)}, u32[]{:S(2)}, u32[]{:S(2)}) %collective-permute-start.25) | collective-permute-done | bytes 589856 | tf_op jit(solution)/shard_map/ppermute | solution.py:345
  217.8 1.9 collective-permute-start.22
  219.7 3.9 %shard_map.84 = (f32[3,256,384]{2,1,0:T(8,128)S(1)}, f32[3,384,384]{2,1,0:T(8,128)S(1)}) custom-call(s32[23]{0:T(128)S(1)} %concatenate.3.place, f32[576]{0:T(1024)S(1)} %reshape.3.weights, f32[3,256,384]{2,1,0:T(8,128)S(1)} %collective-permute-done.20.rest, f32[3,128,384]{2,1,0:T(8,128)S(1)} %collective-permute-done.24.kept, ...), custom_call_target="tpu_custom_call" | custom-call | flops 2038431744 | bytes 7077888 | tf_op jit(solution)/shard_map/pallas_call | solution.py:306
  223.6 11.3 %collective-permute-done.22.low = f32[3,128,384]{2,1,0:T(8,128)S(1)} collective-permute-done((f32[3,128,384]{2,1,0:T(8,128)S(1)}, f32[3,128,384]{2,1,0:T(8,128)S(1)}, u32[]{:S(2)}, u32[]{:S(2)}) %collective-permute-start.22) | collective-permute-done | bytes 589856 | tf_op jit(solution)/shard_map/ppermute | solution.py:359
  234.8 2.7 shard_map.85
  237.6 7.1 %shard_map.87 = (f32[3,128,384]{2,1,0:T(8,128)S(1)}, f32[3,128,384]{2,1,0:T(8,128)S(1)}, f32[3,128,384]{2,1,0:T(8,128)S(1)}) custom-call(s32[23]{0:T(128)S(1)} %concatenate.3.place, f32[576]{0:T(1024)S(1)} %reshape.3.weights, f32[3,128,384]{2,1,0:T(8,128)S(1)} %get-tuple-element.89.env_low, f32[3,256,384]{2,1,0:T(8,128)S(1)} %get-tuple-element.90.env_high, ...), custom_call_target="tpu_custom_call" | custom-call | flops 2038431744 | bytes 7077888 | tf_op jit(solution)/shard_map/pallas_call | solution.py:306
  244.7 6.2 %collective-permute-start.31 = (f32[3,128,384]{2,1,0:T(8,128)S(1)}, f32[3,128,384]{2,1,0:T(8,128)S(1)}, u32[]{:S(2)}, u32[]{:S(2)}) collective-permute-start(f32[3,128,384]{2,1,0:T(8,128)S(1)} %get-tuple-element.93), channel_id=1, source_target_pairs={{0,1},{1,2},{2,3},{3,4},{4,5},{5,6},{6,7},{7,8},{8,9},{9,10},{10,1... | collective-permute-start | bytes 1769480 | tf_op jit(solution)/shard_map/ppermute | solution.py:344
  250.9 1.9 collective-permute-start.34
  252.8 1.9 collective-permute-start.36
  254.7 1.9 collective-permute-start.38
  256.7 4.5 %shard_map.86 = (f32[3,128,384]{2,1,0:T(8,128)S(1)}, f32[3,256,384]{2,1,0:T(8,128)S(1)}) custom-call(s32[23]{0:T(128)S(1)} %concatenate.3.place, f32[576]{0:T(1024)S(1)} %reshape.3.weights, f32[3,128,384]{2,1,0:T(8,128)S(1)} %get-tuple-element.89.env_low, f32[3,256,384]{2,1,0:T(8,128)S(1)} %get-tuple-element.90.env_high, ...), custom_call_target="tpu_custom_call" | custom-call | flops 2038431744 | bytes 7077888 | tf_op jit(solution)/shard_map/pallas_call | solution.py:306
  261.2 1.9 collective-permute-start.33
  263.1 3.0 collective-permute-done.31
  266.1 1.9 collective-permute-start.30
  268.1 1.9 collective-permute-start.32
  270.1 8.5 %collective-permute-done.36 = f32[3,128,384]{2,1,0:T(8,128)S(1)} collective-permute-done((f32[3,128,384]{2,1,0:T(8,128)S(1)}, f32[3,128,384]{2,1,0:T(8,128)S(1)}, u32[]{:S(2)}, u32[]{:S(2)}) %collective-permute-start.36) | collective-permute-done | bytes 589856 | tf_op jit(solution)/shard_map/ppermute | solution.py:332
  278.6 9.3 %collective-permute-start.35 = (f32[3,128,384]{2,1,0:T(8,128)S(1)}, f32[3,128,384]{2,1,0:T(8,128)S(1)}, u32[]{:S(2)}, u32[]{:S(2)}) collective-permute-start(f32[3,128,384]{2,1,0:T(8,128)S(1)} %collective-permute-done.34), channel_id=1, source_target_pairs={{19,18},{16,19},{21,20},{22,21},{23,22},{20,23},{25,24},{26,25},{2... | collective-permute-start | bytes 1769480 | tf_op jit(solution)/shard_map/ppermute | solution.py:360
  287.9 6.0 %collective-permute-start.37 = (f32[3,128,384]{2,1,0:T(8,128)S(1)}, f32[3,128,384]{2,1,0:T(8,128)S(1)}, u32[]{:S(2)}, u32[]{:S(2)}) collective-permute-start(f32[3,128,384]{2,1,0:T(8,128)S(1)} %collective-permute-done.36), channel_id=1, source_target_pairs={{19,18},{16,19},{21,20},{22,21},{23,22},{20,23},{25,24},{26,25},{2... | collective-permute-start | bytes 1769480 | tf_op jit(solution)/shard_map/ppermute | solution.py:361
  294.0 9.5 %collective-permute-done.33.high = f32[3,128,384]{2,1,0:T(8,128)S(1)} collective-permute-done((f32[3,128,384]{2,1,0:T(8,128)S(1)}, f32[3,128,384]{2,1,0:T(8,128)S(1)}, u32[]{:S(2)}, u32[]{:S(2)}) %collective-permute-start.33) | collective-permute-done | bytes 589856 | tf_op jit(solution)/shard_map/ppermute | solution.py:345
  303.6 1.9 collective-permute-start.39
  305.5 3.2 collective-permute-done.32.kept
  308.7 14.1 %collective-permute-done.39.low = f32[3,128,384]{2,1,0:T(8,128)S(1)} collective-permute-done((f32[3,128,384]{2,1,0:T(8,128)S(1)}, f32[3,128,384]{2,1,0:T(8,128)S(1)}, u32[]{:S(2)}, u32[]{:S(2)}) %collective-permute-start.39) | collective-permute-done | bytes 589856 | tf_op jit(solution)/shard_map/ppermute | solution.py:359
  322.8 2.0 shard_map.88
  (52 shorter events, 15.5 us)
Async XLA Ops:
  2.5 1.7 copy-start
  4.2 1.5 copy-start.1
  9.7 18.4 %collective-permute-start.6 = (f32[3,128,384]{2,1,0:T(8,128)S(1)}, f32[3,128,384]{2,1,0:T(8,128)S(1)}, u32[]{:S(2)}, u32[]{:S(2)}) collective-permute-start(f32[3,128,384]{2,1,0:T(8,128)S(1)} %get-tuple-element.62), channel_id=1, source_target_pairs={{0,19},{1,16},{2,21},{3,22},{4,23},{5,20},{6,25},{7,26},{8,27},{9,... | collective-permute-start | bytes 1769480 | tf_op jit(solution)/shard_map/ppermute | solution.py:330
  11.0 39.2 %collective-permute-start.1 = (f32[3,128,384]{2,1,0:T(8,128)S(1)}, f32[3,128,384]{2,1,0:T(8,128)S(1)}, u32[]{:S(2)}, u32[]{:S(2)}) collective-permute-start(f32[3,128,384]{2,1,0:T(8,128)S(1)} %get-tuple-element.58), channel_id=1, source_target_pairs={{0,1},{1,2},{2,3},{3,4},{4,5},{5,6},{6,7},{7,8},{8,9},{9,10},{10,1... | collective-permute-start | bytes 1769480 | tf_op jit(solution)/shard_map/ppermute | solution.py:331
  11.7 28.2 %collective-permute-start.8 = (f32[3,128,384]{2,1,0:T(8,128)S(1)}, f32[3,128,384]{2,1,0:T(8,128)S(1)}, u32[]{:S(2)}, u32[]{:S(2)}) collective-permute-start(f32[3,128,384]{2,1,0:T(8,128)S(1)} %get-tuple-element.63), channel_id=1, source_target_pairs={{0,19},{1,16},{2,21},{3,22},{4,23},{5,20},{6,25},{7,26},{8,27},{9,... | collective-permute-start | bytes 1769480 | tf_op jit(solution)/shard_map/ppermute | solution.py:332
  20.5 25.2 %collective-permute-start.3 = (f32[3,128,384]{2,1,0:T(8,128)S(1)}, f32[3,128,384]{2,1,0:T(8,128)S(1)}, u32[]{:S(2)}, u32[]{:S(2)}) collective-permute-start(f32[3,128,384]{2,1,0:T(8,128)S(1)} %get-tuple-element.60), channel_id=1, source_target_pairs={{0,1},{1,2},{2,3},{3,4},{4,5},{5,6},{6,7},{7,8},{8,9},{9,10},{10,1... | collective-permute-start | bytes 1769480 | tf_op jit(solution)/shard_map/ppermute | solution.py:344
  21.2 49.9 %slice-start = ((s8[7077888]{0:T(1024)(128)(4,1)}), s8[4194304]{0:T(1024)(128)(4,1)S(1)}, s32[]{:S(2)}) async-start(s8[7077888]{0:T(1024)(128)(4,1)} %bitcast.6), calls=%async_computation | async-start | bytes 8388608
  21.3 49.9 %slice-start.1 = ((s8[7077888]{0:T(1024)(128)(4,1)}), s8[2883584]{0:T(1024)(128)(4,1)S(1)}, s32[]{:S(2)}) async-start(s8[7077888]{0:T(1024)(128)(4,1)} %bitcast.6), calls=%async_computation.1 | async-start | bytes 5767168
  26.0 45.1 %collective-permute-start = (f32[3,256,384]{2,1,0:T(8,128)S(1)}, f32[3,256,384]{2,1,0:T(8,128)S(1)}, u32[]{:S(2)}, u32[]{:S(2)}) collective-permute-start(f32[3,256,384]{2,1,0:T(8,128)S(1)} %get-tuple-element.56), channel_id=1, source_target_pairs={{0,16},{1,17},{2,18},{3,19},{4,20},{5,21},{6,22},{7,23},{8,24},{9,... | collective-permute-start | bytes 3538952 | tf_op jit(solution)/shard_map/ppermute | solution.py:357
  28.1 28.0 %collective-permute-start.5 = (f32[3,128,384]{2,1,0:T(8,128)S(1)}, f32[3,128,384]{2,1,0:T(8,128)S(1)}, u32[]{:S(2)}, u32[]{:S(2)}) collective-permute-start(f32[3,128,384]{2,1,0:T(8,128)S(1)} %get-tuple-element.61), channel_id=1, source_target_pairs={{0,17},{1,18},{2,19},{3,20},{4,21},{5,22},{6,23},{7,24},{8,25},{9,... | collective-permute-start | bytes 1769480 | tf_op jit(solution)/shard_map/ppermute | solution.py:345
  39.9 17.5 %collective-permute-start.7 = (f32[3,128,384]{2,1,0:T(8,128)S(1)}, f32[3,128,384]{2,1,0:T(8,128)S(1)}, u32[]{:S(2)}, u32[]{:S(2)}) collective-permute-start(f32[3,128,384]{2,1,0:T(8,128)S(1)} %collective-permute-done.6), channel_id=1, source_target_pairs={{19,18},{16,19},{21,20},{22,21},{23,22},{20,23},{25,24},{26,25},{2... | collective-permute-start | bytes 1769480 | tf_op jit(solution)/shard_map/ppermute | solution.py:360
  45.8 14.3 %collective-permute-start.9 = (f32[3,128,384]{2,1,0:T(8,128)S(1)}, f32[3,128,384]{2,1,0:T(8,128)S(1)}, u32[]{:S(2)}, u32[]{:S(2)}) collective-permute-start(f32[3,128,384]{2,1,0:T(8,128)S(1)} %collective-permute-done.8), channel_id=1, source_target_pairs={{19,18},{16,19},{21,20},{22,21},{23,22},{20,23},{25,24},{26,25},{2... | collective-permute-start | bytes 1769480 | tf_op jit(solution)/shard_map/ppermute | solution.py:361
  50.3 20.9 %collective-permute-start.4 = (f32[3,128,384]{2,1,0:T(8,128)S(1)}, f32[3,128,384]{2,1,0:T(8,128)S(1)}, u32[]{:S(2)}, u32[]{:S(2)}) collective-permute-start(f32[3,128,384]{2,1,0:T(8,128)S(1)} %add.25), channel_id=1, source_target_pairs={{0,16},{1,17},{2,18},{3,19},{4,20},{5,21},{6,22},{7,23},{8,24},{9,... | collective-permute-start | bytes 1769480 | tf_op jit(solution)/shard_map/ppermute | solution.py:358
  56.1 18.7 %collective-permute-start.2 = (f32[3,128,384]{2,1,0:T(8,128)S(1)}, f32[3,128,384]{2,1,0:T(8,128)S(1)}, u32[]{:S(2)}, u32[]{:S(2)}) collective-permute-start(f32[3,128,384]{2,1,0:T(8,128)S(1)} %add.24), channel_id=1, source_target_pairs={{0,17},{1,18},{2,19},{3,20},{4,21},{5,22},{6,23},{7,24},{8,25},{9,... | collective-permute-start | bytes 1769480 | tf_op jit(solution)/shard_map/ppermute | solution.py:359
  77.6 25.6 %collective-permute-start.16 = (f32[3,128,384]{2,1,0:T(8,128)S(1)}, f32[3,128,384]{2,1,0:T(8,128)S(1)}, u32[]{:S(2)}, u32[]{:S(2)}) collective-permute-start(f32[3,128,384]{2,1,0:T(8,128)S(1)} %get-tuple-element.75), channel_id=1, source_target_pairs={{0,19},{1,16},{2,21},{3,22},{4,23},{5,20},{6,25},{7,26},{8,27},{9,... | collective-permute-start | bytes 1769480 | tf_op jit(solution)/shard_map/ppermute | solution.py:330
  79.5 28.3 %collective-permute-start.18 = (f32[3,128,384]{2,1,0:T(8,128)S(1)}, f32[3,128,384]{2,1,0:T(8,128)S(1)}, u32[]{:S(2)}, u32[]{:S(2)}) collective-permute-start(f32[3,128,384]{2,1,0:T(8,128)S(1)} %get-tuple-element.76), channel_id=1, source_target_pairs={{0,19},{1,16},{2,21},{3,22},{4,23},{5,20},{6,25},{7,26},{8,27},{9,... | collective-permute-start | bytes 1769480 | tf_op jit(solution)/shard_map/ppermute | solution.py:332
  88.8 23.4 %collective-permute-start.13 = (f32[3,128,384]{2,1,0:T(8,128)S(1)}, f32[3,128,384]{2,1,0:T(8,128)S(1)}, u32[]{:S(2)}, u32[]{:S(2)}) collective-permute-start(f32[3,128,384]{2,1,0:T(8,128)S(1)} %get-tuple-element.73), channel_id=1, source_target_pairs={{0,1},{1,2},{2,3},{3,4},{4,5},{5,6},{6,7},{7,8},{8,9},{9,10},{10,1... | collective-permute-start | bytes 1769480 | tf_op jit(solution)/shard_map/ppermute | solution.py:344
  98.9 20.0 %collective-permute-start.11 = (f32[3,128,384]{2,1,0:T(8,128)S(1)}, f32[3,128,384]{2,1,0:T(8,128)S(1)}, u32[]{:S(2)}, u32[]{:S(2)}) collective-permute-start(f32[3,128,384]{2,1,0:T(8,128)S(1)} %get-tuple-element.71), channel_id=1, source_target_pairs={{0,1},{1,2},{2,3},{3,4},{4,5},{5,6},{6,7},{7,8},{8,9},{9,10},{10,1... | collective-permute-start | bytes 1769480 | tf_op jit(solution)/shard_map/ppermute | solution.py:331
  101.2 36.4 %collective-permute-start.10 = (f32[3,256,384]{2,1,0:T(8,128)S(1)}, f32[3,256,384]{2,1,0:T(8,128)S(1)}, u32[]{:S(2)}, u32[]{:S(2)}) collective-permute-start(f32[3,256,384]{2,1,0:T(8,128)S(1)} %get-tuple-element.69), channel_id=1, source_target_pairs={{0,16},{1,17},{2,18},{3,19},{4,20},{5,21},{6,22},{7,23},{8,24},{9,... | collective-permute-start | bytes 3538952 | tf_op jit(solution)/shard_map/ppermute | solution.py:357
  103.2 32.5 %collective-permute-start.15 = (f32[3,128,384]{2,1,0:T(8,128)S(1)}, f32[3,128,384]{2,1,0:T(8,128)S(1)}, u32[]{:S(2)}, u32[]{:S(2)}) collective-permute-start(f32[3,128,384]{2,1,0:T(8,128)S(1)} %get-tuple-element.74), channel_id=1, source_target_pairs={{0,17},{1,18},{2,19},{3,20},{4,21},{5,22},{6,23},{7,24},{8,25},{9,... | collective-permute-start | bytes 1769480 | tf_op jit(solution)/shard_map/ppermute | solution.py:345
  107.8 29.8 %collective-permute-start.17 = (f32[3,128,384]{2,1,0:T(8,128)S(1)}, f32[3,128,384]{2,1,0:T(8,128)S(1)}, u32[]{:S(2)}, u32[]{:S(2)}) collective-permute-start(f32[3,128,384]{2,1,0:T(8,128)S(1)} %collective-permute-done.16), channel_id=1, source_target_pairs={{19,18},{16,19},{21,20},{22,21},{23,22},{20,23},{25,24},{26,25},{2... | collective-permute-start | bytes 1769480 | tf_op jit(solution)/shard_map/ppermute | solution.py:360
  112.2 25.4 %collective-permute-start.19 = (f32[3,128,384]{2,1,0:T(8,128)S(1)}, f32[3,128,384]{2,1,0:T(8,128)S(1)}, u32[]{:S(2)}, u32[]{:S(2)}) collective-permute-start(f32[3,128,384]{2,1,0:T(8,128)S(1)} %collective-permute-done.18), channel_id=1, source_target_pairs={{19,18},{16,19},{21,20},{22,21},{23,22},{20,23},{25,24},{26,25},{2... | collective-permute-start | bytes 1769480 | tf_op jit(solution)/shard_map/ppermute | solution.py:361
  118.9 18.6 %collective-permute-start.14 = (f32[3,128,384]{2,1,0:T(8,128)S(1)}, f32[3,128,384]{2,1,0:T(8,128)S(1)}, u32[]{:S(2)}, u32[]{:S(2)}) collective-permute-start(f32[3,128,384]{2,1,0:T(8,128)S(1)} %add.27), channel_id=1, source_target_pairs={{0,16},{1,17},{2,18},{3,19},{4,20},{5,21},{6,22},{7,23},{8,24},{9,... | collective-permute-start | bytes 1769480 | tf_op jit(solution)/shard_map/ppermute | solution.py:358
  135.7 17.9 %collective-permute-start.12 = (f32[3,128,384]{2,1,0:T(8,128)S(1)}, f32[3,128,384]{2,1,0:T(8,128)S(1)}, u32[]{:S(2)}, u32[]{:S(2)}) collective-permute-start(f32[3,128,384]{2,1,0:T(8,128)S(1)} %add.26), channel_id=1, source_target_pairs={{0,17},{1,18},{2,19},{3,20},{4,21},{5,22},{6,23},{7,24},{8,25},{9,... | collective-permute-start | bytes 1769480 | tf_op jit(solution)/shard_map/ppermute | solution.py:359
  156.2 26.8 %collective-permute-start.26 = (f32[3,128,384]{2,1,0:T(8,128)S(1)}, f32[3,128,384]{2,1,0:T(8,128)S(1)}, u32[]{:S(2)}, u32[]{:S(2)}) collective-permute-start(f32[3,128,384]{2,1,0:T(8,128)S(1)} %get-tuple-element.86), channel_id=1, source_target_pairs={{0,19},{1,16},{2,21},{3,22},{4,23},{5,20},{6,25},{7,26},{8,27},{9,... | collective-permute-start | bytes 1769480 | tf_op jit(solution)/shard_map/ppermute | solution.py:330
  158.2 29.0 %collective-permute-start.28 = (f32[3,128,384]{2,1,0:T(8,128)S(1)}, f32[3,128,384]{2,1,0:T(8,128)S(1)}, u32[]{:S(2)}, u32[]{:S(2)}) collective-permute-start(f32[3,128,384]{2,1,0:T(8,128)S(1)} %get-tuple-element.87), channel_id=1, source_target_pairs={{0,19},{1,16},{2,21},{3,22},{4,23},{5,20},{6,25},{7,26},{8,27},{9,... | collective-permute-start | bytes 1769480 | tf_op jit(solution)/shard_map/ppermute | solution.py:332
  167.2 27.2 %collective-permute-start.23 = (f32[3,128,384]{2,1,0:T(8,128)S(1)}, f32[3,128,384]{2,1,0:T(8,128)S(1)}, u32[]{:S(2)}, u32[]{:S(2)}) collective-permute-start(f32[3,128,384]{2,1,0:T(8,128)S(1)} %get-tuple-element.84), channel_id=1, source_target_pairs={{0,1},{1,2},{2,3},{3,4},{4,5},{5,6},{6,7},{7,8},{8,9},{9,10},{10,1... | collective-permute-start | bytes 1769480 | tf_op jit(solution)/shard_map/ppermute | solution.py:344
  179.1 21.7 %collective-permute-start.21 = (f32[3,128,384]{2,1,0:T(8,128)S(1)}, f32[3,128,384]{2,1,0:T(8,128)S(1)}, u32[]{:S(2)}, u32[]{:S(2)}) collective-permute-start(f32[3,128,384]{2,1,0:T(8,128)S(1)} %get-tuple-element.82), channel_id=1, source_target_pairs={{0,1},{1,2},{2,3},{3,4},{4,5},{5,6},{6,7},{7,8},{8,9},{9,10},{10,1... | collective-permute-start | bytes 1769480 | tf_op jit(solution)/shard_map/ppermute | solution.py:331
  181.1 38.6 %collective-permute-start.20 = (f32[3,256,384]{2,1,0:T(8,128)S(1)}, f32[3,256,384]{2,1,0:T(8,128)S(1)}, u32[]{:S(2)}, u32[]{:S(2)}) collective-permute-start(f32[3,256,384]{2,1,0:T(8,128)S(1)} %get-tuple-element.80), channel_id=1, source_target_pairs={{0,16},{1,17},{2,18},{3,19},{4,20},{5,21},{6,22},{7,23},{8,24},{9,... | collective-permute-start | bytes 3538952 | tf_op jit(solution)/shard_map/ppermute | solution.py:357
  183.0 34.8 %collective-permute-start.25 = (f32[3,128,384]{2,1,0:T(8,128)S(1)}, f32[3,128,384]{2,1,0:T(8,128)S(1)}, u32[]{:S(2)}, u32[]{:S(2)}) collective-permute-start(f32[3,128,384]{2,1,0:T(8,128)S(1)} %get-tuple-element.85), channel_id=1, source_target_pairs={{0,17},{1,18},{2,19},{3,20},{4,21},{5,22},{6,23},{7,24},{8,25},{9,... | collective-permute-start | bytes 1769480 | tf_op jit(solution)/shard_map/ppermute | solution.py:345
  187.1 32.6 %collective-permute-start.27 = (f32[3,128,384]{2,1,0:T(8,128)S(1)}, f32[3,128,384]{2,1,0:T(8,128)S(1)}, u32[]{:S(2)}, u32[]{:S(2)}) collective-permute-start(f32[3,128,384]{2,1,0:T(8,128)S(1)} %collective-permute-done.26), channel_id=1, source_target_pairs={{19,18},{16,19},{21,20},{22,21},{23,22},{20,23},{25,24},{26,25},{2... | collective-permute-start | bytes 1769480 | tf_op jit(solution)/shard_map/ppermute | solution.py:360
  194.5 25.2 %collective-permute-start.29 = (f32[3,128,384]{2,1,0:T(8,128)S(1)}, f32[3,128,384]{2,1,0:T(8,128)S(1)}, u32[]{:S(2)}, u32[]{:S(2)}) collective-permute-start(f32[3,128,384]{2,1,0:T(8,128)S(1)} %collective-permute-done.28), channel_id=1, source_target_pairs={{19,18},{16,19},{21,20},{22,21},{23,22},{20,23},{25,24},{26,25},{2... | collective-permute-start | bytes 1769480 | tf_op jit(solution)/shard_map/ppermute | solution.py:361
  200.8 18.9 %collective-permute-start.24 = (f32[3,128,384]{2,1,0:T(8,128)S(1)}, f32[3,128,384]{2,1,0:T(8,128)S(1)}, u32[]{:S(2)}, u32[]{:S(2)}) collective-permute-start(f32[3,128,384]{2,1,0:T(8,128)S(1)} %add.29), channel_id=1, source_target_pairs={{0,16},{1,17},{2,18},{3,19},{4,20},{5,21},{6,22},{7,23},{8,24},{9,... | collective-permute-start | bytes 1769480 | tf_op jit(solution)/shard_map/ppermute | solution.py:358
  217.8 17.1 %collective-permute-start.22 = (f32[3,128,384]{2,1,0:T(8,128)S(1)}, f32[3,128,384]{2,1,0:T(8,128)S(1)}, u32[]{:S(2)}, u32[]{:S(2)}) collective-permute-start(f32[3,128,384]{2,1,0:T(8,128)S(1)} %add.28), channel_id=1, source_target_pairs={{0,17},{1,18},{2,19},{3,20},{4,21},{5,22},{6,23},{7,24},{8,25},{9,... | collective-permute-start | bytes 1769480 | tf_op jit(solution)/shard_map/ppermute | solution.py:359
  244.7 21.4 %collective-permute-start.31 = (f32[3,128,384]{2,1,0:T(8,128)S(1)}, f32[3,128,384]{2,1,0:T(8,128)S(1)}, u32[]{:S(2)}, u32[]{:S(2)}) collective-permute-start(f32[3,128,384]{2,1,0:T(8,128)S(1)} %get-tuple-element.93), channel_id=1, source_target_pairs={{0,1},{1,2},{2,3},{3,4},{4,5},{5,6},{6,7},{7,8},{8,9},{9,10},{10,1... | collective-permute-start | bytes 1769480 | tf_op jit(solution)/shard_map/ppermute | solution.py:344
  250.9 17.2 %collective-permute-start.34 = (f32[3,128,384]{2,1,0:T(8,128)S(1)}, f32[3,128,384]{2,1,0:T(8,128)S(1)}, u32[]{:S(2)}, u32[]{:S(2)}) collective-permute-start(f32[3,128,384]{2,1,0:T(8,128)S(1)} %get-tuple-element.95), channel_id=1, source_target_pairs={{0,19},{1,16},{2,21},{3,22},{4,23},{5,20},{6,25},{7,26},{8,27},{9,... | collective-permute-start | bytes 1769480 | tf_op jit(solution)/shard_map/ppermute | solution.py:330
  252.8 25.8 %collective-permute-start.36 = (f32[3,128,384]{2,1,0:T(8,128)S(1)}, f32[3,128,384]{2,1,0:T(8,128)S(1)}, u32[]{:S(2)}, u32[]{:S(2)}) collective-permute-start(f32[3,128,384]{2,1,0:T(8,128)S(1)} %get-tuple-element.96), channel_id=1, source_target_pairs={{0,19},{1,16},{2,21},{3,22},{4,23},{5,20},{6,25},{7,26},{8,27},{9,... | collective-permute-start | bytes 1769480 | tf_op jit(solution)/shard_map/ppermute | solution.py:332
  254.7 33.2 %collective-permute-start.38 = (f32[3,128,384]{2,1,0:T(8,128)S(1)}, f32[3,128,384]{2,1,0:T(8,128)S(1)}, u32[]{:S(2)}, u32[]{:S(2)}) collective-permute-start(f32[3,128,384]{2,1,0:T(8,128)S(1)} %get-tuple-element.98), channel_id=1, source_target_pairs={{0,1},{1,2},{2,3},{3,4},{4,5},{5,6},{6,7},{7,8},{8,9},{9,10},{10,1... | collective-permute-start | bytes 1769480 | tf_op jit(solution)/shard_map/ppermute | solution.py:331
  261.2 42.4 %collective-permute-start.33 = (f32[3,128,384]{2,1,0:T(8,128)S(1)}, f32[3,128,384]{2,1,0:T(8,128)S(1)}, u32[]{:S(2)}, u32[]{:S(2)}) collective-permute-start(f32[3,128,384]{2,1,0:T(8,128)S(1)} %get-tuple-element.94), channel_id=1, source_target_pairs={{0,17},{1,18},{2,19},{3,20},{4,21},{5,22},{6,23},{7,24},{8,25},{9,... | collective-permute-start | bytes 1769480 | tf_op jit(solution)/shard_map/ppermute | solution.py:345
  266.1 56.7 %collective-permute-start.30 = (f32[3,256,384]{2,1,0:T(8,128)S(1)}, f32[3,256,384]{2,1,0:T(8,128)S(1)}, u32[]{:S(2)}, u32[]{:S(2)}) collective-permute-start(f32[3,256,384]{2,1,0:T(8,128)S(1)} %get-tuple-element.91), channel_id=1, source_target_pairs={{0,16},{1,17},{2,18},{3,19},{4,20},{5,21},{6,22},{7,23},{8,24},{9,... | collective-permute-start | bytes 3538952 | tf_op jit(solution)/shard_map/ppermute | solution.py:357
  268.1 40.6 %collective-permute-start.32 = (f32[3,128,384]{2,1,0:T(8,128)S(1)}, f32[3,128,384]{2,1,0:T(8,128)S(1)}, u32[]{:S(2)}, u32[]{:S(2)}) collective-permute-start(f32[3,128,384]{2,1,0:T(8,128)S(1)} %add.30), channel_id=1, source_target_pairs={{0,16},{1,17},{2,18},{3,19},{4,20},{5,21},{6,22},{7,23},{8,24},{9,... | collective-permute-start | bytes 1769480 | tf_op jit(solution)/shard_map/ppermute | solution.py:358
  278.6 26.9 %collective-permute-start.35 = (f32[3,128,384]{2,1,0:T(8,128)S(1)}, f32[3,128,384]{2,1,0:T(8,128)S(1)}, u32[]{:S(2)}, u32[]{:S(2)}) collective-permute-start(f32[3,128,384]{2,1,0:T(8,128)S(1)} %collective-permute-done.34), channel_id=1, source_target_pairs={{19,18},{16,19},{21,20},{22,21},{23,22},{20,23},{25,24},{26,25},{2... | collective-permute-start | bytes 1769480 | tf_op jit(solution)/shard_map/ppermute | solution.py:360
  287.9 17.6 %collective-permute-start.37 = (f32[3,128,384]{2,1,0:T(8,128)S(1)}, f32[3,128,384]{2,1,0:T(8,128)S(1)}, u32[]{:S(2)}, u32[]{:S(2)}) collective-permute-start(f32[3,128,384]{2,1,0:T(8,128)S(1)} %collective-permute-done.36), channel_id=1, source_target_pairs={{19,18},{16,19},{21,20},{22,21},{23,22},{20,23},{25,24},{26,25},{2... | collective-permute-start | bytes 1769480 | tf_op jit(solution)/shard_map/ppermute | solution.py:361
  303.6 19.2 %collective-permute-start.39 = (f32[3,128,384]{2,1,0:T(8,128)S(1)}, f32[3,128,384]{2,1,0:T(8,128)S(1)}, u32[]{:S(2)}, u32[]{:S(2)}) collective-permute-start(f32[3,128,384]{2,1,0:T(8,128)S(1)} %add.31), channel_id=1, source_target_pairs={{0,17},{1,18},{2,19},{3,20},{4,21},{5,22},{6,23},{7,24},{8,25},{9,... | collective-permute-start | bytes 1769480 | tf_op jit(solution)/shard_map/ppermute | solution.py:359

commit v5 on v3

--- a/solution.py
+++ b/solution.py
@@ -131,7 +131,7 @@
     each_state(offset, place, count, body)
 
 
-def row_products(place, weights, env_ref, start, plain_ref, turned_ref, combine):
+def row_products(offset, place, weights, env_ref, start, plain_ref, turned_ref, combine):
     count = plain_ref.shape[0]
     rows, block = env_ref.shape[1], env_ref.shape[2]
 
@@ -150,7 +150,7 @@
             )
             combine(out_term, triple, first)
 
-    each_state(2, place, count, body)
+    each_state(offset, place, count, body)
 
 
 def early_kernel(tick, place, weights, stay, high, far_a, far_b, incoming, plain, turned,
@@ -168,7 +168,7 @@
     def combine(term, value, first):
         part[term] = jnp.where(first, jnp.float32(0.0), part[term]) + value
 
-    row_products(place, weights, env_high, LOW, plain, turned, combine)
+    row_products(2, place, weights, env_high, LOW, plain, turned, combine)
 
 
 def late_kernel(tick, place, weights, stay, low, part, incoming, plain, turned,
@@ -189,7 +189,7 @@
             ref[term] = before + value[row : row + rows]
             row += rows
 
-    row_products(place, weights, env_low, 0, plain, turned, combine)
+    row_products(2, place, weights, env_low, 0, plain, turned, combine)
 
 
 def first_kernel(place, weights, env, states, out_low, out_a, out_b, plain, turned,
@@ -206,7 +206,7 @@
     def ready(state):
         fill(state, place, plain.shape[0], states, plain, turned)
 
-    products(1, place, weights, [env], plain, turned, [out_low, out_high], scratch, ready)
+    looped(1, place, weights, [env], plain, turned, [out_low, out_high], ready)
 
 
 def first_zero_kernel(place, weights, env, states, plain_in, turned_in,
@@ -221,8 +221,21 @@
     products(1, place, weights, [env_low, env_high], plain, turned, [out_low, out_high], scratch)
 
 
-def zero_kernel(place, weights, env_low, env_high, plain, turned, out_low, out_high, *scratch):
-    looped(0, place, weights, [env_low, env_high], plain, turned, [out_low, out_high])
+def early_zero_kernel(place, weights, env_high, plain, turned, part, *scratch):
+    def combine(term, value, first):
+        part[term] = jnp.where(first, jnp.float32(0.0), part[term]) + value
+
+    row_products(0, place, weights, env_high, LOW, plain, turned, combine)
+
+
+def late_zero_kernel(place, weights, env_low, part, plain, turned, out_low, out_high, *scratch):
+    def combine(term, value, first):
+        low = jnp.where(first, part[term, :LOW], out_low[term])
+        high = jnp.where(first, part[term, LOW:], out_high[term])
+        out_low[term] = low + value[:LOW]
+        out_high[term] = high + value[LOW:]
+
+    row_products(0, place, weights, env_low, 0, plain, turned, combine)
 
 
 def final_kernel(tick, place, stay_low, stay_high, high, far_a, far_b, low, incoming, env,
@@ -339,7 +352,7 @@
             )
         else:
             zero_low, zero_high = call(
-                zero_kernel, scalars + (env_low, env_high, plain, turned), parts
+                late_zero_kernel, scalars + (env_low, zero_part, plain, turned), parts, rows=LOW
             )
         kept_high = lax.ppermute(zero_high, AXES, stay)
         kept_low = lax.ppermute(zero_low, AXES, stay)
@@ -352,6 +365,9 @@
                 scalars + (kept_high, high, far_a, far_b, incoming, plain, turned),
                 [parts[1], whole],
                 rows=block - LOW,
+            )
+            (zero_part,) = call(
+                early_zero_kernel, scalars + (env_high, plain, turned), [whole], rows=LOW
             )
     (env,) = call(
         functools.partial(final_kernel, TICKS - 1),

time: 349 us -> 347 us (level)
  Pallas kernels: 72.7 us -> 78.7 us
  starting transfers between devices: 95.4 us -> 91 us
    ppermute x4, waiting for transfers between devices: 15.4 us -> 25.6 us  [local(): kept_low = lax.ppermute(zero_low, AXES, stay)]
    ppermute x4, waiting for transfers between devices: 15.5 us -> 9.36 us  [local(): far_b = lax.ppermute(far_b, AXES, far_one)]
    pallas_call x16 -> x19, Pallas kernels: 72.7 us -> 78.7 us  [call(): pl.pallas_call(kernel, in_specs=specs, out_specs=[VMEM] * len(outputs), o...]
    ppermute x4, starting transfers between devices: 12.6 us -> 7.67 us  [local(): low = lax.ppermute(one_low + two_low, AXES, lift)]
  transfers between devices with their start and end apart: 36 -> 36, of which waited for: 15 -> 15; matrix products, arithmetic and copies ran while one was open for 0% -> 0% of each run, Pallas kernels for 17% -> 19%
where the time goes in v5:
time: 347 us; the launch traced here: 346 us
  waiting for transfers between devices  170 us (49%)
  starting transfers between devices  91 us (26%)
  Pallas kernels  78.7 us (23%)
  local copies, waits for them, and re-layouts  4.99 us (1%)
    ppermute x4, waiting for transfers between devices, local(): two_low = lax.ppermute(two_low, AXES, relay)  85.3 us
    pallas_call x19, Pallas kernels, call(): pl.pallas_call(kernel, in_specs=specs, out_specs=[VMEM] * len(outputs), o...  78.7 us
    ppermute x4, waiting for transfers between devices, local(): low = lax.ppermute(one_low + two_low, AXES, lift)  46.3 us
    ppermute x4, waiting for transfers between devices, local(): kept_low = lax.ppermute(zero_low, AXES, stay)  25.6 us
    ppermute x4, starting transfers between devices, local(): far_a = lax.ppermute(far_a, AXES, far_one)  12.5 us
    ppermute x4, starting transfers between devices, local(): far_a = lax.ppermute(far_a, AXES, far_two)  12.5 us
    ppermute x4, starting transfers between devices, local(): two_low = lax.ppermute(two_low, AXES, relay)  11.2 us
    ppermute x4, starting transfers between devices, local(): kept_low = lax.ppermute(zero_low, AXES, stay)  10.6 us
  transfers between devices with their start and end apart: 36, of which 15 were waited for; matrix products, arithmetic and copies ran while one was open for 0% of the time, Pallas kernels for 19%

profile of v5, /device:TPU:1, one launch (start us, length us, event | category | flops | bytes accessed | tf_op | source)
XLA Modules:
  0.0 345.9 jit_solution(2856848899473145356)
XLA Ops:
  5.6 4.1 %shard_map.73 = (f32[3,128,384]{2,1,0:T(8,128)S(1)}, f32[3,128,384]{2,1,0:T(8,128)S(1)}, f32[3,128,384]{2,1,0:T(8,128)S(1)}, bf16[4,1152,384]{2,1,0:T(8,128)(2,1)S(1)}, bf16[4,384,1152]{2,1,0:T(8,128)(2,1)S(1)}) custom-call(s32[23]{0:T(128)S(1)} %concatenate.3.place, f32[576]{0:T(1024)S(1)} %reshape.3.weights, f32[3,384,384]{2,1,0:T(8,128)S(1)} %bitcast.8, ...), custom_call_target="tpu_custom_call" | custom-call | flops 2038431744 | bytes 7077888 | tf_op jit(solution)/shard_map/pallas_call | solution.py:307
  9.7 6.8 %collective-permute-start.5 = (f32[3,128,384]{2,1,0:T(8,128)S(1)}, f32[3,128,384]{2,1,0:T(8,128)S(1)}, u32[]{:S(2)}, u32[]{:S(2)}) collective-permute-start(f32[3,128,384]{2,1,0:T(8,128)S(1)} %get-tuple-element.57), channel_id=1, source_target_pairs={{0,19},{1,16},{2,21},{3,22},{4,23},{5,20},{6,25},{7,26},{8,27},{9,... | collective-permute-start | bytes 1769480 | tf_op jit(solution)/shard_map/ppermute | solution.py:331
  16.5 3.5 %collective-permute-start.7 = (f32[3,128,384]{2,1,0:T(8,128)S(1)}, f32[3,128,384]{2,1,0:T(8,128)S(1)}, u32[]{:S(2)}, u32[]{:S(2)}) collective-permute-start(f32[3,128,384]{2,1,0:T(8,128)S(1)} %get-tuple-element.58), channel_id=1, source_target_pairs={{0,19},{1,16},{2,21},{3,22},{4,23},{5,20},{6,25},{7,26},{8,27},{9,... | collective-permute-start | bytes 1769480 | tf_op jit(solution)/shard_map/ppermute | solution.py:333
  20.0 8.9 %shard_map.74 = (f32[3,128,384]{2,1,0:T(8,128)S(1)}, f32[3,256,384]{2,1,0:T(8,128)S(1)}, bf16[4,1152,384]{2,1,0:T(8,128)(2,1)S(1)}, bf16[4,384,1152]{2,1,0:T(8,128)(2,1)S(1)}) custom-call(s32[23]{0:T(128)S(1)} %concatenate.3.place, f32[576]{0:T(1024)S(1)} %reshape.3.weights, ...), custom_call_target="tpu_custom_call", output_to_operand_aliasing={{2}: (4, {}), {3}: (5, {})} | custom-call | flops 2038431744 | bytes 7077888 | tf_op jit(solution)/shard_map/pallas_call | solution.py:307
  29.0 3.0 collective-permute-start.4
  32.0 4.8 %shard_map.75 = (f32[3,128,384]{2,1,0:T(8,128)S(1)}, f32[3,256,384]{2,1,0:T(8,128)S(1)}, bf16[4,1152,384]{2,1,0:T(8,128)(2,1)S(1)}, bf16[4,384,1152]{2,1,0:T(8,128)(2,1)S(1)}) custom-call(s32[23]{0:T(128)S(1)} %concatenate.3.place, f32[576]{0:T(1024)S(1)} %reshape.3.weights, ...), custom_call_target="tpu_custom_call", output_to_operand_aliasing={{2}: (4, {}), {3}: (5, {})} | custom-call | flops 2038431744 | bytes 7077888 | tf_op jit(solution)/shard_map/pallas_call | solution.py:307
  36.8 2.6 collective-permute-start.3
  39.5 1.9 collective-permute-start.1
  41.4 5.9 %collective-permute-start.6 = (f32[3,128,384]{2,1,0:T(8,128)S(1)}, f32[3,128,384]{2,1,0:T(8,128)S(1)}, u32[]{:S(2)}, u32[]{:S(2)}) collective-permute-start(f32[3,128,384]{2,1,0:T(8,128)S(1)} %collective-permute-done.5), channel_id=1, source_target_pairs={{19,18},{16,19},{21,20},{22,21},{23,22},{20,23},{25,24},{26,25},{2... | collective-permute-start | bytes 1769480 | tf_op jit(solution)/shard_map/ppermute | solution.py:360
  47.4 3.1 collective-permute-start.8
  50.5 24.6 %collective-permute-done.1 = f32[3,128,384]{2,1,0:T(8,128)S(1)} collective-permute-done((f32[3,128,384]{2,1,0:T(8,128)S(1)}, f32[3,128,384]{2,1,0:T(8,128)S(1)}, u32[]{:S(2)}, u32[]{:S(2)}) %collective-permute-start.1) | collective-permute-done | bytes 589856 | tf_op jit(solution)/shard_map/ppermute | solution.py:332
  75.1 3.7 %collective-permute-start = (f32[3,128,384]{2,1,0:T(8,128)S(1)}, f32[3,128,384]{2,1,0:T(8,128)S(1)}, u32[]{:S(2)}, u32[]{:S(2)}) collective-permute-start(f32[3,128,384]{2,1,0:T(8,128)S(1)} %get-tuple-element.52), channel_id=1, source_target_pairs={{0,16},{1,17},{2,18},{3,19},{4,20},{5,21},{6,22},{7,23},{8,24},{9,... | collective-permute-start | bytes 1769480 | tf_op jit(solution)/shard_map/ppermute | solution.py:358
  78.9 1.9 collective-permute-start.2
  80.9 3.7 %shard_map.76 = (f32[3,256,384]{2,1,0:T(8,128)S(1)}, f32[3,384,384]{2,1,0:T(8,128)S(1)}) custom-call(s32[23]{0:T(128)S(1)} %concatenate.3.place, f32[576]{0:T(1024)S(1)} %reshape.3.weights, f32[3,256,384]{2,1,0:T(8,128)S(1)} %collective-permute-done.3.stay, f32[3,256,384]{2,1,0:T(8,128)S(1)} %collective-permute-done.4.high, ...), custom_call_target="tpu_custom_call" | custom-call | flops 2038431744 | bytes 7077888 | tf_op jit(solution)/shard_map/pallas_call | solution.py:307
  84.6 3.4 collective-permute-done.stay
  88.0 10.9 %collective-permute-done.2.low = f32[3,128,384]{2,1,0:T(8,128)S(1)} collective-permute-done((f32[3,128,384]{2,1,0:T(8,128)S(1)}, f32[3,128,384]{2,1,0:T(8,128)S(1)}, u32[]{:S(2)}, u32[]{:S(2)}) %collective-permute-start.2) | collective-permute-done | bytes 589856 | tf_op jit(solution)/shard_map/ppermute | solution.py:359
  98.9 2.7 shard_map.77
  101.6 1.9 collective-permute-start.14
  103.5 2.1 collective-permute-start.16
  105.7 3.5 %shard_map.78.part = f32[3,384,384]{2,1,0:T(8,128)S(1)} custom-call(s32[23]{0:T(128)S(1)} %concatenate.3.place, f32[576]{0:T(1024)S(1)} %reshape.3.weights, f32[3,256,384]{2,1,0:T(8,128)S(1)} %get-tuple-element.63.env_high, bf16[4,1152,384]{2,1,0:T(8,128)(2,1)S(1)} %get-tuple-element.59.plain, bf16[4,384,1152]{2,1,0:T(8,128)(2,1)S(1)} %get-tuple-element.60.turned), custom_call_target="tpu_custom_call" | custom-call | flops 2038431744 | bytes 7077888 | tf_op jit(solution)/shard_map/pallas_call | solution.py:307
  109.1 7.1 %shard_map.80 = (f32[3,128,384]{2,1,0:T(8,128)S(1)}, f32[3,256,384]{2,1,0:T(8,128)S(1)}) custom-call(s32[23]{0:T(128)S(1)} %concatenate.3.place, f32[576]{0:T(1024)S(1)} %reshape.3.weights, f32[3,128,384]{2,1,0:T(8,128)S(1)} %get-tuple-element.62.env_low, f32[3,256,384]{2,1,0:T(8,128)S(1)} %get-tuple-element.63.env_high, ...), custom_call_target="tpu_custom_call" | custom-call | flops 2038431744 | bytes 7077888 | tf_op jit(solution)/shard_map/pallas_call | solution.py:307
  116.3 2.7 shard_map.79
  118.9 1.9 collective-permute-start.13
  120.9 2.8 collective-permute-start.12
  123.7 3.1 collective-permute-start.10
  126.8 2.4 collective-permute-start.15
  129.2 2.5 collective-permute-done.16
  133.6 31.7 %collective-permute-done.10 = f32[3,128,384]{2,1,0:T(8,128)S(1)} collective-permute-done((f32[3,128,384]{2,1,0:T(8,128)S(1)}, f32[3,128,384]{2,1,0:T(8,128)S(1)}, u32[]{:S(2)}, u32[]{:S(2)}) %collective-permute-start.10) | collective-permute-done | bytes 589856 | tf_op jit(solution)/shard_map/ppermute | solution.py:332
  167.3 1.9 collective-permute-start.11
  169.3 3.7 %shard_map.81 = (f32[3,256,384]{2,1,0:T(8,128)S(1)}, f32[3,384,384]{2,1,0:T(8,128)S(1)}) custom-call(s32[23]{0:T(128)S(1)} %concatenate.3.place, f32[576]{0:T(1024)S(1)} %reshape.3.weights, f32[3,256,384]{2,1,0:T(8,128)S(1)} %collective-permute-done.12.stay, f32[3,256,384]{2,1,0:T(8,128)S(1)} %collective-permute-done.13.high, ...), custom_call_target="tpu_custom_call" | custom-call | flops 2038431744 | bytes 7077888 | tf_op jit(solution)/shard_map/pallas_call | solution.py:307
  172.9 7.4 %collective-permute-done.9.stay = f32[3,128,384]{2,1,0:T(8,128)S(1)} collective-permute-done((f32[3,128,384]{2,1,0:T(8,128)S(1)}, f32[3,128,384]{2,1,0:T(8,128)S(1)}, u32[]{:S(2)}, u32[]{:S(2)}) %collective-permute-start.9) | collective-permute-done | bytes 589856 | tf_op jit(solution)/shard_map/ppermute | solution.py:358
  180.4 5.2 %collective-permute-done.11.low = f32[3,128,384]{2,1,0:T(8,128)S(1)} collective-permute-done((f32[3,128,384]{2,1,0:T(8,128)S(1)}, f32[3,128,384]{2,1,0:T(8,128)S(1)}, u32[]{:S(2)}, u32[]{:S(2)}) %collective-permute-start.11) | collective-permute-done | bytes 589856 | tf_op jit(solution)/shard_map/ppermute | solution.py:359
  185.5 2.7 shard_map.82
  188.3 1.9 collective-permute-start.23
  190.2 1.9 collective-permute-start.25
  192.1 3.5 %shard_map.83.part = f32[3,384,384]{2,1,0:T(8,128)S(1)} custom-call(s32[23]{0:T(128)S(1)} %concatenate.3.place, f32[576]{0:T(1024)S(1)} %reshape.3.weights, f32[3,256,384]{2,1,0:T(8,128)S(1)} %get-tuple-element.73.env_high, bf16[4,1152,384]{2,1,0:T(8,128)(2,1)S(1)} %get-tuple-element.59.plain, bf16[4,384,1152]{2,1,0:T(8,128)(2,1)S(1)} %get-tuple-element.60.turned), custom_call_target="tpu_custom_call" | custom-call | flops 2038431744 | bytes 7077888 | tf_op jit(solution)/shard_map/pallas_call | solution.py:307
  195.6 7.1 %shard_map.85 = (f32[3,128,384]{2,1,0:T(8,128)S(1)}, f32[3,256,384]{2,1,0:T(8,128)S(1)}) custom-call(s32[23]{0:T(128)S(1)} %concatenate.3.place, f32[576]{0:T(1024)S(1)} %reshape.3.weights, f32[3,128,384]{2,1,0:T(8,128)S(1)} %get-tuple-element.72.env_low, f32[3,256,384]{2,1,0:T(8,128)S(1)} %get-tuple-element.73.env_high, ...), custom_call_target="tpu_custom_call" | custom-call | flops 2038431744 | bytes 7077888 | tf_op jit(solution)/shard_map/pallas_call | solution.py:307
  202.8 2.6 shard_map.84
  205.4 2.0 collective-permute-start.22
  207.4 1.9 collective-permute-start.21
  209.4 2.2 collective-permute-start.19
  211.6 2.3 collective-permute-start.24
  213.9 3.6 %collective-permute-done.25 = f32[3,128,384]{2,1,0:T(8,128)S(1)} collective-permute-done((f32[3,128,384]{2,1,0:T(8,128)S(1)}, f32[3,128,384]{2,1,0:T(8,128)S(1)}, u32[]{:S(2)}, u32[]{:S(2)}) %collective-permute-start.25) | collective-permute-done | bytes 589856 | tf_op jit(solution)/shard_map/ppermute | solution.py:333
  219.4 29.0 %collective-permute-done.19 = f32[3,128,384]{2,1,0:T(8,128)S(1)} collective-permute-done((f32[3,128,384]{2,1,0:T(8,128)S(1)}, f32[3,128,384]{2,1,0:T(8,128)S(1)}, u32[]{:S(2)}, u32[]{:S(2)}) %collective-permute-start.19) | collective-permute-done | bytes 589856 | tf_op jit(solution)/shard_map/ppermute | solution.py:332
  248.4 3.1 collective-permute-start.18
  251.6 1.9 collective-permute-start.20
  253.5 3.7 %shard_map.86 = (f32[3,256,384]{2,1,0:T(8,128)S(1)}, f32[3,384,384]{2,1,0:T(8,128)S(1)}) custom-call(s32[23]{0:T(128)S(1)} %concatenate.3.place, f32[576]{0:T(1024)S(1)} %reshape.3.weights, f32[3,256,384]{2,1,0:T(8,128)S(1)} %collective-permute-done.21.stay, f32[3,256,384]{2,1,0:T(8,128)S(1)} %collective-permute-done.22.high, ...), custom_call_target="tpu_custom_call" | custom-call | flops 2038431744 | bytes 7077888 | tf_op jit(solution)/shard_map/pallas_call | solution.py:307
  257.2 6.8 %collective-permute-done.18.stay = f32[3,128,384]{2,1,0:T(8,128)S(1)} collective-permute-done((f32[3,128,384]{2,1,0:T(8,128)S(1)}, f32[3,128,384]{2,1,0:T(8,128)S(1)}, u32[]{:S(2)}, u32[]{:S(2)}) %collective-permute-start.18) | collective-permute-done | bytes 589856 | tf_op jit(solution)/shard_map/ppermute | solution.py:358
  264.0 7.6 %collective-permute-done.20.low = f32[3,128,384]{2,1,0:T(8,128)S(1)} collective-permute-done((f32[3,128,384]{2,1,0:T(8,128)S(1)}, f32[3,128,384]{2,1,0:T(8,128)S(1)}, u32[]{:S(2)}, u32[]{:S(2)}) %collective-permute-start.20) | collective-permute-done | bytes 589856 | tf_op jit(solution)/shard_map/ppermute | solution.py:359
  271.6 2.7 shard_map.87
  274.3 1.9 collective-permute-start.30
  276.2 1.9 collective-permute-start.32
  278.2 4.0 %collective-permute-start.34 = (f32[3,128,384]{2,1,0:T(8,128)S(1)}, f32[3,128,384]{2,1,0:T(8,128)S(1)}, u32[]{:S(2)}, u32[]{:S(2)}) collective-permute-start(f32[3,128,384]{2,1,0:T(8,128)S(1)} %get-tuple-element.90), channel_id=1, source_target_pairs={{0,1},{1,2},{2,3},{3,4},{4,5},{5,6},{6,7},{7,8},{8,9},{9,10},{10,1... | collective-permute-start | bytes 1769480 | tf_op jit(solution)/shard_map/ppermute | solution.py:332
  282.2 3.5 %shard_map.88.part = f32[3,384,384]{2,1,0:T(8,128)S(1)} custom-call(s32[23]{0:T(128)S(1)} %concatenate.3.place, f32[576]{0:T(1024)S(1)} %reshape.3.weights, f32[3,256,384]{2,1,0:T(8,128)S(1)} %get-tuple-element.83.env_high, bf16[4,1152,384]{2,1,0:T(8,128)(2,1)S(1)} %get-tuple-element.59.plain, bf16[4,384,1152]{2,1,0:T(8,128)(2,1)S(1)} %get-tuple-element.60.turned), custom_call_target="tpu_custom_call" | custom-call | flops 2038431744 | bytes 7077888 | tf_op jit(solution)/shard_map/pallas_call | solution.py:307
  285.6 7.1 %shard_map.90 = (f32[3,128,384]{2,1,0:T(8,128)S(1)}, f32[3,256,384]{2,1,0:T(8,128)S(1)}) custom-call(s32[23]{0:T(128)S(1)} %concatenate.3.place, f32[576]{0:T(1024)S(1)} %reshape.3.weights, f32[3,128,384]{2,1,0:T(8,128)S(1)} %get-tuple-element.82.env_low, f32[3,256,384]{2,1,0:T(8,128)S(1)} %get-tuple-element.83.env_high, ...), custom_call_target="tpu_custom_call" | custom-call | flops 2038431744 | bytes 7077888 | tf_op jit(solution)/shard_map/pallas_call | solution.py:307
  292.8 2.7 shard_map.89
  295.4 1.9 collective-permute-start.27
  299.3 1.9 collective-permute-start.29
  301.2 3.2 collective-permute-done.32
  306.3 1.9 collective-permute-start.33
  308.4 8.0 %collective-permute-done.27.stay_low = f32[3,128,384]{2,1,0:T(8,128)S(1)} collective-permute-done((f32[3,128,384]{2,1,0:T(8,128)S(1)}, f32[3,128,384]{2,1,0:T(8,128)S(1)}, u32[]{:S(2)}, u32[]{:S(2)}) %collective-permute-start.27) | collective-permute-done | bytes 589856 | tf_op jit(solution)/shard_map/ppermute | solution.py:358
  318.3 3.0 collective-permute-done.33.far_b
  321.4 22.6 %collective-permute-done.35.low = f32[3,128,384]{2,1,0:T(8,128)S(1)} collective-permute-done((f32[3,128,384]{2,1,0:T(8,128)S(1)}, f32[3,128,384]{2,1,0:T(8,128)S(1)}, u32[]{:S(2)}, u32[]{:S(2)}) %collective-permute-start.35) | collective-permute-done | bytes 589856 | tf_op jit(solution)/shard_map/ppermute | solution.py:359
  344.0 2.0 shard_map.91
  (43 shorter events, 16.8 us)
Async XLA Ops:
  2.5 1.7 copy-start
  4.2 1.5 copy-start.1
  9.7 31.7 %collective-permute-start.5 = (f32[3,128,384]{2,1,0:T(8,128)S(1)}, f32[3,128,384]{2,1,0:T(8,128)S(1)}, u32[]{:S(2)}, u32[]{:S(2)}) collective-permute-start(f32[3,128,384]{2,1,0:T(8,128)S(1)} %get-tuple-element.57), channel_id=1, source_target_pairs={{0,19},{1,16},{2,21},{3,22},{4,23},{5,20},{6,25},{7,26},{8,27},{9,... | collective-permute-start | bytes 1769480 | tf_op jit(solution)/shard_map/ppermute | solution.py:331
  16.5 30.9 %collective-permute-start.7 = (f32[3,128,384]{2,1,0:T(8,128)S(1)}, f32[3,128,384]{2,1,0:T(8,128)S(1)}, u32[]{:S(2)}, u32[]{:S(2)}) collective-permute-start(f32[3,128,384]{2,1,0:T(8,128)S(1)} %get-tuple-element.58), channel_id=1, source_target_pairs={{0,19},{1,16},{2,21},{3,22},{4,23},{5,20},{6,25},{7,26},{8,27},{9,... | collective-permute-start | bytes 1769480 | tf_op jit(solution)/shard_map/ppermute | solution.py:333
  29.0 51.8 %collective-permute-start.4 = (f32[3,256,384]{2,1,0:T(8,128)S(1)}, f32[3,256,384]{2,1,0:T(8,128)S(1)}, u32[]{:S(2)}, u32[]{:S(2)}) collective-permute-start(f32[3,256,384]{2,1,0:T(8,128)S(1)} %get-tuple-element.56), channel_id=1, source_target_pairs={{0,17},{1,18},{2,19},{3,20},{4,21},{5,22},{6,23},{7,24},{8,25},{9,... | collective-permute-start | bytes 3538952 | tf_op jit(solution)/shard_map/ppermute | solution.py:345
  32.0 48.8 %slice-start = ((s8[7077888]{0:T(1024)(128)(4,1)}), s8[4194304]{0:T(1024)(128)(4,1)S(1)}, s32[]{:S(2)}) async-start(s8[7077888]{0:T(1024)(128)(4,1)} %bitcast.6), calls=%async_computation | async-start | bytes 8388608
  32.0 48.8 %slice-start.1 = ((s8[7077888]{0:T(1024)(128)(4,1)}), s8[2883584]{0:T(1024)(128)(4,1)S(1)}, s32[]{:S(2)}) async-start(s8[7077888]{0:T(1024)(128)(4,1)} %bitcast.6), calls=%async_computation.1 | async-start | bytes 5767168
  36.8 44.0 %collective-permute-start.3 = (f32[3,256,384]{2,1,0:T(8,128)S(1)}, f32[3,256,384]{2,1,0:T(8,128)S(1)}, u32[]{:S(2)}, u32[]{:S(2)}) collective-permute-start(f32[3,256,384]{2,1,0:T(8,128)S(1)} %get-tuple-element.55), channel_id=1, source_target_pairs={{0,16},{1,17},{2,18},{3,19},{4,20},{5,21},{6,22},{7,23},{8,24},{9,... | collective-permute-start | bytes 3538952 | tf_op jit(solution)/shard_map/ppermute | solution.py:357
  39.5 35.6 %collective-permute-start.1 = (f32[3,128,384]{2,1,0:T(8,128)S(1)}, f32[3,128,384]{2,1,0:T(8,128)S(1)}, u32[]{:S(2)}, u32[]{:S(2)}) collective-permute-start(f32[3,128,384]{2,1,0:T(8,128)S(1)} %get-tuple-element.54), channel_id=1, source_target_pairs={{0,1},{1,2},{2,3},{3,4},{4,5},{5,6},{6,7},{7,8},{8,9},{9,10},{10,1... | collective-permute-start | bytes 1769480 | tf_op jit(solution)/shard_map/ppermute | solution.py:332
  41.4 37.5 %collective-permute-start.6 = (f32[3,128,384]{2,1,0:T(8,128)S(1)}, f32[3,128,384]{2,1,0:T(8,128)S(1)}, u32[]{:S(2)}, u32[]{:S(2)}) collective-permute-start(f32[3,128,384]{2,1,0:T(8,128)S(1)} %collective-permute-done.5), channel_id=1, source_target_pairs={{19,18},{16,19},{21,20},{22,21},{23,22},{20,23},{25,24},{26,25},{2... | collective-permute-start | bytes 1769480 | tf_op jit(solution)/shard_map/ppermute | solution.py:360
  47.4 33.5 %collective-permute-start.8 = (f32[3,128,384]{2,1,0:T(8,128)S(1)}, f32[3,128,384]{2,1,0:T(8,128)S(1)}, u32[]{:S(2)}, u32[]{:S(2)}) collective-permute-start(f32[3,128,384]{2,1,0:T(8,128)S(1)} %collective-permute-done.7), channel_id=1, source_target_pairs={{19,18},{16,19},{21,20},{22,21},{23,22},{20,23},{25,24},{26,25},{2... | collective-permute-start | bytes 1769480 | tf_op jit(solution)/shard_map/ppermute | solution.py:361
  75.1 12.9 %collective-permute-start = (f32[3,128,384]{2,1,0:T(8,128)S(1)}, f32[3,128,384]{2,1,0:T(8,128)S(1)}, u32[]{:S(2)}, u32[]{:S(2)}) collective-permute-start(f32[3,128,384]{2,1,0:T(8,128)S(1)} %get-tuple-element.52), channel_id=1, source_target_pairs={{0,16},{1,17},{2,18},{3,19},{4,20},{5,21},{6,22},{7,23},{8,24},{9,... | collective-permute-start | bytes 1769480 | tf_op jit(solution)/shard_map/ppermute | solution.py:358
  78.9 20.0 %collective-permute-start.2 = (f32[3,128,384]{2,1,0:T(8,128)S(1)}, f32[3,128,384]{2,1,0:T(8,128)S(1)}, u32[]{:S(2)}, u32[]{:S(2)}) collective-permute-start(f32[3,128,384]{2,1,0:T(8,128)S(1)} %add.12), channel_id=1, source_target_pairs={{0,17},{1,18},{2,19},{3,20},{4,21},{5,22},{6,23},{7,24},{8,25},{9,... | collective-permute-start | bytes 1769480 | tf_op jit(solution)/shard_map/ppermute | solution.py:359
  101.6 25.2 %collective-permute-start.14 = (f32[3,128,384]{2,1,0:T(8,128)S(1)}, f32[3,128,384]{2,1,0:T(8,128)S(1)}, u32[]{:S(2)}, u32[]{:S(2)}) collective-permute-start(f32[3,128,384]{2,1,0:T(8,128)S(1)} %get-tuple-element.69), channel_id=1, source_target_pairs={{0,19},{1,16},{2,21},{3,22},{4,23},{5,20},{6,25},{7,26},{8,27},{9,... | collective-permute-start | bytes 1769480 | tf_op jit(solution)/shard_map/ppermute | solution.py:331
  103.5 28.2 %collective-permute-start.16 = (f32[3,128,384]{2,1,0:T(8,128)S(1)}, f32[3,128,384]{2,1,0:T(8,128)S(1)}, u32[]{:S(2)}, u32[]{:S(2)}) collective-permute-start(f32[3,128,384]{2,1,0:T(8,128)S(1)} %get-tuple-element.70), channel_id=1, source_target_pairs={{0,19},{1,16},{2,21},{3,22},{4,23},{5,20},{6,25},{7,26},{8,27},{9,... | collective-permute-start | bytes 1769480 | tf_op jit(solution)/shard_map/ppermute | solution.py:333
  118.9 50.3 %collective-permute-start.13 = (f32[3,256,384]{2,1,0:T(8,128)S(1)}, f32[3,256,384]{2,1,0:T(8,128)S(1)}, u32[]{:S(2)}, u32[]{:S(2)}) collective-permute-start(f32[3,256,384]{2,1,0:T(8,128)S(1)} %get-tuple-element.68), channel_id=1, source_target_pairs={{0,17},{1,18},{2,19},{3,20},{4,21},{5,22},{6,23},{7,24},{8,25},{9,... | collective-permute-start | bytes 3538952 | tf_op jit(solution)/shard_map/ppermute | solution.py:345
  120.9 48.4 %collective-permute-start.12 = (f32[3,256,384]{2,1,0:T(8,128)S(1)}, f32[3,256,384]{2,1,0:T(8,128)S(1)}, u32[]{:S(2)}, u32[]{:S(2)}) collective-permute-start(f32[3,256,384]{2,1,0:T(8,128)S(1)} %get-tuple-element.67), channel_id=1, source_target_pairs={{0,16},{1,17},{2,18},{3,19},{4,20},{5,21},{6,22},{7,23},{8,24},{9,... | collective-permute-start | bytes 3538952 | tf_op jit(solution)/shard_map/ppermute | solution.py:357
  123.7 41.6 %collective-permute-start.10 = (f32[3,128,384]{2,1,0:T(8,128)S(1)}, f32[3,128,384]{2,1,0:T(8,128)S(1)}, u32[]{:S(2)}, u32[]{:S(2)}) collective-permute-start(f32[3,128,384]{2,1,0:T(8,128)S(1)} %get-tuple-element.66), channel_id=1, source_target_pairs={{0,1},{1,2},{2,3},{3,4},{4,5},{5,6},{6,7},{7,8},{8,9},{9,10},{10,1... | collective-permute-start | bytes 1769480 | tf_op jit(solution)/shard_map/ppermute | solution.py:332
  126.8 40.5 %collective-permute-start.15 = (f32[3,128,384]{2,1,0:T(8,128)S(1)}, f32[3,128,384]{2,1,0:T(8,128)S(1)}, u32[]{:S(2)}, u32[]{:S(2)}) collective-permute-start(f32[3,128,384]{2,1,0:T(8,128)S(1)} %collective-permute-done.14), channel_id=1, source_target_pairs={{19,18},{16,19},{21,20},{22,21},{23,22},{20,23},{25,24},{26,25},{2... | collective-permute-start | bytes 1769480 | tf_op jit(solution)/shard_map/ppermute | solution.py:360
  131.7 37.5 %collective-permute-start.17 = (f32[3,128,384]{2,1,0:T(8,128)S(1)}, f32[3,128,384]{2,1,0:T(8,128)S(1)}, u32[]{:S(2)}, u32[]{:S(2)}) collective-permute-start(f32[3,128,384]{2,1,0:T(8,128)S(1)} %collective-permute-done.16), channel_id=1, source_target_pairs={{19,18},{16,19},{21,20},{22,21},{23,22},{20,23},{25,24},{26,25},{2... | collective-permute-start | bytes 1769480 | tf_op jit(solution)/shard_map/ppermute | solution.py:361
  165.3 15.0 %collective-permute-start.9 = (f32[3,128,384]{2,1,0:T(8,128)S(1)}, f32[3,128,384]{2,1,0:T(8,128)S(1)}, u32[]{:S(2)}, u32[]{:S(2)}) collective-permute-start(f32[3,128,384]{2,1,0:T(8,128)S(1)} %get-tuple-element.64), channel_id=1, source_target_pairs={{0,16},{1,17},{2,18},{3,19},{4,20},{5,21},{6,22},{7,23},{8,24},{9,... | collective-permute-start | bytes 1769480 | tf_op jit(solution)/shard_map/ppermute | solution.py:358
  167.3 18.2 %collective-permute-start.11 = (f32[3,128,384]{2,1,0:T(8,128)S(1)}, f32[3,128,384]{2,1,0:T(8,128)S(1)}, u32[]{:S(2)}, u32[]{:S(2)}) collective-permute-start(f32[3,128,384]{2,1,0:T(8,128)S(1)} %add.13), channel_id=1, source_target_pairs={{0,17},{1,18},{2,19},{3,20},{4,21},{5,22},{6,23},{7,24},{8,25},{9,... | collective-permute-start | bytes 1769480 | tf_op jit(solution)/shard_map/ppermute | solution.py:359
  188.3 23.3 %collective-permute-start.23 = (f32[3,128,384]{2,1,0:T(8,128)S(1)}, f32[3,128,384]{2,1,0:T(8,128)S(1)}, u32[]{:S(2)}, u32[]{:S(2)}) collective-permute-start(f32[3,128,384]{2,1,0:T(8,128)S(1)} %get-tuple-element.79), channel_id=1, source_target_pairs={{0,19},{1,16},{2,21},{3,22},{4,23},{5,20},{6,25},{7,26},{8,27},{9,... | collective-permute-start | bytes 1769480 | tf_op jit(solution)/shard_map/ppermute | solution.py:331
  190.2 27.3 %collective-permute-start.25 = (f32[3,128,384]{2,1,0:T(8,128)S(1)}, f32[3,128,384]{2,1,0:T(8,128)S(1)}, u32[]{:S(2)}, u32[]{:S(2)}) collective-permute-start(f32[3,128,384]{2,1,0:T(8,128)S(1)} %get-tuple-element.80), channel_id=1, source_target_pairs={{0,19},{1,16},{2,21},{3,22},{4,23},{5,20},{6,25},{7,26},{8,27},{9,... | collective-permute-start | bytes 1769480 | tf_op jit(solution)/shard_map/ppermute | solution.py:333
  205.4 48.1 %collective-permute-start.22 = (f32[3,256,384]{2,1,0:T(8,128)S(1)}, f32[3,256,384]{2,1,0:T(8,128)S(1)}, u32[]{:S(2)}, u32[]{:S(2)}) collective-permute-start(f32[3,256,384]{2,1,0:T(8,128)S(1)} %get-tuple-element.78), channel_id=1, source_target_pairs={{0,17},{1,18},{2,19},{3,20},{4,21},{5,22},{6,23},{7,24},{8,25},{9,... | collective-permute-start | bytes 3538952 | tf_op jit(solution)/shard_map/ppermute | solution.py:345
  207.4 46.1 %collective-permute-start.21 = (f32[3,256,384]{2,1,0:T(8,128)S(1)}, f32[3,256,384]{2,1,0:T(8,128)S(1)}, u32[]{:S(2)}, u32[]{:S(2)}) collective-permute-start(f32[3,256,384]{2,1,0:T(8,128)S(1)} %get-tuple-element.77), channel_id=1, source_target_pairs={{0,16},{1,17},{2,18},{3,19},{4,20},{5,21},{6,22},{7,23},{8,24},{9,... | collective-permute-start | bytes 3538952 | tf_op jit(solution)/shard_map/ppermute | solution.py:357
  209.4 39.0 %collective-permute-start.19 = (f32[3,128,384]{2,1,0:T(8,128)S(1)}, f32[3,128,384]{2,1,0:T(8,128)S(1)}, u32[]{:S(2)}, u32[]{:S(2)}) collective-permute-start(f32[3,128,384]{2,1,0:T(8,128)S(1)} %get-tuple-element.76), channel_id=1, source_target_pairs={{0,1},{1,2},{2,3},{3,4},{4,5},{5,6},{6,7},{7,8},{8,9},{9,10},{10,1... | collective-permute-start | bytes 1769480 | tf_op jit(solution)/shard_map/ppermute | solution.py:332
  211.6 40.0 %collective-permute-start.24 = (f32[3,128,384]{2,1,0:T(8,128)S(1)}, f32[3,128,384]{2,1,0:T(8,128)S(1)}, u32[]{:S(2)}, u32[]{:S(2)}) collective-permute-start(f32[3,128,384]{2,1,0:T(8,128)S(1)} %collective-permute-done.23), channel_id=1, source_target_pairs={{19,18},{16,19},{21,20},{22,21},{23,22},{20,23},{25,24},{26,25},{2... | collective-permute-start | bytes 1769480 | tf_op jit(solution)/shard_map/ppermute | solution.py:360
  217.5 36.0 %collective-permute-start.26 = (f32[3,128,384]{2,1,0:T(8,128)S(1)}, f32[3,128,384]{2,1,0:T(8,128)S(1)}, u32[]{:S(2)}, u32[]{:S(2)}) collective-permute-start(f32[3,128,384]{2,1,0:T(8,128)S(1)} %collective-permute-done.25), channel_id=1, source_target_pairs={{19,18},{16,19},{21,20},{22,21},{23,22},{20,23},{25,24},{26,25},{2... | collective-permute-start | bytes 1769480 | tf_op jit(solution)/shard_map/ppermute | solution.py:361
  248.4 15.6 %collective-permute-start.18 = (f32[3,128,384]{2,1,0:T(8,128)S(1)}, f32[3,128,384]{2,1,0:T(8,128)S(1)}, u32[]{:S(2)}, u32[]{:S(2)}) collective-permute-start(f32[3,128,384]{2,1,0:T(8,128)S(1)} %get-tuple-element.74), channel_id=1, source_target_pairs={{0,16},{1,17},{2,18},{3,19},{4,20},{5,21},{6,22},{7,23},{8,24},{9,... | collective-permute-start | bytes 1769480 | tf_op jit(solution)/shard_map/ppermute | solution.py:358
  251.6 20.0 %collective-permute-start.20 = (f32[3,128,384]{2,1,0:T(8,128)S(1)}, f32[3,128,384]{2,1,0:T(8,128)S(1)}, u32[]{:S(2)}, u32[]{:S(2)}) collective-permute-start(f32[3,128,384]{2,1,0:T(8,128)S(1)} %add.14), channel_id=1, source_target_pairs={{0,17},{1,18},{2,19},{3,20},{4,21},{5,22},{6,23},{7,24},{8,25},{9,... | collective-permute-start | bytes 1769480 | tf_op jit(solution)/shard_map/ppermute | solution.py:359
  274.3 25.0 %collective-permute-start.30 = (f32[3,128,384]{2,1,0:T(8,128)S(1)}, f32[3,128,384]{2,1,0:T(8,128)S(1)}, u32[]{:S(2)}, u32[]{:S(2)}) collective-permute-start(f32[3,128,384]{2,1,0:T(8,128)S(1)} %get-tuple-element.87), channel_id=1, source_target_pairs={{0,19},{1,16},{2,21},{3,22},{4,23},{5,20},{6,25},{7,26},{8,27},{9,... | collective-permute-start | bytes 1769480 | tf_op jit(solution)/shard_map/ppermute | solution.py:331
  276.2 28.2 %collective-permute-start.32 = (f32[3,128,384]{2,1,0:T(8,128)S(1)}, f32[3,128,384]{2,1,0:T(8,128)S(1)}, u32[]{:S(2)}, u32[]{:S(2)}) collective-permute-start(f32[3,128,384]{2,1,0:T(8,128)S(1)} %get-tuple-element.88), channel_id=1, source_target_pairs={{0,19},{1,16},{2,21},{3,22},{4,23},{5,20},{6,25},{7,26},{8,27},{9,... | collective-permute-start | bytes 1769480 | tf_op jit(solution)/shard_map/ppermute | solution.py:333
  278.2 28.2 %collective-permute-start.34 = (f32[3,128,384]{2,1,0:T(8,128)S(1)}, f32[3,128,384]{2,1,0:T(8,128)S(1)}, u32[]{:S(2)}, u32[]{:S(2)}) collective-permute-start(f32[3,128,384]{2,1,0:T(8,128)S(1)} %get-tuple-element.90), channel_id=1, source_target_pairs={{0,1},{1,2},{2,3},{3,4},{4,5},{5,6},{6,7},{7,8},{8,9},{9,10},{10,1... | collective-permute-start | bytes 1769480 | tf_op jit(solution)/shard_map/ppermute | solution.py:332
  295.4 20.9 %collective-permute-start.27 = (f32[3,128,384]{2,1,0:T(8,128)S(1)}, f32[3,128,384]{2,1,0:T(8,128)S(1)}, u32[]{:S(2)}, u32[]{:S(2)}) collective-permute-start(f32[3,128,384]{2,1,0:T(8,128)S(1)} %get-tuple-element.84), channel_id=1, source_target_pairs={{0,16},{1,17},{2,18},{3,19},{4,20},{5,21},{6,22},{7,23},{8,24},{9,... | collective-permute-start | bytes 1769480 | tf_op jit(solution)/shard_map/ppermute | solution.py:358
  297.4 46.6 %collective-permute-start.28 = (f32[3,256,384]{2,1,0:T(8,128)S(1)}, f32[3,256,384]{2,1,0:T(8,128)S(1)}, u32[]{:S(2)}, u32[]{:S(2)}) collective-permute-start(f32[3,256,384]{2,1,0:T(8,128)S(1)} %get-tuple-element.85), channel_id=1, source_target_pairs={{0,16},{1,17},{2,18},{3,19},{4,20},{5,21},{6,22},{7,23},{8,24},{9,... | collective-permute-start | bytes 3538952 | tf_op jit(solution)/shard_map/ppermute | solution.py:357
  299.3 44.7 %collective-permute-start.29 = (f32[3,256,384]{2,1,0:T(8,128)S(1)}, f32[3,256,384]{2,1,0:T(8,128)S(1)}, u32[]{:S(2)}, u32[]{:S(2)}) collective-permute-start(f32[3,256,384]{2,1,0:T(8,128)S(1)} %get-tuple-element.86), channel_id=1, source_target_pairs={{0,17},{1,18},{2,19},{3,20},{4,21},{5,22},{6,23},{7,24},{8,25},{9,... | collective-permute-start | bytes 3538952 | tf_op jit(solution)/shard_map/ppermute | solution.py:345
  304.4 13.9 %collective-permute-start.31 = (f32[3,128,384]{2,1,0:T(8,128)S(1)}, f32[3,128,384]{2,1,0:T(8,128)S(1)}, u32[]{:S(2)}, u32[]{:S(2)}) collective-permute-start(f32[3,128,384]{2,1,0:T(8,128)S(1)} %collective-permute-done.30), channel_id=1, source_target_pairs={{19,18},{16,19},{21,20},{22,21},{23,22},{20,23},{25,24},{26,25},{2... | collective-permute-start | bytes 1769480 | tf_op jit(solution)/shard_map/ppermute | solution.py:360
  306.3 15.0 %collective-permute-start.33 = (f32[3,128,384]{2,1,0:T(8,128)S(1)}, f32[3,128,384]{2,1,0:T(8,128)S(1)}, u32[]{:S(2)}, u32[]{:S(2)}) collective-permute-start(f32[3,128,384]{2,1,0:T(8,128)S(1)} %collective-permute-done.32), channel_id=1, source_target_pairs={{19,18},{16,19},{21,20},{22,21},{23,22},{20,23},{25,24},{26,25},{2... | collective-permute-start | bytes 1769480 | tf_op jit(solution)/shard_map/ppermute | solution.py:361
  316.4 27.6 %collective-permute-start.35 = (f32[3,128,384]{2,1,0:T(8,128)S(1)}, f32[3,128,384]{2,1,0:T(8,128)S(1)}, u32[]{:S(2)}, u32[]{:S(2)}) collective-permute-start(f32[3,128,384]{2,1,0:T(8,128)S(1)} %add.15), channel_id=1, source_target_pairs={{0,17},{1,18},{2,19},{3,20},{4,21},{5,22},{6,23},{7,24},{8,25},{9,... | collective-permute-start | bytes 1769480 | tf_op jit(solution)/shard_map/ppermute | solution.py:359
